TPU v7x, 32 devices: a whole 2x2x4 slice. The times are simulated.
32 devices in a mesh: dom: 8 (over z, x), feat: 4 (over y, core).
Axes of the slice: x: 2, y: 2, z: 4, core: 2. Of those that a mesh axis runs over, the one named last changes fastest.
Arguments:
- features: bfloat16 [8192, 1024], P('dom', 'feat'), may hold values from -6 to 6
- adjacency: bfloat16 [64, 16, 128, 128], P('dom'), may hold values from -0.125 to 0.125
- tile_src: int32 [64, 16], replicated, may hold values from 0 to 63, as said below
- mig_slot: int32 [8, 2], replicated, may hold values from 0 to 7, as said below
- weight_one: bfloat16 [1024, 1024], replicated, may hold values from -0.1875 to 0.1875
- weight_two: bfloat16 [1024, 1024], replicated, may hold values from -0.1875 to 0.1875
Outputs:
- mixed: bfloat16 [8192, 1024], P('dom', 'feat')
Inputs may be any that keep to these rules, and one draw needn't show every extreme that they name: `tile_src`: the tiles of the row blocks that one partition holds name at most 2 distinct blocks held by any one other partition, both in the starting placement and in the placement after the move; in the starting placement they name exactly 2 blocks of every other partition, one of which leaves that partition in the move. `mig_slot`: each row holds 2 distinct slots.
All inputs are finite; a program needn't handle non-finite values.
Results may differ from a plain program's by a relative error of at most 0.0064.
Values may be sent and summed in bfloat16 or wider, within the bound.
No kernel may reach another device: no remote copies, remote signals or barrier semaphores. Data moves between devices by JAX's collectives and lax.ppermute only.
A program may use at most 128 MiB of HBM per device.

v0:
```python
import functools

import jax
import jax.numpy as jnp
from jax import lax
from jax.experimental import pallas as pl
from jax.experimental.pallas import tpu as pltpu
from jax.sharding import PartitionSpec as P


BF16 = jnp.bfloat16
F32 = jnp.float32
I32 = jnp.int32
VMEM = pl.BlockSpec(memory_space=pltpu.VMEM)
SMEM = pl.BlockSpec(memory_space=pltpu.SMEM)
ANY = pl.BlockSpec(memory_space=pl.ANY)
HBM = pl.BlockSpec(memory_space=pltpu.HBM)


def swap(value, axis, flip):
    return lax.ppermute(value, axis, [(i, i ^ flip) for i in range(lax.axis_size(axis))])


def block(shape, dtype=BF16):
    return pltpu.VMEM(shape, dtype)


def copy_all(*triples):
    copies = [pltpu.make_async_copy(*triple) for triple in triples]
    for copy in copies:
        copy.start()
    for copy in copies:
        copy.wait()


def pair_kernel(mig_ref, x_ref, pair_ref, mig, sems):
    copy_all((mig_ref, mig, sems.at[0]))
    me = lax.axis_index("dom")
    copy_all(*[(x_ref.at[mig[m, me]], pair_ref.at[m], sems.at[m]) for m in range(2)])


def write_sends(domains, slots_ref, own_ref, near_refs, far_refs):
    half = domains // 2
    for k in range(1, half):
        near_refs[k - 1][0] = own_ref[slots_ref[2 * k]]
        near_refs[k - 1][1] = own_ref[slots_ref[2 * k + 1]]
    for k in range(half, domains):
        far_refs[k - half][0] = own_ref[slots_ref[2 * k + 1]]


def first_kernel(domains, rows, tiles_ref, mig_ref, x_ref, slots_ref, which_ref, own_ref, *refs):
    *sends, tiles, mig, sems = refs
    half = domains // 2
    loads = [
        pltpu.make_async_copy(*triple)
        for triple in (
            (tiles_ref, tiles, sems.at[0]),
            (mig_ref, mig, sems.at[1]),
            (x_ref, own_ref, sems.at[2]),
        )
    ]
    for load in loads:
        load.start()
    for load in loads[:2]:
        load.wait()
    me = lax.axis_index("dom")
    mine0, mine1 = mig[0, me], mig[1, me]
    slots_ref[0] = mine0
    slots_ref[1] = mine1
    opposite = me ^ half
    opposite_last = opposite * rows + mig[1, opposite]

    named = tiles[...]
    user = lax.broadcasted_iota(I32, named.shape, 1) // rows
    slot = named - me * rows
    leaves = (slot == mine0) | (slot == mine1)
    staying = jnp.where((slot >= 0) & (slot < rows) & jnp.logical_not(leaves), slot, 0)
    last = jnp.where(slot == mine1, 1, 0)
    relayed = jnp.where(named == opposite_last, 1, 0)

    def requests(k):
        asks = user == (me ^ k)
        slots_ref[2 * k + 1] = jnp.max(jnp.where(asks, staying, 0))
        slots_ref[2 * k] = jnp.where(jnp.max(jnp.where(asks, last, 0)) == 1, mine1, mine0)
        which_ref[k] = jnp.max(jnp.where(asks, relayed, 0))

    if domains <= 16:
        for k in range(1, domains):
            requests(k)
    else:
        pl.loop(1, domains)(requests)
    loads[2].wait()
    write_sends(domains, slots_ref, own_ref, sends[: half - 1], sends[half - 1 :])


def table_kernel(
    domains, rows, after_ref, tiles_ref, mig_ref, adjacency_ref, table_ref, held_ref, *refs
):
    del after_ref
    tiles, mig, sems = refs
    load = pltpu.make_async_copy(adjacency_ref, held_ref, sems.at[2])
    load.start()
    copy_all((tiles_ref, tiles, sems.at[0]), (mig_ref, mig, sems.at[1]))
    half = domains // 2
    named = tiles[...]
    user = lax.broadcasted_iota(I32, named.shape, 1) // rows
    holder = named // rows
    slot = named - holder * rows
    flip = holder ^ user

    def mark(q, carry):
        first, last = carry
        here = holder == q
        first = first | (here & (slot == mig[0, q])).astype(I32)
        last = last | (here & (slot == mig[1, q])).astype(I32)
        return first, last

    zeros = jnp.zeros_like(named)
    first, last = lax.fori_loop(0, domains, mark, (zeros, zeros))
    leaves = first | last
    place = rows + 2 * flip + 1 - leaves
    place = jnp.where((flip == half) & (leaves == 1), rows + last, place)
    table_ref[...] = jnp.where(flip == 0, slot, place)
    load.wait()


def relay_kernel(half, which_ref, pair_ref, near_ref, first_ref, *outs):
    first_ref[0:2] = near_ref[...]
    first_ref[2] = pair_ref[which_ref[1]]
    for k in range(2, half):
        outs[k - 2][0] = pair_ref[which_ref[k]]


def fill_pool(domains, chunks, arrived, pool_ref):
    half = domains // 2
    per = chunks[0].shape[0]
    rows = per * len(chunks)
    if len(chunks) == 1:
        pool_ref[0:rows] = chunks[0][...]
    else:
        feat = lax.axis_index("feat")
        for j, chunk in enumerate(chunks):
            for i in range(per):
                pool_ref[(feat ^ j) * per + i] = chunk[i]
    pair, near, far, relay = split_arrived(half, arrived)
    pool_ref[rows : rows + 2] = pair[...]
    for k in range(1, half):
        pool_ref[rows + 2 * k : rows + 2 * k + 2] = near[k - 1][0:2]
    pool_ref[rows + 2 * (half + 1)] = near[0][2]
    for k in range(half, domains):
        pool_ref[rows + 2 * k + 1] = far[k - half][0]
    for k in range(2, half):
        pool_ref[rows + 2 * (half + k)] = relay[k - 2][0]


def split_arrived(half, arrived):
    cuts = (1, half, 2 * half)
    pair, near, far, relay = (arrived[i:j] for i, j in zip((0,) + cuts, cuts + (None,)))
    return pair[0], near, far, relay


def sum_row(r, table_ref, adjacency_ref, pool_ref):
    rows, tiles = adjacency_ref.shape[:2]
    g = lax.axis_index("dom") * rows + r
    total = None
    for t in range(0, tiles, 2):
        left = jnp.concatenate([adjacency_ref[r, t], adjacency_ref[r, t + 1]], axis=1)
        right = jnp.concatenate(
            [pool_ref[table_ref[t, g]], pool_ref[table_ref[t + 1, g]]], axis=0
        )
        part = jnp.dot(left, right, preferred_element_type=F32)
        total = part if total is None else total + part
    return total.astype(BF16)


def first_sum_kernel(domains, feats, j, table_ref, adjacency_ref, own_ref, *refs):
    *arrived, pool_ref, out_ref = refs
    fill_pool(domains, [own_ref], arrived, pool_ref)
    sum_part(feats, j, table_ref, adjacency_ref, pool_ref, out_ref)


def part_sum_kernel(feats, js, table_ref, adjacency_ref, pool_ref, *outs):
    for j, out_ref in zip(js, outs, strict=True):
        sum_part(feats, j, table_ref, adjacency_ref, pool_ref, out_ref)


def sum_part(feats, j, table_ref, adjacency_ref, pool_ref, out_ref):
    start = (lax.axis_index("feat") ^ j) * (adjacency_ref.shape[0] // feats)

    @pl.loop(0, out_ref.shape[0])
    def _(i):
        out_ref[i] = sum_row(start + i, table_ref, adjacency_ref, pool_ref)


def leaving_sum_kernel(domains, feats, table_ref, slots_ref, adjacency_ref, *refs):
    *blocks, pool_ref, out_ref = refs
    fill_pool(domains, blocks[:feats], blocks[feats:], pool_ref)

    @pl.loop(0, out_ref.shape[0])
    def _(i):
        out_ref[i] = sum_row(slots_ref[i], table_ref, adjacency_ref, pool_ref)


def staying_sum_kernel(table_ref, slots_ref, adjacency_ref, pool_ref, out_ref):
    @pl.loop(0, out_ref.shape[0])
    def _(r):
        @pl.when((r != slots_ref[0]) & (r != slots_ref[1]))
        def _():
            out_ref[r] = sum_row(r, table_ref, adjacency_ref, pool_ref)


def dense_kernel(feats, weight_one_ref, weight_two_ref, *refs):
    parts, outs, hidden_ref = refs[:feats], refs[feats : 2 * feats], refs[2 * feats]
    feat = lax.axis_index("feat")
    width = parts[0].shape[1]
    columns = weight_one_ref.shape[1]
    for c in range(0, columns, width):
        total = None
        for j in range(feats):
            start = pl.multiple_of((feat ^ j) * width, width)
            part = jnp.dot(
                parts[j][...],
                weight_one_ref[pl.ds(start, width), c : c + width],
                preferred_element_type=F32,
            )
            total = part if total is None else total + part
        hidden_ref[:, c : c + width] = jnp.maximum(total, 0.0).astype(BF16)
    for j in range(feats):
        start = pl.multiple_of((feat ^ j) * width, width)
        outs[j][...] = jnp.dot(
            hidden_ref[...],
            weight_two_ref[:, pl.ds(start, width)],
            preferred_element_type=F32,
        ).astype(BF16)


def second_kernel(domains, feats, slots_ref, *refs):
    chunks, pair_ref, sends, own_ref = refs[:feats], refs[feats], refs[feats + 1 : -1], refs[-1]
    half = domains // 2
    per = chunks[0].shape[0]
    feat = lax.axis_index("feat")
    for j, chunk in enumerate(chunks):
        for i in range(per):
            own_ref[(feat ^ j) * per + i] = chunk[i]
    for m in range(2):
        pair_ref[m] = own_ref[slots_ref[m]]
    write_sends(domains, slots_ref, own_ref, sends[: half - 1], sends[half - 1 :])


def place_kernel(slots_ref, moved_ref, out_in_ref, out_ref, sems):
    del out_in_ref
    copies = [
        pltpu.make_async_copy(moved_ref.at[i], out_ref.at[slots_ref[i]], sems.at[i])
        for i in range(moved_ref.shape[0])
    ]
    for copy in copies:
        copy.start()
    for copy in copies:
        copy.wait()


def call(kernel, out_shape, in_specs, out_specs, scratch=(), flops=0, moved=0, **kwargs):
    run = pl.pallas_call(
        kernel,
        out_shape=out_shape,
        in_specs=in_specs,
        out_specs=out_specs,
        scratch_shapes=list(scratch),
        cost_estimate=pl.CostEstimate(flops=flops, bytes_accessed=moved, transcendentals=0),
        compiler_params=pltpu.CompilerParams(vmem_limit_bytes=16 << 20),
        **kwargs,
    )

    def place_and_run(*args):
        placed = [
            a
            if spec in (SMEM, ANY)
            else pltpu.with_memory_space_constraint(a, spec.memory_space)
            for a, spec in zip(args, in_specs, strict=True)
        ]
        return run(*placed)

    return place_and_run


def exchange(domains, pair, sends, which):
    half = domains // 2
    shape = pair.shape[1:]
    near, far = sends[: half - 1], sends[half - 1 :]
    pair = swap(pair, "dom", half)
    near_z = [swap(near[k - 1], "dom", k) for k in range(2, half)]
    far = [swap(far[k - half], "dom", k) for k in range(half, domains)]
    first, *relay = call(
        functools.partial(relay_kernel, half),
        [block((3, *shape))] + [block((1, *shape))] * (half - 2),
        [SMEM, VMEM, VMEM],
        [VMEM] * (half - 1),
        moved=4 * pair.size * half,
    )(which, pair, near[0])
    relay = [swap(relay[k - 2], "dom", k) for k in range(2, half)]
    return [pair, swap(first, "dom", 1), *near_z, *far, *relay]


def on_device(features, adjacency, tile_src, mig_slot, weight_one, weight_two):
    domains = lax.axis_size("dom")
    feats = lax.axis_size("feat")
    half = domains // 2
    rows, tiles, size, _ = adjacency.shape
    width = features.shape[1]
    per = rows // feats
    blocks = features.reshape(rows, size, width)
    named, leaving_slots = tile_src.T, mig_slot.T
    near_far = [block((2, size, width))] * (half - 1) + [block((1, size, width))] * half
    pool = block((rows + 2 * domains, size, width))
    work = 2 * tiles * size * size * width
    read = adjacency.size * 2 // rows
    tables = [pltpu.VMEM(named.shape, I32), pltpu.SMEM(leaving_slots.shape, I32)]
    sems = pltpu.SemaphoreType.DMA((3,))

    pair = call(
        pair_kernel,
        [block((2, size, width))],
        [HBM, HBM],
        [VMEM],
        [tables[1], sems],
        moved=8 * size * width,
    )(leaving_slots, blocks)[0]
    slots, which, own, *sends = call(
        functools.partial(first_kernel, domains, rows),
        [
            jax.ShapeDtypeStruct((2 * domains,), I32),
            jax.ShapeDtypeStruct((domains,), I32),
            block((rows, size, width)),
            *near_far,
        ],
        [HBM, HBM, HBM],
        [SMEM, SMEM] + [VMEM] * (1 + len(near_far)),
        [*tables, sems],
        moved=8 * size * width * domains,
    )(named, leaving_slots, blocks)
    arrived = exchange(domains, pair, sends, which)
    table, adjacency = call(
        functools.partial(table_kernel, domains, rows),
        [block(named.shape, I32), block(adjacency.shape)],
        [SMEM, HBM, HBM, HBM],
        [VMEM, VMEM],
        [*tables, sems],
        moved=adjacency.size * 2,
    )(which, named, leaving_slots, adjacency)

    early = list(range(2, feats))
    parts = [None] * feats
    pool_one, parts[2] = call(
        functools.partial(first_sum_kernel, domains, feats, 2),
        [pool, block((per, size, width))],
        [SMEM] + [VMEM] * (2 + len(arrived)),
        [VMEM] * 2,
        flops=work * per,
        moved=read * per,
    )(table, adjacency, own, *arrived)
    for js in [[j] for j in early[1:]] + [[1, 0]]:
        outs = call(
            functools.partial(part_sum_kernel, feats, js),
            [block((per, size, width))] * len(js),
            [SMEM, VMEM, VMEM],
            [VMEM] * len(js),
            flops=work * per * len(js),
            moved=read * per * len(js),
        )(table, adjacency, pool_one)
        for j, out in zip(js, outs):
            parts[j] = out
    parts = [p.reshape(per * size, width) for p in parts]
    parts = [p if j == 0 else swap(p, "feat", j) for j, p in enumerate(parts)]

    chunks = call(
        functools.partial(dense_kernel, feats),
        [block((per * size, width))] * feats,
        [VMEM] * (2 + feats),
        [VMEM] * feats,
        [pltpu.VMEM((per * size, weight_one.shape[1]), BF16)],
        flops=4 * per * size * weight_one.size,
        moved=weight_one.size * 4,
    )(weight_one, weight_two, *parts)
    chunks = [c if j == 0 else swap(c, "feat", j) for j, c in enumerate(chunks)]
    chunks = [c.reshape(per, size, width) for c in chunks]

    pair, *sends = call(
        functools.partial(second_kernel, domains, feats),
        [block((2, size, width)), *near_far],
        [SMEM] + [VMEM] * feats,
        [VMEM] * (1 + len(near_far)),
        [pltpu.VMEM((rows, size, width), BF16)],
        moved=8 * size * width * domains,
    )(slots, *chunks)
    arrived = exchange(domains, pair, sends, which)

    pool_two, leaving = call(
        functools.partial(leaving_sum_kernel, domains, feats),
        [pool, block((2, size, width))],
        [SMEM, SMEM] + [VMEM] * (1 + feats + len(arrived)),
        [VMEM] * 2,
        flops=work * 2,
        moved=read * 2,
    )(table, slots, adjacency, *chunks, *arrived)
    moved = lax.ppermute(leaving, "dom", [(i, (i + 1) % domains) for i in range(domains)])
    out = call(
        staying_sum_kernel,
        jax.ShapeDtypeStruct((rows, size, width), BF16),
        [SMEM, SMEM, VMEM, VMEM],
        VMEM,
        flops=work * (rows - 2),
        moved=read * (rows - 2),
    )(table, slots, adjacency, pool_two)
    out = call(
        place_kernel,
        jax.ShapeDtypeStruct((rows, size, width), BF16),
        [SMEM, VMEM, ANY],
        ANY,
        [pltpu.SemaphoreType.DMA((2,))],
        moved=4 * size * width * 2,
        input_output_aliases={2: 0},
    )(slots, moved, out)
    return out.reshape(rows * size, width)


def solution(mesh):
    in_specs = (P("dom", "feat"), P("dom", None, None, None), P(), P(), P(), P())
    return jax.shard_map(
        on_device, mesh=mesh, in_specs=in_specs, out_specs=P("dom", "feat"), check_vma=False
    )
```

profile of v0, /device:TPU:0, one launch (start us, length us, event | category | flops | bytes accessed | tf_op | source)
XLA Modules:
  0.0 98.1 jit_solution(9908169522504757286)
XLA Ops:
  0.0 1.6 %shard_map.66 = bf16[2,128,256]{2,1,0:T(8,128)(2,1)S(1)} custom-call(s32[2,8]{1,0:T(2,128)} %bitcast.28, bf16[8,128,256]{2,1,0:T(8,128)(2,1)} %bitcast.24), custom_call_target="tpu_custom_call" | custom-call | bytes 262144 | tf_op jit(solution)/shard_map/pallas_call | solution.py:281
  1.6 4.1 %collective-permute-start = (bf16[2,128,256]{2,1,0:T(8,128)(2,1)S(1)}, bf16[2,128,256]{2,1,0:T(8,128)(2,1)S(1)}, u32[]{:S(2)}, u32[]{:S(2)}) collective-permute-start(bf16[2,128,256]{2,1,0:T(8,128)(2,1)S(1)} %shard_map.66), channel_id=1, source_target_pairs={{0,16},{4,20},{8,24},{12,28},{16,0},{20,4},{24,8},{28,12},{1,17},{... | collective-permute-start | bytes 393224 | tf_op jit(solution)/shard_map/ppermute | solution.py:21
  5.7 1.7 %shard_map.64 = (s32[16]{0:T(128)S(1)}, s32[8]{0:T(128)S(1)}, bf16[8,128,256]{2,1,0:T(8,128)(2,1)S(1)}, bf16[2,128,256]{2,1,0:T(8,128)(2,1)S(1)}, bf16[2,128,256...) custom-call(s32[16,64]{1,0:T(8,128)} %bitcast.26, ...), custom_call_target="tpu_custom_call" | custom-call | bytes 2097152 | tf_op jit(solution)/shard_map/pallas_call | solution.py:281
  7.4 0.1 collective-permute-start.4
  7.5 3.8 %collective-permute-start.5 = (bf16[1,128,256]{2,1,0:T(8,128)(2,1)S(1)}, bf16[1,128,256]{2,1,0:T(8,128)(2,1)S(1)}, u32[]{:S(2)}, u32[]{:S(2)}) collective-permute-start(bf16[1,128,256]{2,1,0:T(8,128)(2,1)S(1)} %get-tuple-element.51), channel_id=1, source_target_pairs={{0,20},{4,16},{8,28},{12,24},{16,4},{20,0},{24,12},{28,8},{1,21},{... | collective-permute-start | bytes 196616 | tf_op jit(solution)/shard_map/ppermute | solution.py:21
  11.4 4.3 %collective-permute-done.pair_ref.refs_0_ = bf16[2,128,256]{2,1,0:T(8,128)(2,1)S(1)} collective-permute-done((bf16[2,128,256]{2,1,0:T(8,128)(2,1)S(1)}, bf16[2,128,256]{2,1,0:T(8,128)(2,1)S(1)}, u32[]{:S(2)}, u32[]{:S(2)}) %collective-permute-start) | collective-permute-done | bytes 131104 | tf_op jit(solution)/shard_map/ppermute | solution.py:21
  15.7 0.6 shard_map.67
  16.3 1.9 %collective-permute-start.1 = (bf16[3,128,256]{2,1,0:T(8,128)(2,1)S(1)}, bf16[3,128,256]{2,1,0:T(8,128)(2,1)S(1)}, u32[]{:S(2)}, u32[]{:S(2)}) collective-permute-start(bf16[3,128,256]{2,1,0:T(8,128)(2,1)S(1)} %get-tuple-element.47), channel_id=1, source_target_pairs={{0,4},{4,0},{8,12},{12,8},{16,20},{20,16},{24,28},{28,24},{1,5},{5... | collective-permute-start | bytes 589832 | tf_op jit(solution)/shard_map/ppermute | solution.py:21
  18.1 2.5 %collective-permute-start.6 = (bf16[1,128,256]{2,1,0:T(8,128)(2,1)S(1)}, bf16[1,128,256]{2,1,0:T(8,128)(2,1)S(1)}, u32[]{:S(2)}, u32[]{:S(2)}) collective-permute-start(bf16[1,128,256]{2,1,0:T(8,128)(2,1)S(1)} %get-tuple-element.52), channel_id=1, source_target_pairs={{0,24},{4,28},{8,16},{12,20},{16,8},{20,12},{24,0},{28,4},{1,25},{... | collective-permute-start | bytes 196616 | tf_op jit(solution)/shard_map/ppermute | solution.py:21
  20.6 1.0 %collective-permute-start.7 = (bf16[1,128,256]{2,1,0:T(8,128)(2,1)S(1)}, bf16[1,128,256]{2,1,0:T(8,128)(2,1)S(1)}, u32[]{:S(2)}, u32[]{:S(2)}) collective-permute-start(bf16[1,128,256]{2,1,0:T(8,128)(2,1)S(1)} %get-tuple-element.53), channel_id=1, source_target_pairs={{0,28},{4,24},{8,20},{12,16},{16,12},{20,8},{24,4},{28,0},{1,29},{... | collective-permute-start | bytes 196616 | tf_op jit(solution)/shard_map/ppermute | solution.py:21
  21.6 3.3 %collective-permute-start.3 = (bf16[2,128,256]{2,1,0:T(8,128)(2,1)S(1)}, bf16[2,128,256]{2,1,0:T(8,128)(2,1)S(1)}, u32[]{:S(2)}, u32[]{:S(2)}) collective-permute-start(bf16[2,128,256]{2,1,0:T(8,128)(2,1)S(1)} %get-tuple-element.49), channel_id=1, source_target_pairs={{0,12},{4,8},{8,4},{12,0},{16,28},{20,24},{24,20},{28,16},{1,13},{... | collective-permute-start | bytes 393224 | tf_op jit(solution)/shard_map/ppermute | solution.py:21
  25.0 3.3 %collective-permute-done.7.refs_7_ = bf16[1,128,256]{2,1,0:T(8,128)(2,1)S(1)} collective-permute-done((bf16[1,128,256]{2,1,0:T(8,128)(2,1)S(1)}, bf16[1,128,256]{2,1,0:T(8,128)(2,1)S(1)}, u32[]{:S(2)}, u32[]{:S(2)}) %collective-permute-start.7) | collective-permute-done | bytes 65568 | tf_op jit(solution)/shard_map/ppermute | solution.py:21
  28.3 2.8 %shard_map.65 = (s32[16,64]{1,0:T(8,128)S(1)}, bf16[8,16,128,128]{3,2,1,0:T(8,128)(2,1)S(1)}) custom-call(s32[8]{0:T(128)S(1)} %get-tuple-element.42.after_ref.which_ref, s32[16,64]{1,0:T(8,128)} %bitcast.27, s32[2,8]{1,0:T(2,128)} %bitcast.30, bf16[8,16,128,128]{3,2,1,0:T(8,128)(2,1)} %adjacency_ref.1), custom_call_target="tpu_custom_call" | custom-call | bytes 4194304 | tf_op jit(solution)/shard_map/pallas_call | solution.py:281
  31.0 1.3 %collective-permute-done.3.refs_3_ = bf16[2,128,256]{2,1,0:T(8,128)(2,1)S(1)} collective-permute-done((bf16[2,128,256]{2,1,0:T(8,128)(2,1)S(1)}, bf16[2,128,256]{2,1,0:T(8,128)(2,1)S(1)}, u32[]{:S(2)}, u32[]{:S(2)}) %collective-permute-start.3) | collective-permute-done | bytes 131104 | tf_op jit(solution)/shard_map/ppermute | solution.py:21
  32.3 0.1 collective-permute-done.8.refs_8_
  32.4 1.3 %collective-permute-done.9.refs_9_ = bf16[1,128,256]{2,1,0:T(8,128)(2,1)S(1)} collective-permute-done((bf16[1,128,256]{2,1,0:T(8,128)(2,1)S(1)}, bf16[1,128,256]{2,1,0:T(8,128)(2,1)S(1)}, u32[]{:S(2)}, u32[]{:S(2)}) %collective-permute-start.9) | collective-permute-done | bytes 65568 | tf_op jit(solution)/shard_map/ppermute | solution.py:21
  33.7 1.4 %shard_map.68 = (bf16[24,128,256]{2,1,0:T(8,128)(2,1)S(1)}, bf16[2,128,256]{2,1,0:T(8,128)(2,1)S(1)}) custom-call(s32[16,64]{1,0:T(8,128)S(1)} %get-tuple-element.43.table_ref, bf16[8,16,128,128]{3,2,1,0:T(8,128)(2,1)S(1)} %get-tuple-element.44.adjacency_ref, bf16[8,128,256]{2,1,0:T(8,128)(2,1)S(1)} %get-tuple-element.45.own_ref, ...), custom_call_target="tpu_custom_call" | custom-call | flops 268435456 | bytes 1048576 | tf_op jit(solution)/shard_map/pallas_call | solution.py:281
  35.1 1.3 %shard_map.70 = bf16[2,128,256]{2,1,0:T(8,128)(2,1)S(1)} custom-call(s32[16,64]{1,0:T(8,128)S(1)} %get-tuple-element.43.table_ref, bf16[8,16,128,128]{3,2,1,0:T(8,128)(2,1)S(1)} %get-tuple-element.44.adjacency_ref, bf16[24,128,256]{2,1,0:T(8,128)(2,1)S(1)} %get-tuple-element.56.pool_ref), custom_call_target="tpu_custom_call" | custom-call | flops 268435456 | bytes 1048576 | tf_op jit(solution)/shard_map/pallas_call | solution.py:281
  36.5 2.0 %shard_map.69 = (bf16[2,128,256]{2,1,0:T(8,128)(2,1)S(1)}, bf16[2,128,256]{2,1,0:T(8,128)(2,1)S(1)}) custom-call(s32[16,64]{1,0:T(8,128)S(1)} %get-tuple-element.43.table_ref, bf16[8,16,128,128]{3,2,1,0:T(8,128)(2,1)S(1)} %get-tuple-element.44.adjacency_ref, bf16[24,128,256]{2,1,0:T(8,128)(2,1)S(1)} %get-tuple-element.56.pool_ref), custom_call_target="tpu_custom_call" | custom-call | flops 536870912 | bytes 2097152 | tf_op jit(solution)/shard_map/pallas_call | solution.py:281
  38.6 1.9 %collective-permute-start.10 = (bf16[256,256]{1,0:T(8,128)(2,1)S(1)}, bf16[256,256]{1,0:T(8,128)(2,1)S(1)}, u32[]{:S(2)}, u32[]{:S(2)}) collective-permute-start(bf16[256,256]{1,0:T(8,128)(2,1)S(1)} %bitcast.23), channel_id=1, source_target_pairs={{0,1},{1,0},{2,3},{3,2},{4,5},{5,4},{6,7},{7,6},{8,9},{9,8},{10,11... | collective-permute-start | bytes 393224 | tf_op jit(solution)/shard_map/ppermute | solution.py:21
  40.5 0.2 collective-permute-start.11
  40.7 3.3 %collective-permute-done.12.refs_3_ = bf16[256,256]{1,0:T(8,128)(2,1)S(1)} collective-permute-done((bf16[256,256]{1,0:T(8,128)(2,1)S(1)}, bf16[256,256]{1,0:T(8,128)(2,1)S(1)}, u32[]{:S(2)}, u32[]{:S(2)}) %collective-permute-start.12) | collective-permute-done | bytes 131104 | tf_op jit(solution)/shard_map/ppermute | solution.py:21
  44.0 3.2 %collective-permute-done.11.refs_2_ = bf16[256,256]{1,0:T(8,128)(2,1)S(1)} collective-permute-done((bf16[256,256]{1,0:T(8,128)(2,1)S(1)}, bf16[256,256]{1,0:T(8,128)(2,1)S(1)}, u32[]{:S(2)}, u32[]{:S(2)}) %collective-permute-start.11) | collective-permute-done | bytes 131104 | tf_op jit(solution)/shard_map/ppermute | solution.py:21
  47.2 1.3 %shard_map.71 = (bf16[256,256]{1,0:T(8,128)(2,1)S(1)}, bf16[256,256]{1,0:T(8,128)(2,1)S(1)}, bf16[256,256]{1,0:T(8,128)(2,1)S(1)}, bf16[256,256]{1,0:T(8,128)(2,1)S(1)}) custom-call(bf16[1024,1024]{1,0:T(8,128)(2,1)S(1)} %copy-done, bf16[1024,1024]{1,0:T(8,128)(2,1)S(1)} %copy-done.1, bf16[256,256]{1,0:T(8,128)(2,1)S(1)} %bitcast.20, ...), custom_call_target="tpu_custom_call" | custom-call | flops 1073741824 | bytes 4194304 | tf_op jit(solution)/shard_map/pallas_call | solution.py:281
  48.5 0.4 collective-permute-start.14
  48.9 1.5 %collective-permute-start.15 = (bf16[256,256]{1,0:T(8,128)(2,1)S(1)}, bf16[256,256]{1,0:T(8,128)(2,1)S(1)}, u32[]{:S(2)}, u32[]{:S(2)}) collective-permute-start(bf16[256,256]{1,0:T(8,128)(2,1)S(1)} %get-tuple-element.63), channel_id=1, source_target_pairs={{0,3},{1,2},{2,1},{3,0},{4,7},{5,6},{6,5},{7,4},{8,11},{9,10},{10,... | collective-permute-start | bytes 393224 | tf_op jit(solution)/shard_map/ppermute | solution.py:21
  50.4 4.6 %collective-permute-done.14 = bf16[256,256]{1,0:T(8,128)(2,1)S(1)} collective-permute-done((bf16[256,256]{1,0:T(8,128)(2,1)S(1)}, bf16[256,256]{1,0:T(8,128)(2,1)S(1)}, u32[]{:S(2)}, u32[]{:S(2)}) %collective-permute-start.14) | collective-permute-done | bytes 131104 | tf_op jit(solution)/shard_map/ppermute | solution.py:21
  55.0 1.7 %collective-permute-done.15 = bf16[256,256]{1,0:T(8,128)(2,1)S(1)} collective-permute-done((bf16[256,256]{1,0:T(8,128)(2,1)S(1)}, bf16[256,256]{1,0:T(8,128)(2,1)S(1)}, u32[]{:S(2)}, u32[]{:S(2)}) %collective-permute-start.15) | collective-permute-done | bytes 131104 | tf_op jit(solution)/shard_map/ppermute | solution.py:21
  56.7 0.6 shard_map.72
  57.3 2.0 %collective-permute-start.16 = (bf16[2,128,256]{2,1,0:T(8,128)(2,1)S(1)}, bf16[2,128,256]{2,1,0:T(8,128)(2,1)S(1)}, u32[]{:S(2)}, u32[]{:S(2)}) collective-permute-start(bf16[2,128,256]{2,1,0:T(8,128)(2,1)S(1)} %get-tuple-element.64), channel_id=1, source_target_pairs={{0,16},{4,20},{8,24},{12,28},{16,0},{20,4},{24,8},{28,12},{1,17},{... | collective-permute-start | bytes 393224 | tf_op jit(solution)/shard_map/ppermute | solution.py:21
  59.4 1.0 collective-permute-start.20
  60.3 1.9 %collective-permute-start.21 = (bf16[1,128,256]{2,1,0:T(8,128)(2,1)S(1)}, bf16[1,128,256]{2,1,0:T(8,128)(2,1)S(1)}, u32[]{:S(2)}, u32[]{:S(2)}) collective-permute-start(bf16[1,128,256]{2,1,0:T(8,128)(2,1)S(1)} %get-tuple-element.70), channel_id=1, source_target_pairs={{0,20},{4,16},{8,28},{12,24},{16,4},{20,0},{24,12},{28,8},{1,21},{... | collective-permute-start | bytes 196616 | tf_op jit(solution)/shard_map/ppermute | solution.py:21
  62.3 7.5 %collective-permute-done.16.pair_ref.refs_4_ = bf16[2,128,256]{2,1,0:T(8,128)(2,1)S(1)} collective-permute-done((bf16[2,128,256]{2,1,0:T(8,128)(2,1)S(1)}, bf16[2,128,256]{2,1,0:T(8,128)(2,1)S(1)}, u32[]{:S(2)}, u32[]{:S(2)}) %collective-permute-start.16) | collective-permute-done | bytes 131104 | tf_op jit(solution)/shard_map/ppermute | solution.py:21
  69.8 0.6 shard_map.73
  70.4 1.3 %collective-permute-start.17 = (bf16[3,128,256]{2,1,0:T(8,128)(2,1)S(1)}, bf16[3,128,256]{2,1,0:T(8,128)(2,1)S(1)}, u32[]{:S(2)}, u32[]{:S(2)}) collective-permute-start(bf16[3,128,256]{2,1,0:T(8,128)(2,1)S(1)} %get-tuple-element.66), channel_id=1, source_target_pairs={{0,4},{4,0},{8,12},{12,8},{16,20},{20,16},{24,28},{28,24},{1,5},{5... | collective-permute-start | bytes 589832 | tf_op jit(solution)/shard_map/ppermute | solution.py:21
  71.7 2.1 %collective-permute-start.22 = (bf16[1,128,256]{2,1,0:T(8,128)(2,1)S(1)}, bf16[1,128,256]{2,1,0:T(8,128)(2,1)S(1)}, u32[]{:S(2)}, u32[]{:S(2)}) collective-permute-start(bf16[1,128,256]{2,1,0:T(8,128)(2,1)S(1)} %get-tuple-element.71), channel_id=1, source_target_pairs={{0,24},{4,28},{8,16},{12,20},{16,8},{20,12},{24,0},{28,4},{1,25},{... | collective-permute-start | bytes 196616 | tf_op jit(solution)/shard_map/ppermute | solution.py:21
  73.8 2.0 %collective-permute-start.23 = (bf16[1,128,256]{2,1,0:T(8,128)(2,1)S(1)}, bf16[1,128,256]{2,1,0:T(8,128)(2,1)S(1)}, u32[]{:S(2)}, u32[]{:S(2)}) collective-permute-start(bf16[1,128,256]{2,1,0:T(8,128)(2,1)S(1)} %get-tuple-element.72), channel_id=1, source_target_pairs={{0,28},{4,24},{8,20},{12,16},{16,12},{20,8},{24,4},{28,0},{1,29},{... | collective-permute-start | bytes 196616 | tf_op jit(solution)/shard_map/ppermute | solution.py:21
  75.7 2.7 %collective-permute-start.19 = (bf16[2,128,256]{2,1,0:T(8,128)(2,1)S(1)}, bf16[2,128,256]{2,1,0:T(8,128)(2,1)S(1)}, u32[]{:S(2)}, u32[]{:S(2)}) collective-permute-start(bf16[2,128,256]{2,1,0:T(8,128)(2,1)S(1)} %get-tuple-element.68), channel_id=1, source_target_pairs={{0,12},{4,8},{8,4},{12,0},{16,28},{20,24},{24,20},{28,16},{1,13},{... | collective-permute-start | bytes 393224 | tf_op jit(solution)/shard_map/ppermute | solution.py:21
  78.5 2.9 %collective-permute-done.23.refs_11_ = bf16[1,128,256]{2,1,0:T(8,128)(2,1)S(1)} collective-permute-done((bf16[1,128,256]{2,1,0:T(8,128)(2,1)S(1)}, bf16[1,128,256]{2,1,0:T(8,128)(2,1)S(1)}, u32[]{:S(2)}, u32[]{:S(2)}) %collective-permute-start.23) | collective-permute-done | bytes 65568 | tf_op jit(solution)/shard_map/ppermute | solution.py:21
  81.4 1.4 %collective-permute-done.18.refs_6_ = bf16[2,128,256]{2,1,0:T(8,128)(2,1)S(1)} collective-permute-done((bf16[2,128,256]{2,1,0:T(8,128)(2,1)S(1)}, bf16[2,128,256]{2,1,0:T(8,128)(2,1)S(1)}, u32[]{:S(2)}, u32[]{:S(2)}) %collective-permute-start.18) | collective-permute-done | bytes 131104 | tf_op jit(solution)/shard_map/ppermute | solution.py:21
  82.8 3.5 %collective-permute-done.19.refs_7_ = bf16[2,128,256]{2,1,0:T(8,128)(2,1)S(1)} collective-permute-done((bf16[2,128,256]{2,1,0:T(8,128)(2,1)S(1)}, bf16[2,128,256]{2,1,0:T(8,128)(2,1)S(1)}, u32[]{:S(2)}, u32[]{:S(2)}) %collective-permute-start.19) | collective-permute-done | bytes 131104 | tf_op jit(solution)/shard_map/ppermute | solution.py:21
  86.3 0.6 collective-permute-done.24.refs_12_
  86.9 0.9 collective-permute-done.25.refs_13_
  87.8 1.4 %shard_map.74 = (bf16[24,128,256]{2,1,0:T(8,128)(2,1)S(1)}, bf16[2,128,256]{2,1,0:T(8,128)(2,1)S(1)}) custom-call(s32[16,64]{1,0:T(8,128)S(1)} %get-tuple-element.43.table_ref, s32[16]{0:T(128)S(1)} %get-tuple-element.41.slots_ref, bf16[8,16,128,128]{3,2,1,0:T(8,128)(2,1)S(1)} %get-tuple-element.44.adjacency_ref, bf16[2,128,256]{2,1,0:T(8,128)(2,1)S(1)} %bitcast.13, ...), custom_call_target="tpu_custom_call" | custom-call | flops 268435456 | bytes 1048576 | tf_op jit(solution)/shard_map/pallas_call | solution.py:281
  89.2 1.3 %collective-permute-start.26 = (bf16[2,128,256]{2,1,0:T(8,128)(2,1)S(1)}, bf16[2,128,256]{2,1,0:T(8,128)(2,1)S(1)}, u32[]{:S(2)}, u32[]{:S(2)}) collective-permute-start(bf16[2,128,256]{2,1,0:T(8,128)(2,1)S(1)} %get-tuple-element.75), channel_id=1, source_target_pairs={{0,4},{4,8},{8,12},{12,16},{16,20},{20,24},{24,28},{28,0},{1,5},{5... | collective-permute-start | bytes 393224 | tf_op jit(solution)/shard_map/ppermute | solution.py:405
  90.5 3.5 %shard_map.75.out_in_ref = bf16[8,128,256]{2,1,0:T(8,128)(2,1)} custom-call(s32[16,64]{1,0:T(8,128)S(1)} %get-tuple-element.43.table_ref, s32[16]{0:T(128)S(1)} %get-tuple-element.41.slots_ref, bf16[8,16,128,128]{3,2,1,0:T(8,128)(2,1)S(1)} %get-tuple-element.44.adjacency_ref, bf16[24,128,256]{2,1,0:T(8,128)(2,1)S(1)} %get-tuple-element.76.pool_ref), custom_call_target="tpu_custom_call" | custom-call | flops 805306368 | bytes 3145728 | tf_op jit(solution)/shard_map/pallas_call | solution.py:281
  94.0 2.9 %collective-permute-done.26.moved_ref = bf16[2,128,256]{2,1,0:T(8,128)(2,1)S(1)} collective-permute-done((bf16[2,128,256]{2,1,0:T(8,128)(2,1)S(1)}, bf16[2,128,256]{2,1,0:T(8,128)(2,1)S(1)}, u32[]{:S(2)}, u32[]{:S(2)}) %collective-permute-start.26) | collective-permute-done | bytes 131104 | tf_op jit(solution)/shard_map/ppermute | solution.py:405
  96.9 1.2 %shard_map.76 = bf16[8,128,256]{2,1,0:T(8,128)(2,1)} custom-call(s32[16]{0:T(128)S(1)} %get-tuple-element.41.slots_ref, bf16[2,128,256]{2,1,0:T(8,128)(2,1)S(1)} %collective-permute-done.26.moved_ref, bf16[8,128,256]{2,1,0:T(8,128)(2,1)} %shard_map.75.out_in_ref), custom_call_target="tpu_custom_call", output_to_operand_aliasing={{}: (2, {})} | custom-call | bytes 262144 | tf_op jit(solution)/shard_map/pallas_call | solution.py:281
  (23 shorter events, 0.3 us)
Async XLA Ops:
  1.6 14.1 %collective-permute-start = (bf16[2,128,256]{2,1,0:T(8,128)(2,1)S(1)}, bf16[2,128,256]{2,1,0:T(8,128)(2,1)S(1)}, u32[]{:S(2)}, u32[]{:S(2)}) collective-permute-start(bf16[2,128,256]{2,1,0:T(8,128)(2,1)S(1)} %shard_map.66), channel_id=1, source_target_pairs={{0,16},{4,20},{8,24},{12,28},{16,0},{20,4},{24,8},{28,12},{1,17},{... | collective-permute-start | bytes 393224 | tf_op jit(solution)/shard_map/ppermute | solution.py:21
  7.4 14.2 %collective-permute-start.4 = (bf16[1,128,256]{2,1,0:T(8,128)(2,1)S(1)}, bf16[1,128,256]{2,1,0:T(8,128)(2,1)S(1)}, u32[]{:S(2)}, u32[]{:S(2)}) collective-permute-start(bf16[1,128,256]{2,1,0:T(8,128)(2,1)S(1)} %get-tuple-element.50), channel_id=1, source_target_pairs={{0,16},{4,20},{8,24},{12,28},{16,0},{20,4},{24,8},{28,12},{1,17},{... | collective-permute-start | bytes 196616 | tf_op jit(solution)/shard_map/ppermute | solution.py:21
  7.5 14.1 %collective-permute-start.5 = (bf16[1,128,256]{2,1,0:T(8,128)(2,1)S(1)}, bf16[1,128,256]{2,1,0:T(8,128)(2,1)S(1)}, u32[]{:S(2)}, u32[]{:S(2)}) collective-permute-start(bf16[1,128,256]{2,1,0:T(8,128)(2,1)S(1)} %get-tuple-element.51), channel_id=1, source_target_pairs={{0,20},{4,16},{8,28},{12,24},{16,4},{20,0},{24,12},{28,8},{1,21},{... | collective-permute-start | bytes 196616 | tf_op jit(solution)/shard_map/ppermute | solution.py:21
  16.3 17.4 %collective-permute-start.1 = (bf16[3,128,256]{2,1,0:T(8,128)(2,1)S(1)}, bf16[3,128,256]{2,1,0:T(8,128)(2,1)S(1)}, u32[]{:S(2)}, u32[]{:S(2)}) collective-permute-start(bf16[3,128,256]{2,1,0:T(8,128)(2,1)S(1)} %get-tuple-element.47), channel_id=1, source_target_pairs={{0,4},{4,0},{8,12},{12,8},{16,20},{20,16},{24,28},{28,24},{1,5},{5... | collective-permute-start | bytes 589832 | tf_op jit(solution)/shard_map/ppermute | solution.py:21
  18.1 6.8 %collective-permute-start.6 = (bf16[1,128,256]{2,1,0:T(8,128)(2,1)S(1)}, bf16[1,128,256]{2,1,0:T(8,128)(2,1)S(1)}, u32[]{:S(2)}, u32[]{:S(2)}) collective-permute-start(bf16[1,128,256]{2,1,0:T(8,128)(2,1)S(1)} %get-tuple-element.52), channel_id=1, source_target_pairs={{0,24},{4,28},{8,16},{12,20},{16,8},{20,12},{24,0},{28,4},{1,25},{... | collective-permute-start | bytes 196616 | tf_op jit(solution)/shard_map/ppermute | solution.py:21
  20.6 7.7 %collective-permute-start.7 = (bf16[1,128,256]{2,1,0:T(8,128)(2,1)S(1)}, bf16[1,128,256]{2,1,0:T(8,128)(2,1)S(1)}, u32[]{:S(2)}, u32[]{:S(2)}) collective-permute-start(bf16[1,128,256]{2,1,0:T(8,128)(2,1)S(1)} %get-tuple-element.53), channel_id=1, source_target_pairs={{0,28},{4,24},{8,20},{12,16},{16,12},{20,8},{24,4},{28,0},{1,29},{... | collective-permute-start | bytes 196616 | tf_op jit(solution)/shard_map/ppermute | solution.py:21
  21.6 9.4 %collective-permute-start.2 = (bf16[2,128,256]{2,1,0:T(8,128)(2,1)S(1)}, bf16[2,128,256]{2,1,0:T(8,128)(2,1)S(1)}, u32[]{:S(2)}, u32[]{:S(2)}) collective-permute-start(bf16[2,128,256]{2,1,0:T(8,128)(2,1)S(1)} %get-tuple-element.48), channel_id=1, source_target_pairs={{0,8},{4,12},{8,0},{12,4},{16,24},{20,28},{24,16},{28,20},{1,9},{5... | collective-permute-start | bytes 393224 | tf_op jit(solution)/shard_map/ppermute | solution.py:21
  21.6 10.7 %collective-permute-start.3 = (bf16[2,128,256]{2,1,0:T(8,128)(2,1)S(1)}, bf16[2,128,256]{2,1,0:T(8,128)(2,1)S(1)}, u32[]{:S(2)}, u32[]{:S(2)}) collective-permute-start(bf16[2,128,256]{2,1,0:T(8,128)(2,1)S(1)} %get-tuple-element.49), channel_id=1, source_target_pairs={{0,12},{4,8},{8,4},{12,0},{16,28},{20,24},{24,20},{28,16},{1,13},{... | collective-permute-start | bytes 393224 | tf_op jit(solution)/shard_map/ppermute | solution.py:21
  24.9 7.5 %collective-permute-start.8 = (bf16[1,128,256]{2,1,0:T(8,128)(2,1)S(1)}, bf16[1,128,256]{2,1,0:T(8,128)(2,1)S(1)}, u32[]{:S(2)}, u32[]{:S(2)}) collective-permute-start(bf16[1,128,256]{2,1,0:T(8,128)(2,1)S(1)} %get-tuple-element.54), channel_id=1, source_target_pairs={{0,8},{4,12},{8,0},{12,4},{16,24},{20,28},{24,16},{28,20},{1,9},{5... | collective-permute-start | bytes 196616 | tf_op jit(solution)/shard_map/ppermute | solution.py:21
  28.3 5.4 %collective-permute-start.9 = (bf16[1,128,256]{2,1,0:T(8,128)(2,1)S(1)}, bf16[1,128,256]{2,1,0:T(8,128)(2,1)S(1)}, u32[]{:S(2)}, u32[]{:S(2)}) collective-permute-start(bf16[1,128,256]{2,1,0:T(8,128)(2,1)S(1)} %get-tuple-element.55), channel_id=1, source_target_pairs={{0,12},{4,8},{8,4},{12,0},{16,28},{20,24},{24,20},{28,16},{1,13},{... | collective-permute-start | bytes 196616 | tf_op jit(solution)/shard_map/ppermute | solution.py:21
  36.5 10.7 %copy-start = (bf16[1024,1024]{1,0:T(8,128)(2,1)S(1)}, bf16[1024,1024]{1,0:T(8,128)(2,1)}, u32[]{:S(2)}) copy-start(bf16[1024,1024]{1,0:T(8,128)(2,1)} %weight_one_ref.1) | copy-start | bytes 6291460
  36.5 10.7 %copy-start.1 = (bf16[1024,1024]{1,0:T(8,128)(2,1)S(1)}, bf16[1024,1024]{1,0:T(8,128)(2,1)}, u32[]{:S(2)}) copy-start(bf16[1024,1024]{1,0:T(8,128)(2,1)} %weight_two_ref.1) | copy-start | bytes 6291460
  38.5 5.5 %collective-permute-start.12 = (bf16[256,256]{1,0:T(8,128)(2,1)S(1)}, bf16[256,256]{1,0:T(8,128)(2,1)S(1)}, u32[]{:S(2)}, u32[]{:S(2)}) collective-permute-start(bf16[256,256]{1,0:T(8,128)(2,1)S(1)} %bitcast.21), channel_id=1, source_target_pairs={{0,3},{1,2},{2,1},{3,0},{4,7},{5,6},{6,5},{7,4},{8,11},{9,10},{10,... | collective-permute-start | bytes 393224 | tf_op jit(solution)/shard_map/ppermute | solution.py:21
  38.6 5.4 %collective-permute-start.10 = (bf16[256,256]{1,0:T(8,128)(2,1)S(1)}, bf16[256,256]{1,0:T(8,128)(2,1)S(1)}, u32[]{:S(2)}, u32[]{:S(2)}) collective-permute-start(bf16[256,256]{1,0:T(8,128)(2,1)S(1)} %bitcast.23), channel_id=1, source_target_pairs={{0,1},{1,0},{2,3},{3,2},{4,5},{5,4},{6,7},{7,6},{8,9},{9,8},{10,11... | collective-permute-start | bytes 393224 | tf_op jit(solution)/shard_map/ppermute | solution.py:21
  40.5 6.7 %collective-permute-start.11 = (bf16[256,256]{1,0:T(8,128)(2,1)S(1)}, bf16[256,256]{1,0:T(8,128)(2,1)S(1)}, u32[]{:S(2)}, u32[]{:S(2)}) collective-permute-start(bf16[256,256]{1,0:T(8,128)(2,1)S(1)} %bitcast.22), channel_id=1, source_target_pairs={{0,2},{1,3},{2,0},{3,1},{4,6},{5,7},{6,4},{7,5},{8,10},{9,11},{10,... | collective-permute-start | bytes 393224 | tf_op jit(solution)/shard_map/ppermute | solution.py:21
  48.5 1.9 %collective-permute-start.13 = (bf16[256,256]{1,0:T(8,128)(2,1)S(1)}, bf16[256,256]{1,0:T(8,128)(2,1)S(1)}, u32[]{:S(2)}, u32[]{:S(2)}) collective-permute-start(bf16[256,256]{1,0:T(8,128)(2,1)S(1)} %get-tuple-element.61), channel_id=1, source_target_pairs={{0,1},{1,0},{2,3},{3,2},{4,5},{5,4},{6,7},{7,6},{8,9},{9,8},{10,11... | collective-permute-start | bytes 393224 | tf_op jit(solution)/shard_map/ppermute | solution.py:21
  48.5 6.4 %collective-permute-start.14 = (bf16[256,256]{1,0:T(8,128)(2,1)S(1)}, bf16[256,256]{1,0:T(8,128)(2,1)S(1)}, u32[]{:S(2)}, u32[]{:S(2)}) collective-permute-start(bf16[256,256]{1,0:T(8,128)(2,1)S(1)} %get-tuple-element.62), channel_id=1, source_target_pairs={{0,2},{1,3},{2,0},{3,1},{4,6},{5,7},{6,4},{7,5},{8,10},{9,11},{10,... | collective-permute-start | bytes 393224 | tf_op jit(solution)/shard_map/ppermute | solution.py:21
  48.9 7.8 %collective-permute-start.15 = (bf16[256,256]{1,0:T(8,128)(2,1)S(1)}, bf16[256,256]{1,0:T(8,128)(2,1)S(1)}, u32[]{:S(2)}, u32[]{:S(2)}) collective-permute-start(bf16[256,256]{1,0:T(8,128)(2,1)S(1)} %get-tuple-element.63), channel_id=1, source_target_pairs={{0,3},{1,2},{2,1},{3,0},{4,7},{5,6},{6,5},{7,4},{8,11},{9,10},{10,... | collective-permute-start | bytes 393224 | tf_op jit(solution)/shard_map/ppermute | solution.py:21
  57.3 12.5 %collective-permute-start.16 = (bf16[2,128,256]{2,1,0:T(8,128)(2,1)S(1)}, bf16[2,128,256]{2,1,0:T(8,128)(2,1)S(1)}, u32[]{:S(2)}, u32[]{:S(2)}) collective-permute-start(bf16[2,128,256]{2,1,0:T(8,128)(2,1)S(1)} %get-tuple-element.64), channel_id=1, source_target_pairs={{0,16},{4,20},{8,24},{12,28},{16,0},{20,4},{24,8},{28,12},{1,17},{... | collective-permute-start | bytes 393224 | tf_op jit(solution)/shard_map/ppermute | solution.py:21
  59.4 16.4 %collective-permute-start.20 = (bf16[1,128,256]{2,1,0:T(8,128)(2,1)S(1)}, bf16[1,128,256]{2,1,0:T(8,128)(2,1)S(1)}, u32[]{:S(2)}, u32[]{:S(2)}) collective-permute-start(bf16[1,128,256]{2,1,0:T(8,128)(2,1)S(1)} %get-tuple-element.69), channel_id=1, source_target_pairs={{0,16},{4,20},{8,24},{12,28},{16,0},{20,4},{24,8},{28,12},{1,17},{... | collective-permute-start | bytes 196616 | tf_op jit(solution)/shard_map/ppermute | solution.py:21
  60.3 15.4 %collective-permute-start.21 = (bf16[1,128,256]{2,1,0:T(8,128)(2,1)S(1)}, bf16[1,128,256]{2,1,0:T(8,128)(2,1)S(1)}, u32[]{:S(2)}, u32[]{:S(2)}) collective-permute-start(bf16[1,128,256]{2,1,0:T(8,128)(2,1)S(1)} %get-tuple-element.70), channel_id=1, source_target_pairs={{0,20},{4,16},{8,28},{12,24},{16,4},{20,0},{24,12},{28,8},{1,21},{... | collective-permute-start | bytes 196616 | tf_op jit(solution)/shard_map/ppermute | solution.py:21
  70.4 17.4 %collective-permute-start.17 = (bf16[3,128,256]{2,1,0:T(8,128)(2,1)S(1)}, bf16[3,128,256]{2,1,0:T(8,128)(2,1)S(1)}, u32[]{:S(2)}, u32[]{:S(2)}) collective-permute-start(bf16[3,128,256]{2,1,0:T(8,128)(2,1)S(1)} %get-tuple-element.66), channel_id=1, source_target_pairs={{0,4},{4,0},{8,12},{12,8},{16,20},{20,16},{24,28},{28,24},{1,5},{5... | collective-permute-start | bytes 589832 | tf_op jit(solution)/shard_map/ppermute | solution.py:21
  71.7 6.8 %collective-permute-start.22 = (bf16[1,128,256]{2,1,0:T(8,128)(2,1)S(1)}, bf16[1,128,256]{2,1,0:T(8,128)(2,1)S(1)}, u32[]{:S(2)}, u32[]{:S(2)}) collective-permute-start(bf16[1,128,256]{2,1,0:T(8,128)(2,1)S(1)} %get-tuple-element.71), channel_id=1, source_target_pairs={{0,24},{4,28},{8,16},{12,20},{16,8},{20,12},{24,0},{28,4},{1,25},{... | collective-permute-start | bytes 196616 | tf_op jit(solution)/shard_map/ppermute | solution.py:21
  73.8 7.7 %collective-permute-start.23 = (bf16[1,128,256]{2,1,0:T(8,128)(2,1)S(1)}, bf16[1,128,256]{2,1,0:T(8,128)(2,1)S(1)}, u32[]{:S(2)}, u32[]{:S(2)}) collective-permute-start(bf16[1,128,256]{2,1,0:T(8,128)(2,1)S(1)} %get-tuple-element.72), channel_id=1, source_target_pairs={{0,28},{4,24},{8,20},{12,16},{16,12},{20,8},{24,4},{28,0},{1,29},{... | collective-permute-start | bytes 196616 | tf_op jit(solution)/shard_map/ppermute | solution.py:21
  75.7 7.1 %collective-permute-start.18 = (bf16[2,128,256]{2,1,0:T(8,128)(2,1)S(1)}, bf16[2,128,256]{2,1,0:T(8,128)(2,1)S(1)}, u32[]{:S(2)}, u32[]{:S(2)}) collective-permute-start(bf16[2,128,256]{2,1,0:T(8,128)(2,1)S(1)} %get-tuple-element.67), channel_id=1, source_target_pairs={{0,8},{4,12},{8,0},{12,4},{16,24},{20,28},{24,16},{28,20},{1,9},{5... | collective-permute-start | bytes 393224 | tf_op jit(solution)/shard_map/ppermute | solution.py:21
  75.7 10.6 %collective-permute-start.19 = (bf16[2,128,256]{2,1,0:T(8,128)(2,1)S(1)}, bf16[2,128,256]{2,1,0:T(8,128)(2,1)S(1)}, u32[]{:S(2)}, u32[]{:S(2)}) collective-permute-start(bf16[2,128,256]{2,1,0:T(8,128)(2,1)S(1)} %get-tuple-element.68), channel_id=1, source_target_pairs={{0,12},{4,8},{8,4},{12,0},{16,28},{20,24},{24,20},{28,16},{1,13},{... | collective-permute-start | bytes 393224 | tf_op jit(solution)/shard_map/ppermute | solution.py:21
  78.5 8.4 %collective-permute-start.24 = (bf16[1,128,256]{2,1,0:T(8,128)(2,1)S(1)}, bf16[1,128,256]{2,1,0:T(8,128)(2,1)S(1)}, u32[]{:S(2)}, u32[]{:S(2)}) collective-permute-start(bf16[1,128,256]{2,1,0:T(8,128)(2,1)S(1)} %get-tuple-element.73), channel_id=1, source_target_pairs={{0,8},{4,12},{8,0},{12,4},{16,24},{20,28},{24,16},{28,20},{1,9},{5... | collective-permute-start | bytes 196616 | tf_op jit(solution)/shard_map/ppermute | solution.py:21
  81.4 6.4 %collective-permute-start.25 = (bf16[1,128,256]{2,1,0:T(8,128)(2,1)S(1)}, bf16[1,128,256]{2,1,0:T(8,128)(2,1)S(1)}, u32[]{:S(2)}, u32[]{:S(2)}) collective-permute-start(bf16[1,128,256]{2,1,0:T(8,128)(2,1)S(1)} %get-tuple-element.74), channel_id=1, source_target_pairs={{0,12},{4,8},{8,4},{12,0},{16,28},{20,24},{24,20},{28,16},{1,13},{... | collective-permute-start | bytes 196616 | tf_op jit(solution)/shard_map/ppermute | solution.py:21
  89.2 7.7 %collective-permute-start.26 = (bf16[2,128,256]{2,1,0:T(8,128)(2,1)S(1)}, bf16[2,128,256]{2,1,0:T(8,128)(2,1)S(1)}, u32[]{:S(2)}, u32[]{:S(2)}) collective-permute-start(bf16[2,128,256]{2,1,0:T(8,128)(2,1)S(1)} %get-tuple-element.75), channel_id=1, source_target_pairs={{0,4},{4,8},{8,12},{12,16},{16,20},{20,24},{24,28},{28,0},{1,5},{5... | collective-permute-start | bytes 393224 | tf_op jit(solution)/shard_map/ppermute | solution.py:405
where the time goes:
time: 98.4 us; the launch traced here: 98.1 us
  waiting for transfers between devices  42.8 us (43%)
  starting transfers between devices  35.2 us (36%)
  Pallas kernels  19.9 us (20%)
    ppermute x26, waiting for transfers between devices, swap(): lax.ppermute(value, axis, [(i, i ^ flip) for i in range(lax.axis_size(axi...  39.9 us
    ppermute x26, starting transfers between devices, swap(): lax.ppermute(value, axis, [(i, i ^ flip) for i in range(lax.axis_size(axi...  33.9 us
    pallas_call x13, Pallas kernels, place_and_run(): return run(*placed)  19.9 us
    ppermute x1, waiting for transfers between devices, on_device(): lax.ppermute(leaving, 'dom', [(i, (i + 1) % domains) for i in range(domai...  2.92 us
  transfers between devices with their start and end apart: 27, of which 16 were waited for; matrix products, arithmetic and copies ran while one was open for 0% of the time, Pallas kernels for 9%

commit v1 on v0

--- a/solution.py
+++ b/solution.py
@@ -25,6 +25,10 @@
     return pltpu.VMEM(shape, dtype)
 
 
+def scalars(shape):
+    return pltpu.SMEM(shape, I32)
+
+
 def copy_all(*triples):
     copies = [pltpu.make_async_copy(*triple) for triple in triples]
     for copy in copies:
@@ -33,10 +37,15 @@
         copy.wait()
 
 
-def pair_kernel(mig_ref, x_ref, pair_ref, mig, sems):
-    copy_all((mig_ref, mig, sems.at[0]))
+def load_kernel(tiles_ref, mig_ref, x_ref, named_ref, slots_ref, own_ref, pair_ref, sems):
+    copy_all(
+        (tiles_ref, named_ref, sems.at[0]),
+        (mig_ref, slots_ref, sems.at[1]),
+        (x_ref, own_ref, sems.at[2]),
+    )
     me = lax.axis_index("dom")
-    copy_all(*[(x_ref.at[mig[m, me]], pair_ref.at[m], sems.at[m]) for m in range(2)])
+    for m in range(2):
+        pair_ref[m] = own_ref[slots_ref[m, me]]
 
 
 def write_sends(domains, slots_ref, own_ref, near_refs, far_refs):
@@ -48,21 +57,8 @@
         far_refs[k - half][0] = own_ref[slots_ref[2 * k + 1]]
 
 
-def first_kernel(domains, rows, tiles_ref, mig_ref, x_ref, slots_ref, which_ref, own_ref, *refs):
-    *sends, tiles, mig, sems = refs
-    half = domains // 2
-    loads = [
-        pltpu.make_async_copy(*triple)
-        for triple in (
-            (tiles_ref, tiles, sems.at[0]),
-            (mig_ref, mig, sems.at[1]),
-            (x_ref, own_ref, sems.at[2]),
-        )
-    ]
-    for load in loads:
-        load.start()
-    for load in loads[:2]:
-        load.wait()
+def first_kernel(domains, rows, mig, tiles_ref, own_ref, slots_ref, which_ref, *sends):
+    half = domains // 2
     me = lax.axis_index("dom")
     mine0, mine1 = mig[0, me], mig[1, me]
     slots_ref[0] = mine0
@@ -70,7 +66,7 @@
     opposite = me ^ half
     opposite_last = opposite * rows + mig[1, opposite]
 
-    named = tiles[...]
+    named = tiles_ref[...]
     user = lax.broadcasted_iota(I32, named.shape, 1) // rows
     slot = named - me * rows
     leaves = (slot == mine0) | (slot == mine1)
@@ -89,20 +85,16 @@
             requests(k)
     else:
         pl.loop(1, domains)(requests)
-    loads[2].wait()
     write_sends(domains, slots_ref, own_ref, sends[: half - 1], sends[half - 1 :])
 
 
 def table_kernel(
-    domains, rows, after_ref, tiles_ref, mig_ref, adjacency_ref, table_ref, held_ref, *refs
+    domains, rows, mig, tiles_ref, adjacency_ref, table_ref, held_ref, found_ref, sems
 ):
-    del after_ref
-    tiles, mig, sems = refs
-    load = pltpu.make_async_copy(adjacency_ref, held_ref, sems.at[2])
+    load = pltpu.make_async_copy(adjacency_ref, held_ref, sems.at[0])
     load.start()
-    copy_all((tiles_ref, tiles, sems.at[0]), (mig_ref, mig, sems.at[1]))
-    half = domains // 2
-    named = tiles[...]
+    half = domains // 2
+    named = tiles_ref[...]
     user = lax.broadcasted_iota(I32, named.shape, 1) // rows
     holder = named // rows
     slot = named - holder * rows
@@ -120,7 +112,8 @@
     leaves = first | last
     place = rows + 2 * flip + 1 - leaves
     place = jnp.where((flip == half) & (leaves == 1), rows + last, place)
-    table_ref[...] = jnp.where(flip == 0, slot, place)
+    found_ref[...] = jnp.where(flip == 0, slot, place)
+    copy_all((found_ref, table_ref, sems.at[1]))
     load.wait()
 
 
@@ -273,9 +266,7 @@
 
     def place_and_run(*args):
         placed = [
-            a
-            if spec in (SMEM, ANY)
-            else pltpu.with_memory_space_constraint(a, spec.memory_space)
+            a if spec is ANY else pltpu.with_memory_space_constraint(a, spec.memory_space)
             for a, spec in zip(args, in_specs, strict=True)
         ]
         return run(*placed)
@@ -314,39 +305,35 @@
     pool = block((rows + 2 * domains, size, width))
     work = 2 * tiles * size * size * width
     read = adjacency.size * 2 // rows
-    tables = [pltpu.VMEM(named.shape, I32), pltpu.SMEM(leaving_slots.shape, I32)]
-    sems = pltpu.SemaphoreType.DMA((3,))
-
-    pair = call(
-        pair_kernel,
-        [block((2, size, width))],
-        [HBM, HBM],
-        [VMEM],
-        [tables[1], sems],
-        moved=8 * size * width,
-    )(leaving_slots, blocks)[0]
-    slots, which, own, *sends = call(
-        functools.partial(first_kernel, domains, rows),
+    named, mig, own, pair = call(
+        load_kernel,
         [
-            jax.ShapeDtypeStruct((2 * domains,), I32),
-            jax.ShapeDtypeStruct((domains,), I32),
+            block(named.shape, I32),
+            scalars(leaving_slots.shape),
             block((rows, size, width)),
-            *near_far,
+            block((2, size, width)),
         ],
         [HBM, HBM, HBM],
-        [SMEM, SMEM] + [VMEM] * (1 + len(near_far)),
-        [*tables, sems],
+        [VMEM, SMEM, VMEM, VMEM],
+        [pltpu.SemaphoreType.DMA((3,))],
+        moved=features.size * 2,
+    )(named, leaving_slots, blocks)
+    slots, which, *sends = call(
+        functools.partial(first_kernel, domains, rows),
+        [scalars((2 * domains,)), scalars((domains,)), *near_far],
+        [SMEM, VMEM, VMEM],
+        [SMEM, SMEM] + [VMEM] * len(near_far),
         moved=8 * size * width * domains,
-    )(named, leaving_slots, blocks)
+    )(mig, named, own)
     arrived = exchange(domains, pair, sends, which)
     table, adjacency = call(
         functools.partial(table_kernel, domains, rows),
-        [block(named.shape, I32), block(adjacency.shape)],
-        [SMEM, HBM, HBM, HBM],
-        [VMEM, VMEM],
-        [*tables, sems],
+        [scalars(named.shape), block(adjacency.shape)],
+        [SMEM, VMEM, HBM],
+        [SMEM, VMEM],
+        [pltpu.VMEM(named.shape, I32), pltpu.SemaphoreType.DMA((2,))],
         moved=adjacency.size * 2,
-    )(which, named, leaving_slots, adjacency)
+    )(mig, named, adjacency)
 
     early = list(range(2, feats))
     parts = [None] * feats

time: 98.4 us -> 92.9 us (0.944)
  Pallas kernels: 19.9 us -> 11.8 us
  waiting for transfers between devices: 42.8 us -> 45.5 us
    pallas_call x13, Pallas kernels: 19.9 us -> 11.8 us  [place_and_run(): return run(*placed)]
    ppermute x26, waiting for transfers between devices: 39.9 us -> 41.9 us  [swap(): lax.ppermute(value, axis, [(i, i ^ flip) for i in range(lax.axis_size(axi...]
  transfers between devices with their start and end apart: 27 -> 27, of which waited for: 16 -> 16; matrix products, arithmetic and copies ran while one was open for 0% -> 0% of each run, Pallas kernels for 9% -> 6%
where the time goes in v1:
time: 92.9 us; the launch traced here: 92.7 us
  waiting for transfers between devices  45.5 us (49%)
  starting transfers between devices  35.2 us (38%)
  Pallas kernels  11.8 us (13%)
    ppermute x26, waiting for transfers between devices, swap(): lax.ppermute(value, axis, [(i, i ^ flip) for i in range(lax.axis_size(axi...  41.9 us
    ppermute x26, starting transfers between devices, swap(): lax.ppermute(value, axis, [(i, i ^ flip) for i in range(lax.axis_size(axi...  33.9 us
    pallas_call x13, Pallas kernels, place_and_run(): return run(*placed)  11.8 us
    ppermute x1, waiting for transfers between devices, on_device(): lax.ppermute(leaving, 'dom', [(i, (i + 1) % domains) for i in range(domai...  3.6 us
  transfers between devices with their start and end apart: 27, of which 16 were waited for; matrix products, arithmetic and copies ran while one was open for 0% of the time, Pallas kernels for 6%

profile of v1, /device:TPU:0, one launch (start us, length us, event | category | flops | bytes accessed | tf_op | source)
XLA Modules:
  0.0 92.7 jit_solution(209079007637252482)
XLA Ops:
  0.0 1.1 %shard_map.64 = (s32[16,64]{1,0:T(8,128)S(1)}, s32[2,8]{1,0:T(2,128)S(4)}, bf16[8,128,256]{2,1,0:T(8,128)(2,1)S(1)}, bf16[2,128,256]{2,1,0:T(8,128)(2,1)S(1)}) custom-call(s32[16,64]{1,0:T(8,128)} %bitcast.25, s32[2,8]{1,0:T(2,128)} %bitcast.26, bf16[8,128,256]{2,1,0:T(8,128)(2,1)} %bitcast.24), custom_call_target="tpu_custom_call" | custom-call | bytes 524288 | tf_op jit(solution)/shard_map/pallas_call | solution.py:272
  1.1 4.1 %collective-permute-start = (bf16[2,128,256]{2,1,0:T(8,128)(2,1)S(1)}, bf16[2,128,256]{2,1,0:T(8,128)(2,1)S(1)}, u32[]{:S(2)}, u32[]{:S(2)}) collective-permute-start(bf16[2,128,256]{2,1,0:T(8,128)(2,1)S(1)} %get-tuple-element.50), channel_id=1, source_target_pairs={{0,16},{4,20},{8,24},{12,28},{16,0},{20,4},{24,8},{28,12},{1,17},{... | collective-permute-start | bytes 393224 | tf_op jit(solution)/shard_map/ppermute | solution.py:21
  5.2 0.3 shard_map.65
  5.5 0.1 collective-permute-start.4
  5.6 3.8 %collective-permute-start.5 = (bf16[1,128,256]{2,1,0:T(8,128)(2,1)S(1)}, bf16[1,128,256]{2,1,0:T(8,128)(2,1)S(1)}, u32[]{:S(2)}, u32[]{:S(2)}) collective-permute-start(bf16[1,128,256]{2,1,0:T(8,128)(2,1)S(1)} %get-tuple-element.57), channel_id=1, source_target_pairs={{0,20},{4,16},{8,28},{12,24},{16,4},{20,0},{24,12},{28,8},{1,21},{... | collective-permute-start | bytes 196616 | tf_op jit(solution)/shard_map/ppermute | solution.py:21
  9.4 5.8 %collective-permute-done.pair_ref.refs_0_ = bf16[2,128,256]{2,1,0:T(8,128)(2,1)S(1)} collective-permute-done((bf16[2,128,256]{2,1,0:T(8,128)(2,1)S(1)}, bf16[2,128,256]{2,1,0:T(8,128)(2,1)S(1)}, u32[]{:S(2)}, u32[]{:S(2)}) %collective-permute-start) | collective-permute-done | bytes 131104 | tf_op jit(solution)/shard_map/ppermute | solution.py:21
  15.2 1.9 %collective-permute-start.1 = (bf16[3,128,256]{2,1,0:T(8,128)(2,1)S(1)}, bf16[3,128,256]{2,1,0:T(8,128)(2,1)S(1)}, u32[]{:S(2)}, u32[]{:S(2)}) collective-permute-start(bf16[3,128,256]{2,1,0:T(8,128)(2,1)S(1)} %get-tuple-element.53), channel_id=1, source_target_pairs={{0,4},{4,0},{8,12},{12,8},{16,20},{20,16},{24,28},{28,24},{1,5},{5... | collective-permute-start | bytes 589832 | tf_op jit(solution)/shard_map/ppermute | solution.py:21
  17.1 2.5 %collective-permute-start.6 = (bf16[1,128,256]{2,1,0:T(8,128)(2,1)S(1)}, bf16[1,128,256]{2,1,0:T(8,128)(2,1)S(1)}, u32[]{:S(2)}, u32[]{:S(2)}) collective-permute-start(bf16[1,128,256]{2,1,0:T(8,128)(2,1)S(1)} %get-tuple-element.58), channel_id=1, source_target_pairs={{0,24},{4,28},{8,16},{12,20},{16,8},{20,12},{24,0},{28,4},{1,25},{... | collective-permute-start | bytes 196616 | tf_op jit(solution)/shard_map/ppermute | solution.py:21
  19.6 1.0 %collective-permute-start.7 = (bf16[1,128,256]{2,1,0:T(8,128)(2,1)S(1)}, bf16[1,128,256]{2,1,0:T(8,128)(2,1)S(1)}, u32[]{:S(2)}, u32[]{:S(2)}) collective-permute-start(bf16[1,128,256]{2,1,0:T(8,128)(2,1)S(1)} %get-tuple-element.59), channel_id=1, source_target_pairs={{0,28},{4,24},{8,20},{12,16},{16,12},{20,8},{24,4},{28,0},{1,29},{... | collective-permute-start | bytes 196616 | tf_op jit(solution)/shard_map/ppermute | solution.py:21
  20.6 3.3 %collective-permute-start.3 = (bf16[2,128,256]{2,1,0:T(8,128)(2,1)S(1)}, bf16[2,128,256]{2,1,0:T(8,128)(2,1)S(1)}, u32[]{:S(2)}, u32[]{:S(2)}) collective-permute-start(bf16[2,128,256]{2,1,0:T(8,128)(2,1)S(1)} %get-tuple-element.55), channel_id=1, source_target_pairs={{0,12},{4,8},{8,4},{12,0},{16,28},{20,24},{24,20},{28,16},{1,13},{... | collective-permute-start | bytes 393224 | tf_op jit(solution)/shard_map/ppermute | solution.py:21
  23.9 3.3 %collective-permute-done.7.refs_7_ = bf16[1,128,256]{2,1,0:T(8,128)(2,1)S(1)} collective-permute-done((bf16[1,128,256]{2,1,0:T(8,128)(2,1)S(1)}, bf16[1,128,256]{2,1,0:T(8,128)(2,1)S(1)}, u32[]{:S(2)}, u32[]{:S(2)}) %collective-permute-start.7) | collective-permute-done | bytes 65568 | tf_op jit(solution)/shard_map/ppermute | solution.py:21
  27.2 2.2 %shard_map.66 = (s32[16,64]{1,0:T(8,128)S(4)}, bf16[8,16,128,128]{3,2,1,0:T(8,128)(2,1)S(1)}) custom-call(s32[2,8]{1,0:T(2,128)S(4)} %get-tuple-element.44.mig, s32[16,64]{1,0:T(8,128)S(1)} %get-tuple-element.45.tiles_ref, bf16[8,16,128,128]{3,2,1,0:T(8,128)(2,1)} %adjacency_ref.1), custom_call_target="tpu_custom_call" | custom-call | bytes 4194304 | tf_op jit(solution)/shard_map/pallas_call | solution.py:272
  29.5 1.8 %collective-permute-done.3.refs_3_ = bf16[2,128,256]{2,1,0:T(8,128)(2,1)S(1)} collective-permute-done((bf16[2,128,256]{2,1,0:T(8,128)(2,1)S(1)}, bf16[2,128,256]{2,1,0:T(8,128)(2,1)S(1)}, u32[]{:S(2)}, u32[]{:S(2)}) %collective-permute-start.3) | collective-permute-done | bytes 131104 | tf_op jit(solution)/shard_map/ppermute | solution.py:21
  31.3 0.1 collective-permute-done.8.refs_8_
  31.4 1.3 %collective-permute-done.9.refs_9_ = bf16[1,128,256]{2,1,0:T(8,128)(2,1)S(1)} collective-permute-done((bf16[1,128,256]{2,1,0:T(8,128)(2,1)S(1)}, bf16[1,128,256]{2,1,0:T(8,128)(2,1)S(1)}, u32[]{:S(2)}, u32[]{:S(2)}) %collective-permute-start.9) | collective-permute-done | bytes 65568 | tf_op jit(solution)/shard_map/ppermute | solution.py:21
  32.7 0.7 shard_map.68
  33.4 0.6 shard_map.70
  34.1 1.3 %shard_map.69 = (bf16[2,128,256]{2,1,0:T(8,128)(2,1)S(1)}, bf16[2,128,256]{2,1,0:T(8,128)(2,1)S(1)}) custom-call(s32[16,64]{1,0:T(8,128)S(4)} %get-tuple-element.48.table_ref, bf16[8,16,128,128]{3,2,1,0:T(8,128)(2,1)S(1)} %get-tuple-element.49.adjacency_ref, bf16[24,128,256]{2,1,0:T(8,128)(2,1)S(1)} %get-tuple-element.62.pool_ref), custom_call_target="tpu_custom_call" | custom-call | flops 536870912 | bytes 2097152 | tf_op jit(solution)/shard_map/pallas_call | solution.py:272
  35.4 0.1 collective-permute-start.12
  35.4 1.9 %collective-permute-start.10 = (bf16[256,256]{1,0:T(8,128)(2,1)S(1)}, bf16[256,256]{1,0:T(8,128)(2,1)S(1)}, u32[]{:S(2)}, u32[]{:S(2)}) collective-permute-start(bf16[256,256]{1,0:T(8,128)(2,1)S(1)} %bitcast.23), channel_id=1, source_target_pairs={{0,1},{1,0},{2,3},{3,2},{4,5},{5,4},{6,7},{7,6},{8,9},{9,8},{10,11... | collective-permute-start | bytes 393224 | tf_op jit(solution)/shard_map/ppermute | solution.py:21
  37.4 0.2 collective-permute-start.11
  37.6 3.3 %collective-permute-done.12.refs_3_ = bf16[256,256]{1,0:T(8,128)(2,1)S(1)} collective-permute-done((bf16[256,256]{1,0:T(8,128)(2,1)S(1)}, bf16[256,256]{1,0:T(8,128)(2,1)S(1)}, u32[]{:S(2)}, u32[]{:S(2)}) %collective-permute-start.12) | collective-permute-done | bytes 131104 | tf_op jit(solution)/shard_map/ppermute | solution.py:21
  40.9 3.2 %collective-permute-done.11.refs_2_ = bf16[256,256]{1,0:T(8,128)(2,1)S(1)} collective-permute-done((bf16[256,256]{1,0:T(8,128)(2,1)S(1)}, bf16[256,256]{1,0:T(8,128)(2,1)S(1)}, u32[]{:S(2)}, u32[]{:S(2)}) %collective-permute-start.11) | collective-permute-done | bytes 131104 | tf_op jit(solution)/shard_map/ppermute | solution.py:21
  44.0 1.3 %shard_map.71 = (bf16[256,256]{1,0:T(8,128)(2,1)S(1)}, bf16[256,256]{1,0:T(8,128)(2,1)S(1)}, bf16[256,256]{1,0:T(8,128)(2,1)S(1)}, bf16[256,256]{1,0:T(8,128)(2,1)S(1)}) custom-call(bf16[1024,1024]{1,0:T(8,128)(2,1)S(1)} %copy-done, bf16[1024,1024]{1,0:T(8,128)(2,1)S(1)} %copy-done.1, bf16[256,256]{1,0:T(8,128)(2,1)S(1)} %bitcast.20, ...), custom_call_target="tpu_custom_call" | custom-call | flops 1073741824 | bytes 4194304 | tf_op jit(solution)/shard_map/pallas_call | solution.py:272
  45.3 0.1 collective-permute-start.13
  45.4 0.4 collective-permute-start.14
  45.8 1.5 %collective-permute-start.15 = (bf16[256,256]{1,0:T(8,128)(2,1)S(1)}, bf16[256,256]{1,0:T(8,128)(2,1)S(1)}, u32[]{:S(2)}, u32[]{:S(2)}) collective-permute-start(bf16[256,256]{1,0:T(8,128)(2,1)S(1)} %get-tuple-element.69), channel_id=1, source_target_pairs={{0,3},{1,2},{2,1},{3,0},{4,7},{5,6},{6,5},{7,4},{8,11},{9,10},{10,... | collective-permute-start | bytes 393224 | tf_op jit(solution)/shard_map/ppermute | solution.py:21
  47.2 4.6 %collective-permute-done.14 = bf16[256,256]{1,0:T(8,128)(2,1)S(1)} collective-permute-done((bf16[256,256]{1,0:T(8,128)(2,1)S(1)}, bf16[256,256]{1,0:T(8,128)(2,1)S(1)}, u32[]{:S(2)}, u32[]{:S(2)}) %collective-permute-start.14) | collective-permute-done | bytes 131104 | tf_op jit(solution)/shard_map/ppermute | solution.py:21
  51.8 1.7 %collective-permute-done.15 = bf16[256,256]{1,0:T(8,128)(2,1)S(1)} collective-permute-done((bf16[256,256]{1,0:T(8,128)(2,1)S(1)}, bf16[256,256]{1,0:T(8,128)(2,1)S(1)}, u32[]{:S(2)}, u32[]{:S(2)}) %collective-permute-start.15) | collective-permute-done | bytes 131104 | tf_op jit(solution)/shard_map/ppermute | solution.py:21
  53.6 0.1 shard_map.72
  53.6 2.0 %collective-permute-start.16 = (bf16[2,128,256]{2,1,0:T(8,128)(2,1)S(1)}, bf16[2,128,256]{2,1,0:T(8,128)(2,1)S(1)}, u32[]{:S(2)}, u32[]{:S(2)}) collective-permute-start(bf16[2,128,256]{2,1,0:T(8,128)(2,1)S(1)} %get-tuple-element.70), channel_id=1, source_target_pairs={{0,16},{4,20},{8,24},{12,28},{16,0},{20,4},{24,8},{28,12},{1,17},{... | collective-permute-start | bytes 393224 | tf_op jit(solution)/shard_map/ppermute | solution.py:21
  55.7 1.0 %collective-permute-start.20 = (bf16[1,128,256]{2,1,0:T(8,128)(2,1)S(1)}, bf16[1,128,256]{2,1,0:T(8,128)(2,1)S(1)}, u32[]{:S(2)}, u32[]{:S(2)}) collective-permute-start(bf16[1,128,256]{2,1,0:T(8,128)(2,1)S(1)} %get-tuple-element.75), channel_id=1, source_target_pairs={{0,16},{4,20},{8,24},{12,28},{16,0},{20,4},{24,8},{28,12},{1,17},{... | collective-permute-start | bytes 196616 | tf_op jit(solution)/shard_map/ppermute | solution.py:21
  56.6 1.9 %collective-permute-start.21 = (bf16[1,128,256]{2,1,0:T(8,128)(2,1)S(1)}, bf16[1,128,256]{2,1,0:T(8,128)(2,1)S(1)}, u32[]{:S(2)}, u32[]{:S(2)}) collective-permute-start(bf16[1,128,256]{2,1,0:T(8,128)(2,1)S(1)} %get-tuple-element.76), channel_id=1, source_target_pairs={{0,20},{4,16},{8,28},{12,24},{16,4},{20,0},{24,12},{28,8},{1,21},{... | collective-permute-start | bytes 196616 | tf_op jit(solution)/shard_map/ppermute | solution.py:21
  58.6 7.5 %collective-permute-done.16.pair_ref.refs_4_ = bf16[2,128,256]{2,1,0:T(8,128)(2,1)S(1)} collective-permute-done((bf16[2,128,256]{2,1,0:T(8,128)(2,1)S(1)}, bf16[2,128,256]{2,1,0:T(8,128)(2,1)S(1)}, u32[]{:S(2)}, u32[]{:S(2)}) %collective-permute-start.16) | collective-permute-done | bytes 131104 | tf_op jit(solution)/shard_map/ppermute | solution.py:21
  66.1 1.3 %collective-permute-start.17 = (bf16[3,128,256]{2,1,0:T(8,128)(2,1)S(1)}, bf16[3,128,256]{2,1,0:T(8,128)(2,1)S(1)}, u32[]{:S(2)}, u32[]{:S(2)}) collective-permute-start(bf16[3,128,256]{2,1,0:T(8,128)(2,1)S(1)} %get-tuple-element.72), channel_id=1, source_target_pairs={{0,4},{4,0},{8,12},{12,8},{16,20},{20,16},{24,28},{28,24},{1,5},{5... | collective-permute-start | bytes 589832 | tf_op jit(solution)/shard_map/ppermute | solution.py:21
  67.5 2.1 %collective-permute-start.22 = (bf16[1,128,256]{2,1,0:T(8,128)(2,1)S(1)}, bf16[1,128,256]{2,1,0:T(8,128)(2,1)S(1)}, u32[]{:S(2)}, u32[]{:S(2)}) collective-permute-start(bf16[1,128,256]{2,1,0:T(8,128)(2,1)S(1)} %get-tuple-element.77), channel_id=1, source_target_pairs={{0,24},{4,28},{8,16},{12,20},{16,8},{20,12},{24,0},{28,4},{1,25},{... | collective-permute-start | bytes 196616 | tf_op jit(solution)/shard_map/ppermute | solution.py:21
  69.5 2.0 %collective-permute-start.23 = (bf16[1,128,256]{2,1,0:T(8,128)(2,1)S(1)}, bf16[1,128,256]{2,1,0:T(8,128)(2,1)S(1)}, u32[]{:S(2)}, u32[]{:S(2)}) collective-permute-start(bf16[1,128,256]{2,1,0:T(8,128)(2,1)S(1)} %get-tuple-element.78), channel_id=1, source_target_pairs={{0,28},{4,24},{8,20},{12,16},{16,12},{20,8},{24,4},{28,0},{1,29},{... | collective-permute-start | bytes 196616 | tf_op jit(solution)/shard_map/ppermute | solution.py:21
  71.5 2.7 %collective-permute-start.19 = (bf16[2,128,256]{2,1,0:T(8,128)(2,1)S(1)}, bf16[2,128,256]{2,1,0:T(8,128)(2,1)S(1)}, u32[]{:S(2)}, u32[]{:S(2)}) collective-permute-start(bf16[2,128,256]{2,1,0:T(8,128)(2,1)S(1)} %get-tuple-element.74), channel_id=1, source_target_pairs={{0,12},{4,8},{8,4},{12,0},{16,28},{20,24},{24,20},{28,16},{1,13},{... | collective-permute-start | bytes 393224 | tf_op jit(solution)/shard_map/ppermute | solution.py:21
  74.3 2.9 %collective-permute-done.23.refs_11_ = bf16[1,128,256]{2,1,0:T(8,128)(2,1)S(1)} collective-permute-done((bf16[1,128,256]{2,1,0:T(8,128)(2,1)S(1)}, bf16[1,128,256]{2,1,0:T(8,128)(2,1)S(1)}, u32[]{:S(2)}, u32[]{:S(2)}) %collective-permute-start.23) | collective-permute-done | bytes 65568 | tf_op jit(solution)/shard_map/ppermute | solution.py:21
  77.2 1.4 %collective-permute-done.18.refs_6_ = bf16[2,128,256]{2,1,0:T(8,128)(2,1)S(1)} collective-permute-done((bf16[2,128,256]{2,1,0:T(8,128)(2,1)S(1)}, bf16[2,128,256]{2,1,0:T(8,128)(2,1)S(1)}, u32[]{:S(2)}, u32[]{:S(2)}) %collective-permute-start.18) | collective-permute-done | bytes 131104 | tf_op jit(solution)/shard_map/ppermute | solution.py:21
  78.6 3.5 %collective-permute-done.19.refs_7_ = bf16[2,128,256]{2,1,0:T(8,128)(2,1)S(1)} collective-permute-done((bf16[2,128,256]{2,1,0:T(8,128)(2,1)S(1)}, bf16[2,128,256]{2,1,0:T(8,128)(2,1)S(1)}, u32[]{:S(2)}, u32[]{:S(2)}) %collective-permute-start.19) | collective-permute-done | bytes 131104 | tf_op jit(solution)/shard_map/ppermute | solution.py:21
  82.1 0.6 collective-permute-done.24.refs_12_
  82.6 0.9 collective-permute-done.25.refs_13_
  83.6 0.7 shard_map.74
  84.3 1.3 %collective-permute-start.26 = (bf16[2,128,256]{2,1,0:T(8,128)(2,1)S(1)}, bf16[2,128,256]{2,1,0:T(8,128)(2,1)S(1)}, u32[]{:S(2)}, u32[]{:S(2)}) collective-permute-start(bf16[2,128,256]{2,1,0:T(8,128)(2,1)S(1)} %get-tuple-element.81), channel_id=1, source_target_pairs={{0,4},{4,8},{8,12},{12,16},{16,20},{20,24},{24,28},{28,0},{1,5},{5... | collective-permute-start | bytes 393224 | tf_op jit(solution)/shard_map/ppermute | solution.py:392
  85.6 2.8 %shard_map.75.out_in_ref = bf16[8,128,256]{2,1,0:T(8,128)(2,1)} custom-call(s32[16,64]{1,0:T(8,128)S(4)} %get-tuple-element.48.table_ref, s32[16]{0:T(128)S(4)} %get-tuple-element.47.slots_ref, bf16[8,16,128,128]{3,2,1,0:T(8,128)(2,1)S(1)} %get-tuple-element.49.adjacency_ref, bf16[24,128,256]{2,1,0:T(8,128)(2,1)S(1)} %get-tuple-element.82.pool_ref), custom_call_target="tpu_custom_call" | custom-call | flops 805306368 | bytes 3145728 | tf_op jit(solution)/shard_map/pallas_call | solution.py:272
  88.4 3.6 %collective-permute-done.26.moved_ref = bf16[2,128,256]{2,1,0:T(8,128)(2,1)S(1)} collective-permute-done((bf16[2,128,256]{2,1,0:T(8,128)(2,1)S(1)}, bf16[2,128,256]{2,1,0:T(8,128)(2,1)S(1)}, u32[]{:S(2)}, u32[]{:S(2)}) %collective-permute-start.26) | collective-permute-done | bytes 131104 | tf_op jit(solution)/shard_map/ppermute | solution.py:392
  92.0 0.7 shard_map.76
  (23 shorter events, 0.2 us)
Async XLA Ops:
  1.1 14.1 %collective-permute-start = (bf16[2,128,256]{2,1,0:T(8,128)(2,1)S(1)}, bf16[2,128,256]{2,1,0:T(8,128)(2,1)S(1)}, u32[]{:S(2)}, u32[]{:S(2)}) collective-permute-start(bf16[2,128,256]{2,1,0:T(8,128)(2,1)S(1)} %get-tuple-element.50), channel_id=1, source_target_pairs={{0,16},{4,20},{8,24},{12,28},{16,0},{20,4},{24,8},{28,12},{1,17},{... | collective-permute-start | bytes 393224 | tf_op jit(solution)/shard_map/ppermute | solution.py:21
  5.5 15.1 %collective-permute-start.4 = (bf16[1,128,256]{2,1,0:T(8,128)(2,1)S(1)}, bf16[1,128,256]{2,1,0:T(8,128)(2,1)S(1)}, u32[]{:S(2)}, u32[]{:S(2)}) collective-permute-start(bf16[1,128,256]{2,1,0:T(8,128)(2,1)S(1)} %get-tuple-element.56), channel_id=1, source_target_pairs={{0,16},{4,20},{8,24},{12,28},{16,0},{20,4},{24,8},{28,12},{1,17},{... | collective-permute-start | bytes 196616 | tf_op jit(solution)/shard_map/ppermute | solution.py:21
  5.6 15.0 %collective-permute-start.5 = (bf16[1,128,256]{2,1,0:T(8,128)(2,1)S(1)}, bf16[1,128,256]{2,1,0:T(8,128)(2,1)S(1)}, u32[]{:S(2)}, u32[]{:S(2)}) collective-permute-start(bf16[1,128,256]{2,1,0:T(8,128)(2,1)S(1)} %get-tuple-element.57), channel_id=1, source_target_pairs={{0,20},{4,16},{8,28},{12,24},{16,4},{20,0},{24,12},{28,8},{1,21},{... | collective-permute-start | bytes 196616 | tf_op jit(solution)/shard_map/ppermute | solution.py:21
  15.2 17.4 %collective-permute-start.1 = (bf16[3,128,256]{2,1,0:T(8,128)(2,1)S(1)}, bf16[3,128,256]{2,1,0:T(8,128)(2,1)S(1)}, u32[]{:S(2)}, u32[]{:S(2)}) collective-permute-start(bf16[3,128,256]{2,1,0:T(8,128)(2,1)S(1)} %get-tuple-element.53), channel_id=1, source_target_pairs={{0,4},{4,0},{8,12},{12,8},{16,20},{20,16},{24,28},{28,24},{1,5},{5... | collective-permute-start | bytes 589832 | tf_op jit(solution)/shard_map/ppermute | solution.py:21
  17.1 6.8 %collective-permute-start.6 = (bf16[1,128,256]{2,1,0:T(8,128)(2,1)S(1)}, bf16[1,128,256]{2,1,0:T(8,128)(2,1)S(1)}, u32[]{:S(2)}, u32[]{:S(2)}) collective-permute-start(bf16[1,128,256]{2,1,0:T(8,128)(2,1)S(1)} %get-tuple-element.58), channel_id=1, source_target_pairs={{0,24},{4,28},{8,16},{12,20},{16,8},{20,12},{24,0},{28,4},{1,25},{... | collective-permute-start | bytes 196616 | tf_op jit(solution)/shard_map/ppermute | solution.py:21
  19.6 7.7 %collective-permute-start.7 = (bf16[1,128,256]{2,1,0:T(8,128)(2,1)S(1)}, bf16[1,128,256]{2,1,0:T(8,128)(2,1)S(1)}, u32[]{:S(2)}, u32[]{:S(2)}) collective-permute-start(bf16[1,128,256]{2,1,0:T(8,128)(2,1)S(1)} %get-tuple-element.59), channel_id=1, source_target_pairs={{0,28},{4,24},{8,20},{12,16},{16,12},{20,8},{24,4},{28,0},{1,29},{... | collective-permute-start | bytes 196616 | tf_op jit(solution)/shard_map/ppermute | solution.py:21
  20.6 8.9 %collective-permute-start.2 = (bf16[2,128,256]{2,1,0:T(8,128)(2,1)S(1)}, bf16[2,128,256]{2,1,0:T(8,128)(2,1)S(1)}, u32[]{:S(2)}, u32[]{:S(2)}) collective-permute-start(bf16[2,128,256]{2,1,0:T(8,128)(2,1)S(1)} %get-tuple-element.54), channel_id=1, source_target_pairs={{0,8},{4,12},{8,0},{12,4},{16,24},{20,28},{24,16},{28,20},{1,9},{5... | collective-permute-start | bytes 393224 | tf_op jit(solution)/shard_map/ppermute | solution.py:21
  20.6 10.7 %collective-permute-start.3 = (bf16[2,128,256]{2,1,0:T(8,128)(2,1)S(1)}, bf16[2,128,256]{2,1,0:T(8,128)(2,1)S(1)}, u32[]{:S(2)}, u32[]{:S(2)}) collective-permute-start(bf16[2,128,256]{2,1,0:T(8,128)(2,1)S(1)} %get-tuple-element.55), channel_id=1, source_target_pairs={{0,12},{4,8},{8,4},{12,0},{16,28},{20,24},{24,20},{28,16},{1,13},{... | collective-permute-start | bytes 393224 | tf_op jit(solution)/shard_map/ppermute | solution.py:21
  23.8 7.5 %collective-permute-start.8 = (bf16[1,128,256]{2,1,0:T(8,128)(2,1)S(1)}, bf16[1,128,256]{2,1,0:T(8,128)(2,1)S(1)}, u32[]{:S(2)}, u32[]{:S(2)}) collective-permute-start(bf16[1,128,256]{2,1,0:T(8,128)(2,1)S(1)} %get-tuple-element.60), channel_id=1, source_target_pairs={{0,8},{4,12},{8,0},{12,4},{16,24},{20,28},{24,16},{28,20},{1,9},{5... | collective-permute-start | bytes 196616 | tf_op jit(solution)/shard_map/ppermute | solution.py:21
  27.2 5.4 %collective-permute-start.9 = (bf16[1,128,256]{2,1,0:T(8,128)(2,1)S(1)}, bf16[1,128,256]{2,1,0:T(8,128)(2,1)S(1)}, u32[]{:S(2)}, u32[]{:S(2)}) collective-permute-start(bf16[1,128,256]{2,1,0:T(8,128)(2,1)S(1)} %get-tuple-element.61), channel_id=1, source_target_pairs={{0,12},{4,8},{8,4},{12,0},{16,28},{20,24},{24,20},{28,16},{1,13},{... | collective-permute-start | bytes 196616 | tf_op jit(solution)/shard_map/ppermute | solution.py:21
  34.1 10.0 %copy-start = (bf16[1024,1024]{1,0:T(8,128)(2,1)S(1)}, bf16[1024,1024]{1,0:T(8,128)(2,1)}, u32[]{:S(2)}) copy-start(bf16[1024,1024]{1,0:T(8,128)(2,1)} %weight_one_ref.1) | copy-start | bytes 6291460
  34.1 10.0 %copy-start.1 = (bf16[1024,1024]{1,0:T(8,128)(2,1)S(1)}, bf16[1024,1024]{1,0:T(8,128)(2,1)}, u32[]{:S(2)}) copy-start(bf16[1024,1024]{1,0:T(8,128)(2,1)} %weight_two_ref.1) | copy-start | bytes 6291460
  35.4 5.5 %collective-permute-start.12 = (bf16[256,256]{1,0:T(8,128)(2,1)S(1)}, bf16[256,256]{1,0:T(8,128)(2,1)S(1)}, u32[]{:S(2)}, u32[]{:S(2)}) collective-permute-start(bf16[256,256]{1,0:T(8,128)(2,1)S(1)} %bitcast.21), channel_id=1, source_target_pairs={{0,3},{1,2},{2,1},{3,0},{4,7},{5,6},{6,5},{7,4},{8,11},{9,10},{10,... | collective-permute-start | bytes 393224 | tf_op jit(solution)/shard_map/ppermute | solution.py:21
  35.4 5.4 %collective-permute-start.10 = (bf16[256,256]{1,0:T(8,128)(2,1)S(1)}, bf16[256,256]{1,0:T(8,128)(2,1)S(1)}, u32[]{:S(2)}, u32[]{:S(2)}) collective-permute-start(bf16[256,256]{1,0:T(8,128)(2,1)S(1)} %bitcast.23), channel_id=1, source_target_pairs={{0,1},{1,0},{2,3},{3,2},{4,5},{5,4},{6,7},{7,6},{8,9},{9,8},{10,11... | collective-permute-start | bytes 393224 | tf_op jit(solution)/shard_map/ppermute | solution.py:21
  37.4 6.7 %collective-permute-start.11 = (bf16[256,256]{1,0:T(8,128)(2,1)S(1)}, bf16[256,256]{1,0:T(8,128)(2,1)S(1)}, u32[]{:S(2)}, u32[]{:S(2)}) collective-permute-start(bf16[256,256]{1,0:T(8,128)(2,1)S(1)} %bitcast.22), channel_id=1, source_target_pairs={{0,2},{1,3},{2,0},{3,1},{4,6},{5,7},{6,4},{7,5},{8,10},{9,11},{10,... | collective-permute-start | bytes 393224 | tf_op jit(solution)/shard_map/ppermute | solution.py:21
  45.3 1.9 %collective-permute-start.13 = (bf16[256,256]{1,0:T(8,128)(2,1)S(1)}, bf16[256,256]{1,0:T(8,128)(2,1)S(1)}, u32[]{:S(2)}, u32[]{:S(2)}) collective-permute-start(bf16[256,256]{1,0:T(8,128)(2,1)S(1)} %get-tuple-element.67), channel_id=1, source_target_pairs={{0,1},{1,0},{2,3},{3,2},{4,5},{5,4},{6,7},{7,6},{8,9},{9,8},{10,11... | collective-permute-start | bytes 393224 | tf_op jit(solution)/shard_map/ppermute | solution.py:21
  45.4 6.4 %collective-permute-start.14 = (bf16[256,256]{1,0:T(8,128)(2,1)S(1)}, bf16[256,256]{1,0:T(8,128)(2,1)S(1)}, u32[]{:S(2)}, u32[]{:S(2)}) collective-permute-start(bf16[256,256]{1,0:T(8,128)(2,1)S(1)} %get-tuple-element.68), channel_id=1, source_target_pairs={{0,2},{1,3},{2,0},{3,1},{4,6},{5,7},{6,4},{7,5},{8,10},{9,11},{10,... | collective-permute-start | bytes 393224 | tf_op jit(solution)/shard_map/ppermute | solution.py:21
  45.8 7.8 %collective-permute-start.15 = (bf16[256,256]{1,0:T(8,128)(2,1)S(1)}, bf16[256,256]{1,0:T(8,128)(2,1)S(1)}, u32[]{:S(2)}, u32[]{:S(2)}) collective-permute-start(bf16[256,256]{1,0:T(8,128)(2,1)S(1)} %get-tuple-element.69), channel_id=1, source_target_pairs={{0,3},{1,2},{2,1},{3,0},{4,7},{5,6},{6,5},{7,4},{8,11},{9,10},{10,... | collective-permute-start | bytes 393224 | tf_op jit(solution)/shard_map/ppermute | solution.py:21
  53.6 12.5 %collective-permute-start.16 = (bf16[2,128,256]{2,1,0:T(8,128)(2,1)S(1)}, bf16[2,128,256]{2,1,0:T(8,128)(2,1)S(1)}, u32[]{:S(2)}, u32[]{:S(2)}) collective-permute-start(bf16[2,128,256]{2,1,0:T(8,128)(2,1)S(1)} %get-tuple-element.70), channel_id=1, source_target_pairs={{0,16},{4,20},{8,24},{12,28},{16,0},{20,4},{24,8},{28,12},{1,17},{... | collective-permute-start | bytes 393224 | tf_op jit(solution)/shard_map/ppermute | solution.py:21
  55.7 15.8 %collective-permute-start.20 = (bf16[1,128,256]{2,1,0:T(8,128)(2,1)S(1)}, bf16[1,128,256]{2,1,0:T(8,128)(2,1)S(1)}, u32[]{:S(2)}, u32[]{:S(2)}) collective-permute-start(bf16[1,128,256]{2,1,0:T(8,128)(2,1)S(1)} %get-tuple-element.75), channel_id=1, source_target_pairs={{0,16},{4,20},{8,24},{12,28},{16,0},{20,4},{24,8},{28,12},{1,17},{... | collective-permute-start | bytes 196616 | tf_op jit(solution)/shard_map/ppermute | solution.py:21
  56.6 14.9 %collective-permute-start.21 = (bf16[1,128,256]{2,1,0:T(8,128)(2,1)S(1)}, bf16[1,128,256]{2,1,0:T(8,128)(2,1)S(1)}, u32[]{:S(2)}, u32[]{:S(2)}) collective-permute-start(bf16[1,128,256]{2,1,0:T(8,128)(2,1)S(1)} %get-tuple-element.76), channel_id=1, source_target_pairs={{0,20},{4,16},{8,28},{12,24},{16,4},{20,0},{24,12},{28,8},{1,21},{... | collective-permute-start | bytes 196616 | tf_op jit(solution)/shard_map/ppermute | solution.py:21
  66.1 17.4 %collective-permute-start.17 = (bf16[3,128,256]{2,1,0:T(8,128)(2,1)S(1)}, bf16[3,128,256]{2,1,0:T(8,128)(2,1)S(1)}, u32[]{:S(2)}, u32[]{:S(2)}) collective-permute-start(bf16[3,128,256]{2,1,0:T(8,128)(2,1)S(1)} %get-tuple-element.72), channel_id=1, source_target_pairs={{0,4},{4,0},{8,12},{12,8},{16,20},{20,16},{24,28},{28,24},{1,5},{5... | collective-permute-start | bytes 589832 | tf_op jit(solution)/shard_map/ppermute | solution.py:21
  67.5 6.8 %collective-permute-start.22 = (bf16[1,128,256]{2,1,0:T(8,128)(2,1)S(1)}, bf16[1,128,256]{2,1,0:T(8,128)(2,1)S(1)}, u32[]{:S(2)}, u32[]{:S(2)}) collective-permute-start(bf16[1,128,256]{2,1,0:T(8,128)(2,1)S(1)} %get-tuple-element.77), channel_id=1, source_target_pairs={{0,24},{4,28},{8,16},{12,20},{16,8},{20,12},{24,0},{28,4},{1,25},{... | collective-permute-start | bytes 196616 | tf_op jit(solution)/shard_map/ppermute | solution.py:21
  69.5 7.7 %collective-permute-start.23 = (bf16[1,128,256]{2,1,0:T(8,128)(2,1)S(1)}, bf16[1,128,256]{2,1,0:T(8,128)(2,1)S(1)}, u32[]{:S(2)}, u32[]{:S(2)}) collective-permute-start(bf16[1,128,256]{2,1,0:T(8,128)(2,1)S(1)} %get-tuple-element.78), channel_id=1, source_target_pairs={{0,28},{4,24},{8,20},{12,16},{16,12},{20,8},{24,4},{28,0},{1,29},{... | collective-permute-start | bytes 196616 | tf_op jit(solution)/shard_map/ppermute | solution.py:21
  71.5 7.1 %collective-permute-start.18 = (bf16[2,128,256]{2,1,0:T(8,128)(2,1)S(1)}, bf16[2,128,256]{2,1,0:T(8,128)(2,1)S(1)}, u32[]{:S(2)}, u32[]{:S(2)}) collective-permute-start(bf16[2,128,256]{2,1,0:T(8,128)(2,1)S(1)} %get-tuple-element.73), channel_id=1, source_target_pairs={{0,8},{4,12},{8,0},{12,4},{16,24},{20,28},{24,16},{28,20},{1,9},{5... | collective-permute-start | bytes 393224 | tf_op jit(solution)/shard_map/ppermute | solution.py:21
  71.5 10.6 %collective-permute-start.19 = (bf16[2,128,256]{2,1,0:T(8,128)(2,1)S(1)}, bf16[2,128,256]{2,1,0:T(8,128)(2,1)S(1)}, u32[]{:S(2)}, u32[]{:S(2)}) collective-permute-start(bf16[2,128,256]{2,1,0:T(8,128)(2,1)S(1)} %get-tuple-element.74), channel_id=1, source_target_pairs={{0,12},{4,8},{8,4},{12,0},{16,28},{20,24},{24,20},{28,16},{1,13},{... | collective-permute-start | bytes 393224 | tf_op jit(solution)/shard_map/ppermute | solution.py:21
  74.2 8.4 %collective-permute-start.24 = (bf16[1,128,256]{2,1,0:T(8,128)(2,1)S(1)}, bf16[1,128,256]{2,1,0:T(8,128)(2,1)S(1)}, u32[]{:S(2)}, u32[]{:S(2)}) collective-permute-start(bf16[1,128,256]{2,1,0:T(8,128)(2,1)S(1)} %get-tuple-element.79), channel_id=1, source_target_pairs={{0,8},{4,12},{8,0},{12,4},{16,24},{20,28},{24,16},{28,20},{1,9},{5... | collective-permute-start | bytes 196616 | tf_op jit(solution)/shard_map/ppermute | solution.py:21
  77.2 6.4 %collective-permute-start.25 = (bf16[1,128,256]{2,1,0:T(8,128)(2,1)S(1)}, bf16[1,128,256]{2,1,0:T(8,128)(2,1)S(1)}, u32[]{:S(2)}, u32[]{:S(2)}) collective-permute-start(bf16[1,128,256]{2,1,0:T(8,128)(2,1)S(1)} %get-tuple-element.80), channel_id=1, source_target_pairs={{0,12},{4,8},{8,4},{12,0},{16,28},{20,24},{24,20},{28,16},{1,13},{... | collective-permute-start | bytes 196616 | tf_op jit(solution)/shard_map/ppermute | solution.py:21
  84.3 7.7 %collective-permute-start.26 = (bf16[2,128,256]{2,1,0:T(8,128)(2,1)S(1)}, bf16[2,128,256]{2,1,0:T(8,128)(2,1)S(1)}, u32[]{:S(2)}, u32[]{:S(2)}) collective-permute-start(bf16[2,128,256]{2,1,0:T(8,128)(2,1)S(1)} %get-tuple-element.81), channel_id=1, source_target_pairs={{0,4},{4,8},{8,12},{12,16},{16,20},{20,24},{24,28},{28,0},{1,5},{5... | collective-permute-start | bytes 393224 | tf_op jit(solution)/shard_map/ppermute | solution.py:392

commit v2 on v1

--- a/solution.py
+++ b/solution.py
@@ -57,12 +57,18 @@
         far_refs[k - half][0] = own_ref[slots_ref[2 * k + 1]]
 
 
-def first_kernel(domains, rows, mig, tiles_ref, own_ref, slots_ref, which_ref, *sends):
+def first_kernel(domains, rows, mig, tiles_ref, own_ref, slots_ref, which_ref, deal_ref, *sends):
     half = domains // 2
     me = lax.axis_index("dom")
     mine0, mine1 = mig[0, me], mig[1, me]
     slots_ref[0] = mine0
     slots_ref[1] = mine1
+    deal_ref[0] = mine0
+    deal_ref[1] = mine1
+    place = jnp.int32(2)
+    for s in range(rows):
+        deal_ref[place] = s
+        place = place + jnp.where((mine0 == s) | (mine1 == s), 0, 1)
     opposite = me ^ half
     opposite_last = opposite * rows + mig[1, opposite]
 
@@ -117,33 +123,22 @@
     load.wait()
 
 
-def relay_kernel(half, which_ref, pair_ref, near_ref, first_ref, *outs):
-    first_ref[0:2] = near_ref[...]
-    first_ref[2] = pair_ref[which_ref[1]]
-    for k in range(2, half):
-        outs[k - 2][0] = pair_ref[which_ref[k]]
-
-
-def fill_pool(domains, chunks, arrived, pool_ref):
-    half = domains // 2
-    per = chunks[0].shape[0]
-    rows = per * len(chunks)
-    if len(chunks) == 1:
-        pool_ref[0:rows] = chunks[0][...]
-    else:
-        feat = lax.axis_index("feat")
-        for j, chunk in enumerate(chunks):
-            for i in range(per):
-                pool_ref[(feat ^ j) * per + i] = chunk[i]
+def relay_kernel(half, which_ref, pair_ref, *outs):
+    for k in range(1, half):
+        outs[k - 1][0] = pair_ref[which_ref[k]]
+
+
+def fill_pool(domains, own_ref, arrived, pool_ref):
+    half = domains // 2
+    rows = own_ref.shape[0]
+    pool_ref[0:rows] = own_ref[...]
     pair, near, far, relay = split_arrived(half, arrived)
     pool_ref[rows : rows + 2] = pair[...]
     for k in range(1, half):
-        pool_ref[rows + 2 * k : rows + 2 * k + 2] = near[k - 1][0:2]
-    pool_ref[rows + 2 * (half + 1)] = near[0][2]
+        pool_ref[rows + 2 * k : rows + 2 * k + 2] = near[k - 1][...]
+        pool_ref[rows + 2 * (half + k)] = relay[k - 1][0]
     for k in range(half, domains):
         pool_ref[rows + 2 * k + 1] = far[k - half][0]
-    for k in range(2, half):
-        pool_ref[rows + 2 * (half + k)] = relay[k - 2][0]
 
 
 def split_arrived(half, arrived):
@@ -166,28 +161,24 @@
     return total.astype(BF16)
 
 
-def first_sum_kernel(domains, feats, j, table_ref, adjacency_ref, own_ref, *refs):
+def first_sum_kernel(domains, feats, j, table_ref, deal_ref, adjacency_ref, own_ref, *refs):
     *arrived, pool_ref, out_ref = refs
-    fill_pool(domains, [own_ref], arrived, pool_ref)
-    sum_part(feats, j, table_ref, adjacency_ref, pool_ref, out_ref)
-
-
-def part_sum_kernel(feats, js, table_ref, adjacency_ref, pool_ref, *outs):
+    fill_pool(domains, own_ref, arrived, pool_ref)
+    part_sum_kernel(feats, [j], table_ref, deal_ref, adjacency_ref, pool_ref, out_ref)
+
+
+def part_sum_kernel(feats, js, table_ref, deal_ref, adjacency_ref, pool_ref, *outs):
     for j, out_ref in zip(js, outs, strict=True):
-        sum_part(feats, j, table_ref, adjacency_ref, pool_ref, out_ref)
-
-
-def sum_part(feats, j, table_ref, adjacency_ref, pool_ref, out_ref):
-    start = (lax.axis_index("feat") ^ j) * (adjacency_ref.shape[0] // feats)
-
-    @pl.loop(0, out_ref.shape[0])
-    def _(i):
-        out_ref[i] = sum_row(start + i, table_ref, adjacency_ref, pool_ref)
-
-
-def leaving_sum_kernel(domains, feats, table_ref, slots_ref, adjacency_ref, *refs):
-    *blocks, pool_ref, out_ref = refs
-    fill_pool(domains, blocks[:feats], blocks[feats:], pool_ref)
+        rank = lax.axis_index("feat") ^ j
+
+        @pl.loop(0, out_ref.shape[0])
+        def _(i, rank=rank, out_ref=out_ref):
+            out_ref[i] = sum_row(deal_ref[i * feats + rank], table_ref, adjacency_ref, pool_ref)
+
+
+def leaving_sum_kernel(domains, table_ref, slots_ref, adjacency_ref, own_ref, *refs):
+    *arrived, pool_ref, out_ref = refs
+    fill_pool(domains, own_ref, arrived, pool_ref)
 
     @pl.loop(0, out_ref.shape[0])
     def _(i):
@@ -202,17 +193,18 @@
             out_ref[r] = sum_row(r, table_ref, adjacency_ref, pool_ref)
 
 
-def dense_kernel(feats, weight_one_ref, weight_two_ref, *refs):
+def dense_kernel(feats, chunk, weight_one_ref, weight_two_ref, *refs):
     parts, outs, hidden_ref = refs[:feats], refs[feats : 2 * feats], refs[2 * feats]
     feat = lax.axis_index("feat")
-    width = parts[0].shape[1]
+    width = parts[0].shape[2]
     columns = weight_one_ref.shape[1]
+    rows = [part[chunk] for part in parts]
     for c in range(0, columns, width):
         total = None
         for j in range(feats):
             start = pl.multiple_of((feat ^ j) * width, width)
             part = jnp.dot(
-                parts[j][...],
+                rows[j],
                 weight_one_ref[pl.ds(start, width), c : c + width],
                 preferred_element_type=F32,
             )
@@ -220,23 +212,31 @@
         hidden_ref[:, c : c + width] = jnp.maximum(total, 0.0).astype(BF16)
     for j in range(feats):
         start = pl.multiple_of((feat ^ j) * width, width)
-        outs[j][...] = jnp.dot(
+        outs[j][0] = jnp.dot(
             hidden_ref[...],
             weight_two_ref[:, pl.ds(start, width)],
             preferred_element_type=F32,
         ).astype(BF16)
 
 
-def second_kernel(domains, feats, slots_ref, *refs):
-    chunks, pair_ref, sends, own_ref = refs[:feats], refs[feats], refs[feats + 1 : -1], refs[-1]
-    half = domains // 2
-    per = chunks[0].shape[0]
+def second_pair_kernel(*refs):
+    *blocks, pair_ref = refs
     feat = lax.axis_index("feat")
-    for j, chunk in enumerate(chunks):
-        for i in range(per):
-            own_ref[(feat ^ j) * per + i] = chunk[i]
-    for m in range(2):
-        pair_ref[m] = own_ref[slots_ref[m]]
+    for j, ref in enumerate(blocks):
+
+        @pl.when((feat ^ j) < 2)
+        def _(j=j, ref=ref):
+            pair_ref[feat ^ j] = ref[0]
+
+
+def second_kernel(domains, feats, slots_ref, deal_ref, *refs):
+    half = domains // 2
+    n_blocks = len(refs) - 1 - (domains - 1)
+    blocks, own_ref, sends = refs[:n_blocks], refs[n_blocks], refs[n_blocks + 1 :]
+    feat = lax.axis_index("feat")
+    for n, ref in enumerate(blocks):
+        i, j = divmod(n, feats)
+        own_ref[deal_ref[i * feats + (feat ^ j)]] = ref[0]
     write_sends(domains, slots_ref, own_ref, sends[: half - 1], sends[half - 1 :])
 
 
@@ -252,9 +252,9 @@
         copy.wait()
 
 
-def call(kernel, out_shape, in_specs, out_specs, scratch=(), flops=0, moved=0, **kwargs):
+def call(body, out_shape, in_specs, out_specs, scratch=(), flops=0, moved=0, **kwargs):
     run = pl.pallas_call(
-        kernel,
+        body,
         out_shape=out_shape,
         in_specs=in_specs,
         out_specs=out_specs,
@@ -279,17 +279,17 @@
     shape = pair.shape[1:]
     near, far = sends[: half - 1], sends[half - 1 :]
     pair = swap(pair, "dom", half)
-    near_z = [swap(near[k - 1], "dom", k) for k in range(2, half)]
+    near = [swap(near[k - 1], "dom", k) for k in range(1, half)]
     far = [swap(far[k - half], "dom", k) for k in range(half, domains)]
-    first, *relay = call(
+    relay = call(
         functools.partial(relay_kernel, half),
-        [block((3, *shape))] + [block((1, *shape))] * (half - 2),
-        [SMEM, VMEM, VMEM],
+        [block((1, *shape))] * (half - 1),
+        [SMEM, VMEM],
         [VMEM] * (half - 1),
         moved=4 * pair.size * half,
-    )(which, pair, near[0])
-    relay = [swap(relay[k - 2], "dom", k) for k in range(2, half)]
-    return [pair, swap(first, "dom", 1), *near_z, *far, *relay]
+    )(which, pair)
+    relay = [swap(relay[k - 1], "dom", k) for k in range(1, half)]
+    return [pair, *near, *far, *relay]
 
 
 def on_device(features, adjacency, tile_src, mig_slot, weight_one, weight_two):
@@ -318,11 +318,11 @@
         [pltpu.SemaphoreType.DMA((3,))],
         moved=features.size * 2,
     )(named, leaving_slots, blocks)
-    slots, which, *sends = call(
+    slots, which, deal, *sends = call(
         functools.partial(first_kernel, domains, rows),
-        [scalars((2 * domains,)), scalars((domains,)), *near_far],
+        [scalars((2 * domains,)), scalars((domains,)), scalars((rows + 1,)), *near_far],
         [SMEM, VMEM, VMEM],
-        [SMEM, SMEM] + [VMEM] * len(near_far),
+        [SMEM] * 3 + [VMEM] * len(near_far),
         moved=8 * size * width * domains,
     )(mig, named, own)
     arrived = exchange(domains, pair, sends, which)
@@ -335,60 +335,67 @@
         moved=adjacency.size * 2,
     )(mig, named, adjacency)
 
-    early = list(range(2, feats))
+    one = block((1, size, width))
+    whole = block((per, size, width))
     parts = [None] * feats
     pool_one, parts[2] = call(
         functools.partial(first_sum_kernel, domains, feats, 2),
-        [pool, block((per, size, width))],
-        [SMEM] + [VMEM] * (2 + len(arrived)),
+        [pool, whole],
+        [SMEM, SMEM] + [VMEM] * (2 + len(arrived)),
         [VMEM] * 2,
         flops=work * per,
         moved=read * per,
-    )(table, adjacency, own, *arrived)
-    for js in [[j] for j in early[1:]] + [[1, 0]]:
+    )(table, deal, adjacency, own, *arrived)
+    for js in [[j] for j in range(3, feats)] + [[1, 0]]:
         outs = call(
             functools.partial(part_sum_kernel, feats, js),
-            [block((per, size, width))] * len(js),
-            [SMEM, VMEM, VMEM],
+            [whole] * len(js),
+            [SMEM, SMEM, VMEM, VMEM],
             [VMEM] * len(js),
             flops=work * per * len(js),
             moved=read * per * len(js),
-        )(table, adjacency, pool_one)
+        )(table, deal, adjacency, pool_one)
         for j, out in zip(js, outs):
             parts[j] = out
-    parts = [p.reshape(per * size, width) for p in parts]
     parts = [p if j == 0 else swap(p, "feat", j) for j, p in enumerate(parts)]
 
-    chunks = call(
-        functools.partial(dense_kernel, feats),
-        [block((per * size, width))] * feats,
-        [VMEM] * (2 + feats),
+    columns = []
+    for i in range(per):
+        outs = call(
+            functools.partial(dense_kernel, feats, i),
+            [one] * feats,
+            [VMEM] * (2 + feats),
+            [VMEM] * feats,
+            [pltpu.VMEM((size, weight_one.shape[1]), BF16)],
+            flops=4 * size * weight_one.size,
+            moved=weight_one.size * 4,
+        )(weight_one, weight_two, *parts)
+        columns += [c if j == 0 else swap(c, "feat", j) for j, c in enumerate(outs)]
+
+    pair = call(
+        second_pair_kernel,
+        [block((2, size, width))],
         [VMEM] * feats,
-        [pltpu.VMEM((per * size, weight_one.shape[1]), BF16)],
-        flops=4 * per * size * weight_one.size,
-        moved=weight_one.size * 4,
-    )(weight_one, weight_two, *parts)
-    chunks = [c if j == 0 else swap(c, "feat", j) for j, c in enumerate(chunks)]
-    chunks = [c.reshape(per, size, width) for c in chunks]
-
-    pair, *sends = call(
+        [VMEM],
+        moved=8 * size * width,
+    )(*columns[:feats])[0]
+    own, *sends = call(
         functools.partial(second_kernel, domains, feats),
-        [block((2, size, width)), *near_far],
-        [SMEM] + [VMEM] * feats,
+        [block((rows, size, width)), *near_far],
+        [SMEM, SMEM] + [VMEM] * len(columns),
         [VMEM] * (1 + len(near_far)),
-        [pltpu.VMEM((rows, size, width), BF16)],
         moved=8 * size * width * domains,
-    )(slots, *chunks)
+    )(slots, deal, *columns)
     arrived = exchange(domains, pair, sends, which)
 
     pool_two, leaving = call(
-        functools.partial(leaving_sum_kernel, domains, feats),
+        functools.partial(leaving_sum_kernel, domains),
         [pool, block((2, size, width))],
-        [SMEM, SMEM] + [VMEM] * (1 + feats + len(arrived)),
+        [SMEM, SMEM] + [VMEM] * (2 + len(arrived)),
         [VMEM] * 2,
         flops=work * 2,
         moved=read * 2,
-    )(table, slots, adjacency, *chunks, *arrived)
+    )(table, slots, adjacency, own, *arrived)
     moved = lax.ppermute(leaving, "dom", [(i, (i + 1) % domains) for i in range(domains)])
     out = call(
         staying_sum_kernel,

time: 92.9 us -> 90.2 us (0.971)
  waiting for transfers between devices: 45.5 us -> 32.1 us
  starting transfers between devices: 35.2 us -> 45.6 us
    ppermute x26 -> x31, waiting for transfers between devices: 41.9 us -> 28.7 us  [swap(): lax.ppermute(value, axis, [(i, i ^ flip) for i in range(lax.axis_size(axi...]
    ppermute x26 -> x31, starting transfers between devices: 33.9 us -> 44.1 us  [swap(): lax.ppermute(value, axis, [(i, i ^ flip) for i in range(lax.axis_size(axi...]
    pallas_call x13 -> x15, Pallas kernels: 11.8 us -> 12.1 us  [place_and_run(): return run(*placed)]
  transfers between devices with their start and end apart: 27 -> 32, of which waited for: 16 -> 15; matrix products, arithmetic and copies ran while one was open for 0% -> 0% of each run, Pallas kernels for 6% -> 7%
where the time goes in v2:
time: 90.2 us; the launch traced here: 90 us
  starting transfers between devices  45.6 us (51%)
  waiting for transfers between devices  32.1 us (36%)
  Pallas kernels  12.1 us (13%)
    ppermute x31, starting transfers between devices, swap(): lax.ppermute(value, axis, [(i, i ^ flip) for i in range(lax.axis_size(axi...  44.1 us
    ppermute x31, waiting for transfers between devices, swap(): lax.ppermute(value, axis, [(i, i ^ flip) for i in range(lax.axis_size(axi...  28.7 us
    pallas_call x15, Pallas kernels, place_and_run(): return run(*placed)  12.1 us
    ppermute x1, waiting for transfers between devices, on_device(): lax.ppermute(leaving, 'dom', [(i, (i + 1) % domains) for i in range(domai...  3.39 us
  transfers between devices with their start and end apart: 32, of which 15 were waited for; matrix products, arithmetic and copies ran while one was open for 0% of the time, Pallas kernels for 7%

profile of v2, /device:TPU:0, one launch (start us, length us, event | category | flops | bytes accessed | tf_op | source)
XLA Modules:
  0.0 90.0 jit_solution(15495823480286581331)
XLA Ops:
  0.0 1.1 %shard_map.64 = (s32[16,64]{1,0:T(8,128)S(1)}, s32[2,8]{1,0:T(2,128)S(4)}, bf16[8,128,256]{2,1,0:T(8,128)(2,1)S(1)}, bf16[2,128,256]{2,1,0:T(8,128)(2,1)S(1)}) custom-call(s32[16,64]{1,0:T(8,128)} %bitcast.5, s32[2,8]{1,0:T(2,128)} %bitcast.6, bf16[8,128,256]{2,1,0:T(8,128)(2,1)} %bitcast.4), custom_call_target="tpu_custom_call" | custom-call | bytes 524288 | tf_op jit(solution)/shard_map/pallas_call | solution.py:272
  1.1 4.1 %collective-permute-start = (bf16[2,128,256]{2,1,0:T(8,128)(2,1)S(1)}, bf16[2,128,256]{2,1,0:T(8,128)(2,1)S(1)}, u32[]{:S(2)}, u32[]{:S(2)}) collective-permute-start(bf16[2,128,256]{2,1,0:T(8,128)(2,1)S(1)} %get-tuple-element.56), channel_id=1, source_target_pairs={{0,16},{4,20},{8,24},{12,28},{16,0},{20,4},{24,8},{28,12},{1,17},{... | collective-permute-start | bytes 393224 | tf_op jit(solution)/shard_map/ppermute | solution.py:21
  5.6 3.8 %collective-permute-start.5 = (bf16[1,128,256]{2,1,0:T(8,128)(2,1)S(1)}, bf16[1,128,256]{2,1,0:T(8,128)(2,1)S(1)}, u32[]{:S(2)}, u32[]{:S(2)}) collective-permute-start(bf16[1,128,256]{2,1,0:T(8,128)(2,1)S(1)} %get-tuple-element.61), channel_id=1, source_target_pairs={{0,20},{4,16},{8,28},{12,24},{16,4},{20,0},{24,12},{28,8},{1,21},{... | collective-permute-start | bytes 196616 | tf_op jit(solution)/shard_map/ppermute | solution.py:21
  9.4 0.5 collective-permute-start.1
  10.0 1.3 %collective-permute-start.6 = (bf16[1,128,256]{2,1,0:T(8,128)(2,1)S(1)}, bf16[1,128,256]{2,1,0:T(8,128)(2,1)S(1)}, u32[]{:S(2)}, u32[]{:S(2)}) collective-permute-start(bf16[1,128,256]{2,1,0:T(8,128)(2,1)S(1)} %get-tuple-element.62), channel_id=1, source_target_pairs={{0,24},{4,28},{8,16},{12,20},{16,8},{20,12},{24,0},{28,4},{1,25},{... | collective-permute-start | bytes 196616 | tf_op jit(solution)/shard_map/ppermute | solution.py:21
  11.3 6.7 %collective-permute-done.4.refs_4_ = bf16[1,128,256]{2,1,0:T(8,128)(2,1)S(1)} collective-permute-done((bf16[1,128,256]{2,1,0:T(8,128)(2,1)S(1)}, bf16[1,128,256]{2,1,0:T(8,128)(2,1)S(1)}, u32[]{:S(2)}, u32[]{:S(2)}) %collective-permute-start.4) | collective-permute-done | bytes 65568 | tf_op jit(solution)/shard_map/ppermute | solution.py:21
  18.0 3.7 %collective-permute-start.7 = (bf16[1,128,256]{2,1,0:T(8,128)(2,1)S(1)}, bf16[1,128,256]{2,1,0:T(8,128)(2,1)S(1)}, u32[]{:S(2)}, u32[]{:S(2)}) collective-permute-start(bf16[1,128,256]{2,1,0:T(8,128)(2,1)S(1)} %get-tuple-element.63), channel_id=1, source_target_pairs={{0,28},{4,24},{8,20},{12,16},{16,12},{20,8},{24,4},{28,0},{1,29},{... | collective-permute-start | bytes 196616 | tf_op jit(solution)/shard_map/ppermute | solution.py:21
  21.7 2.0 %collective-permute-start.3 = (bf16[2,128,256]{2,1,0:T(8,128)(2,1)S(1)}, bf16[2,128,256]{2,1,0:T(8,128)(2,1)S(1)}, u32[]{:S(2)}, u32[]{:S(2)}) collective-permute-start(bf16[2,128,256]{2,1,0:T(8,128)(2,1)S(1)} %get-tuple-element.59), channel_id=1, source_target_pairs={{0,12},{4,8},{8,4},{12,0},{16,28},{20,24},{24,20},{28,16},{1,13},{... | collective-permute-start | bytes 393224 | tf_op jit(solution)/shard_map/ppermute | solution.py:21
  23.7 1.6 %collective-permute-start.8 = (bf16[1,128,256]{2,1,0:T(8,128)(2,1)S(1)}, bf16[1,128,256]{2,1,0:T(8,128)(2,1)S(1)}, u32[]{:S(2)}, u32[]{:S(2)}) collective-permute-start(bf16[1,128,256]{2,1,0:T(8,128)(2,1)S(1)} %get-tuple-element.65), channel_id=1, source_target_pairs={{0,4},{4,0},{8,12},{12,8},{16,20},{20,16},{24,28},{28,24},{1,5},{5... | collective-permute-start | bytes 196616 | tf_op jit(solution)/shard_map/ppermute | solution.py:21
  25.3 0.4 collective-permute-done.7.refs_7_
  25.7 3.3 %collective-permute-start.10 = (bf16[1,128,256]{2,1,0:T(8,128)(2,1)S(1)}, bf16[1,128,256]{2,1,0:T(8,128)(2,1)S(1)}, u32[]{:S(2)}, u32[]{:S(2)}) collective-permute-start(bf16[1,128,256]{2,1,0:T(8,128)(2,1)S(1)} %get-tuple-element.67), channel_id=1, source_target_pairs={{0,12},{4,8},{8,4},{12,0},{16,28},{20,24},{24,20},{28,16},{1,13},{... | collective-permute-start | bytes 196616 | tf_op jit(solution)/shard_map/ppermute | solution.py:21
  28.9 2.2 %shard_map.66 = (s32[16,64]{1,0:T(8,128)S(4)}, bf16[8,16,128,128]{3,2,1,0:T(8,128)(2,1)S(1)}) custom-call(s32[2,8]{1,0:T(2,128)S(4)} %get-tuple-element.49.mig, s32[16,64]{1,0:T(8,128)S(1)} %get-tuple-element.50.tiles_ref, bf16[8,16,128,128]{3,2,1,0:T(8,128)(2,1)} %adjacency_ref.1), custom_call_target="tpu_custom_call" | custom-call | bytes 4194304 | tf_op jit(solution)/shard_map/pallas_call | solution.py:272
  31.2 1.2 %collective-permute-done.9.refs_9_ = bf16[1,128,256]{2,1,0:T(8,128)(2,1)S(1)} collective-permute-done((bf16[1,128,256]{2,1,0:T(8,128)(2,1)S(1)}, bf16[1,128,256]{2,1,0:T(8,128)(2,1)S(1)}, u32[]{:S(2)}, u32[]{:S(2)}) %collective-permute-start.9) | collective-permute-done | bytes 65568 | tf_op jit(solution)/shard_map/ppermute | solution.py:21
  32.4 0.7 collective-permute-done.10.refs_10_
  33.1 0.7 shard_map.68
  33.8 0.6 shard_map.70
  34.5 1.3 %shard_map.69 = (bf16[2,128,256]{2,1,0:T(8,128)(2,1)S(1)}, bf16[2,128,256]{2,1,0:T(8,128)(2,1)S(1)}) custom-call(s32[16,64]{1,0:T(8,128)S(4)} %get-tuple-element.53.table_ref, s32[9]{0:T(128)S(4)} %get-tuple-element.55.deal_ref, bf16[8,16,128,128]{3,2,1,0:T(8,128)(2,1)S(1)} %get-tuple-element.54.adjacency_ref, ...), custom_call_target="tpu_custom_call" | custom-call | flops 536870912 | bytes 2097152 | tf_op jit(solution)/shard_map/pallas_call | solution.py:272
  35.9 1.6 %collective-permute-start.13 = (bf16[2,128,256]{2,1,0:T(8,128)(2,1)S(1)}, bf16[2,128,256]{2,1,0:T(8,128)(2,1)S(1)}, u32[]{:S(2)}, u32[]{:S(2)}) collective-permute-start(bf16[2,128,256]{2,1,0:T(8,128)(2,1)S(1)} %shard_map.70), channel_id=1, source_target_pairs={{0,3},{1,2},{2,1},{3,0},{4,7},{5,6},{6,5},{7,4},{8,11},{9,10},{10,... | collective-permute-start | bytes 393224 | tf_op jit(solution)/shard_map/ppermute | solution.py:21
  37.5 0.5 collective-permute-start.12
  38.0 3.3 %collective-permute-done.13.refs_3_ = bf16[2,128,256]{2,1,0:T(8,128)(2,1)S(1)} collective-permute-done((bf16[2,128,256]{2,1,0:T(8,128)(2,1)S(1)}, bf16[2,128,256]{2,1,0:T(8,128)(2,1)S(1)}, u32[]{:S(2)}, u32[]{:S(2)}) %collective-permute-start.13) | collective-permute-done | bytes 131104 | tf_op jit(solution)/shard_map/ppermute | solution.py:21
  41.4 3.2 %collective-permute-done.12.refs_2_ = bf16[2,128,256]{2,1,0:T(8,128)(2,1)S(1)} collective-permute-done((bf16[2,128,256]{2,1,0:T(8,128)(2,1)S(1)}, bf16[2,128,256]{2,1,0:T(8,128)(2,1)S(1)}, u32[]{:S(2)}, u32[]{:S(2)}) %collective-permute-start.12) | collective-permute-done | bytes 131104 | tf_op jit(solution)/shard_map/ppermute | solution.py:21
  44.6 0.8 shard_map.71
  45.4 1.5 %collective-permute-start.15 = (bf16[1,128,256]{2,1,0:T(8,128)(2,1)S(1)}, bf16[1,128,256]{2,1,0:T(8,128)(2,1)S(1)}, u32[]{:S(2)}, u32[]{:S(2)}) collective-permute-start(bf16[1,128,256]{2,1,0:T(8,128)(2,1)S(1)} %get-tuple-element.74), channel_id=1, source_target_pairs={{0,2},{1,3},{2,0},{3,1},{4,6},{5,7},{6,4},{7,5},{8,10},{9,11},{10,... | collective-permute-start | bytes 196616 | tf_op jit(solution)/shard_map/ppermute | solution.py:21
  47.3 0.8 shard_map.72
  48.1 0.4 collective-permute-start.17
  48.5 1.5 %collective-permute-start.18 = (bf16[1,128,256]{2,1,0:T(8,128)(2,1)S(1)}, bf16[1,128,256]{2,1,0:T(8,128)(2,1)S(1)}, u32[]{:S(2)}, u32[]{:S(2)}) collective-permute-start(bf16[1,128,256]{2,1,0:T(8,128)(2,1)S(1)} %get-tuple-element.78), channel_id=1, source_target_pairs={{0,2},{1,3},{2,0},{3,1},{4,6},{5,7},{6,4},{7,5},{8,10},{9,11},{10,... | collective-permute-start | bytes 196616 | tf_op jit(solution)/shard_map/ppermute | solution.py:21
  50.0 1.0 %collective-permute-done.16.refs_3_ = bf16[1,128,256]{2,1,0:T(8,128)(2,1)S(1)} collective-permute-done((bf16[1,128,256]{2,1,0:T(8,128)(2,1)S(1)}, bf16[1,128,256]{2,1,0:T(8,128)(2,1)S(1)}, u32[]{:S(2)}, u32[]{:S(2)}) %collective-permute-start.16) | collective-permute-done | bytes 65568 | tf_op jit(solution)/shard_map/ppermute | solution.py:21
  51.0 1.2 %collective-permute-start.20 = (bf16[2,128,256]{2,1,0:T(8,128)(2,1)S(1)}, bf16[2,128,256]{2,1,0:T(8,128)(2,1)S(1)}, u32[]{:S(2)}, u32[]{:S(2)}) collective-permute-start(bf16[2,128,256]{2,1,0:T(8,128)(2,1)S(1)} %shard_map.74), channel_id=1, source_target_pairs={{0,16},{4,20},{8,24},{12,28},{16,0},{20,4},{24,8},{28,12},{1,17},{... | collective-permute-start | bytes 393224 | tf_op jit(solution)/shard_map/ppermute | solution.py:21
  52.2 0.5 collective-permute-done.18.refs_6_
  52.8 1.5 %collective-permute-done.19.refs_7_ = bf16[1,128,256]{2,1,0:T(8,128)(2,1)S(1)} collective-permute-done((bf16[1,128,256]{2,1,0:T(8,128)(2,1)S(1)}, bf16[1,128,256]{2,1,0:T(8,128)(2,1)S(1)}, u32[]{:S(2)}, u32[]{:S(2)}) %collective-permute-start.19) | collective-permute-done | bytes 65568 | tf_op jit(solution)/shard_map/ppermute | solution.py:21
  54.4 1.2 %collective-permute-start.24 = (bf16[1,128,256]{2,1,0:T(8,128)(2,1)S(1)}, bf16[1,128,256]{2,1,0:T(8,128)(2,1)S(1)}, u32[]{:S(2)}, u32[]{:S(2)}) collective-permute-start(bf16[1,128,256]{2,1,0:T(8,128)(2,1)S(1)} %get-tuple-element.84), channel_id=1, source_target_pairs={{0,16},{4,20},{8,24},{12,28},{16,0},{20,4},{24,8},{28,12},{1,17},{... | collective-permute-start | bytes 196616 | tf_op jit(solution)/shard_map/ppermute | solution.py:21
  55.6 2.7 %collective-permute-start.25 = (bf16[1,128,256]{2,1,0:T(8,128)(2,1)S(1)}, bf16[1,128,256]{2,1,0:T(8,128)(2,1)S(1)}, u32[]{:S(2)}, u32[]{:S(2)}) collective-permute-start(bf16[1,128,256]{2,1,0:T(8,128)(2,1)S(1)} %get-tuple-element.85), channel_id=1, source_target_pairs={{0,20},{4,16},{8,28},{12,24},{16,4},{20,0},{24,12},{28,8},{1,21},{... | collective-permute-start | bytes 196616 | tf_op jit(solution)/shard_map/ppermute | solution.py:21
  58.3 0.5 collective-permute-start.21
  58.8 2.4 %collective-permute-start.26 = (bf16[1,128,256]{2,1,0:T(8,128)(2,1)S(1)}, bf16[1,128,256]{2,1,0:T(8,128)(2,1)S(1)}, u32[]{:S(2)}, u32[]{:S(2)}) collective-permute-start(bf16[1,128,256]{2,1,0:T(8,128)(2,1)S(1)} %get-tuple-element.86), channel_id=1, source_target_pairs={{0,24},{4,28},{8,16},{12,20},{16,8},{20,12},{24,0},{28,4},{1,25},{... | collective-permute-start | bytes 196616 | tf_op jit(solution)/shard_map/ppermute | solution.py:21
  61.2 5.5 %collective-permute-done.24.refs_4_ = bf16[1,128,256]{2,1,0:T(8,128)(2,1)S(1)} collective-permute-done((bf16[1,128,256]{2,1,0:T(8,128)(2,1)S(1)}, bf16[1,128,256]{2,1,0:T(8,128)(2,1)S(1)}, u32[]{:S(2)}, u32[]{:S(2)}) %collective-permute-start.24) | collective-permute-done | bytes 65568 | tf_op jit(solution)/shard_map/ppermute | solution.py:21
  66.7 2.5 %collective-permute-start.27 = (bf16[1,128,256]{2,1,0:T(8,128)(2,1)S(1)}, bf16[1,128,256]{2,1,0:T(8,128)(2,1)S(1)}, u32[]{:S(2)}, u32[]{:S(2)}) collective-permute-start(bf16[1,128,256]{2,1,0:T(8,128)(2,1)S(1)} %get-tuple-element.87), channel_id=1, source_target_pairs={{0,28},{4,24},{8,20},{12,16},{16,12},{20,8},{24,4},{28,0},{1,29},{... | collective-permute-start | bytes 196616 | tf_op jit(solution)/shard_map/ppermute | solution.py:21
  69.2 2.0 %collective-permute-start.23 = (bf16[2,128,256]{2,1,0:T(8,128)(2,1)S(1)}, bf16[2,128,256]{2,1,0:T(8,128)(2,1)S(1)}, u32[]{:S(2)}, u32[]{:S(2)}) collective-permute-start(bf16[2,128,256]{2,1,0:T(8,128)(2,1)S(1)} %get-tuple-element.83), channel_id=1, source_target_pairs={{0,12},{4,8},{8,4},{12,0},{16,28},{20,24},{24,20},{28,16},{1,13},{... | collective-permute-start | bytes 393224 | tf_op jit(solution)/shard_map/ppermute | solution.py:21
  71.2 1.6 %collective-permute-start.28 = (bf16[1,128,256]{2,1,0:T(8,128)(2,1)S(1)}, bf16[1,128,256]{2,1,0:T(8,128)(2,1)S(1)}, u32[]{:S(2)}, u32[]{:S(2)}) collective-permute-start(bf16[1,128,256]{2,1,0:T(8,128)(2,1)S(1)} %get-tuple-element.88), channel_id=1, source_target_pairs={{0,4},{4,0},{8,12},{12,8},{16,20},{20,16},{24,28},{28,24},{1,5},{5... | collective-permute-start | bytes 196616 | tf_op jit(solution)/shard_map/ppermute | solution.py:21
  72.8 1.1 %collective-permute-done.27.refs_7_ = bf16[1,128,256]{2,1,0:T(8,128)(2,1)S(1)} collective-permute-done((bf16[1,128,256]{2,1,0:T(8,128)(2,1)S(1)}, bf16[1,128,256]{2,1,0:T(8,128)(2,1)S(1)}, u32[]{:S(2)}, u32[]{:S(2)}) %collective-permute-start.27) | collective-permute-done | bytes 65568 | tf_op jit(solution)/shard_map/ppermute | solution.py:21
  73.9 3.5 %collective-permute-start.30 = (bf16[1,128,256]{2,1,0:T(8,128)(2,1)S(1)}, bf16[1,128,256]{2,1,0:T(8,128)(2,1)S(1)}, u32[]{:S(2)}, u32[]{:S(2)}) collective-permute-start(bf16[1,128,256]{2,1,0:T(8,128)(2,1)S(1)} %get-tuple-element.90), channel_id=1, source_target_pairs={{0,12},{4,8},{8,4},{12,0},{16,28},{20,24},{24,20},{28,16},{1,13},{... | collective-permute-start | bytes 196616 | tf_op jit(solution)/shard_map/ppermute | solution.py:21
  77.4 1.7 %collective-permute-done.23.refs_3_ = bf16[2,128,256]{2,1,0:T(8,128)(2,1)S(1)} collective-permute-done((bf16[2,128,256]{2,1,0:T(8,128)(2,1)S(1)}, bf16[2,128,256]{2,1,0:T(8,128)(2,1)S(1)}, u32[]{:S(2)}, u32[]{:S(2)}) %collective-permute-start.23) | collective-permute-done | bytes 131104 | tf_op jit(solution)/shard_map/ppermute | solution.py:21
  79.0 1.2 %collective-permute-done.29.refs_9_ = bf16[1,128,256]{2,1,0:T(8,128)(2,1)S(1)} collective-permute-done((bf16[1,128,256]{2,1,0:T(8,128)(2,1)S(1)}, bf16[1,128,256]{2,1,0:T(8,128)(2,1)S(1)}, u32[]{:S(2)}, u32[]{:S(2)}) %collective-permute-start.29) | collective-permute-done | bytes 65568 | tf_op jit(solution)/shard_map/ppermute | solution.py:21
  80.2 0.7 collective-permute-done.30.refs_10_
  80.9 0.7 shard_map.76
  81.7 1.5 %collective-permute-start.31 = (bf16[2,128,256]{2,1,0:T(8,128)(2,1)S(1)}, bf16[2,128,256]{2,1,0:T(8,128)(2,1)S(1)}, u32[]{:S(2)}, u32[]{:S(2)}) collective-permute-start(bf16[2,128,256]{2,1,0:T(8,128)(2,1)S(1)} %get-tuple-element.91), channel_id=1, source_target_pairs={{0,4},{4,8},{8,12},{12,16},{16,20},{20,24},{24,28},{28,0},{1,5},{5... | collective-permute-start | bytes 393224 | tf_op jit(solution)/shard_map/ppermute | solution.py:399
  83.2 2.8 %shard_map.77.out_in_ref = bf16[8,128,256]{2,1,0:T(8,128)(2,1)} custom-call(s32[16,64]{1,0:T(8,128)S(4)} %get-tuple-element.53.table_ref, s32[16]{0:T(128)S(4)} %get-tuple-element.52.slots_ref, bf16[8,16,128,128]{3,2,1,0:T(8,128)(2,1)S(1)} %get-tuple-element.54.adjacency_ref, bf16[24,128,256]{2,1,0:T(8,128)(2,1)S(1)} %get-tuple-element.92.pool_ref), custom_call_target="tpu_custom_call" | custom-call | flops 805306368 | bytes 3145728 | tf_op jit(solution)/shard_map/pallas_call | solution.py:272
  86.0 3.4 %collective-permute-done.31.moved_ref = bf16[2,128,256]{2,1,0:T(8,128)(2,1)S(1)} collective-permute-done((bf16[2,128,256]{2,1,0:T(8,128)(2,1)S(1)}, bf16[2,128,256]{2,1,0:T(8,128)(2,1)S(1)}, u32[]{:S(2)}, u32[]{:S(2)}) %collective-permute-start.31) | collective-permute-done | bytes 131104 | tf_op jit(solution)/shard_map/ppermute | solution.py:399
  89.4 0.7 shard_map.78
  (35 shorter events, 1.1 us)
Async XLA Ops:
  1.1 20.6 %collective-permute-start = (bf16[2,128,256]{2,1,0:T(8,128)(2,1)S(1)}, bf16[2,128,256]{2,1,0:T(8,128)(2,1)S(1)}, u32[]{:S(2)}, u32[]{:S(2)}) collective-permute-start(bf16[2,128,256]{2,1,0:T(8,128)(2,1)S(1)} %get-tuple-element.56), channel_id=1, source_target_pairs={{0,16},{4,20},{8,24},{12,28},{16,0},{20,4},{24,8},{28,12},{1,17},{... | collective-permute-start | bytes 393224 | tf_op jit(solution)/shard_map/ppermute | solution.py:21
  5.5 12.5 %collective-permute-start.4 = (bf16[1,128,256]{2,1,0:T(8,128)(2,1)S(1)}, bf16[1,128,256]{2,1,0:T(8,128)(2,1)S(1)}, u32[]{:S(2)}, u32[]{:S(2)}) collective-permute-start(bf16[1,128,256]{2,1,0:T(8,128)(2,1)S(1)} %get-tuple-element.60), channel_id=1, source_target_pairs={{0,16},{4,20},{8,24},{12,28},{16,0},{20,4},{24,8},{28,12},{1,17},{... | collective-permute-start | bytes 196616 | tf_op jit(solution)/shard_map/ppermute | solution.py:21
  5.6 16.1 %collective-permute-start.5 = (bf16[1,128,256]{2,1,0:T(8,128)(2,1)S(1)}, bf16[1,128,256]{2,1,0:T(8,128)(2,1)S(1)}, u32[]{:S(2)}, u32[]{:S(2)}) collective-permute-start(bf16[1,128,256]{2,1,0:T(8,128)(2,1)S(1)} %get-tuple-element.61), channel_id=1, source_target_pairs={{0,20},{4,16},{8,28},{12,24},{16,4},{20,0},{24,12},{28,8},{1,21},{... | collective-permute-start | bytes 196616 | tf_op jit(solution)/shard_map/ppermute | solution.py:21
  9.4 16.2 %collective-permute-start.1 = (bf16[2,128,256]{2,1,0:T(8,128)(2,1)S(1)}, bf16[2,128,256]{2,1,0:T(8,128)(2,1)S(1)}, u32[]{:S(2)}, u32[]{:S(2)}) collective-permute-start(bf16[2,128,256]{2,1,0:T(8,128)(2,1)S(1)} %get-tuple-element.57), channel_id=1, source_target_pairs={{0,4},{4,0},{8,12},{12,8},{16,20},{20,16},{24,28},{28,24},{1,5},{5... | collective-permute-start | bytes 393224 | tf_op jit(solution)/shard_map/ppermute | solution.py:21
  10.0 13.8 %collective-permute-start.6 = (bf16[1,128,256]{2,1,0:T(8,128)(2,1)S(1)}, bf16[1,128,256]{2,1,0:T(8,128)(2,1)S(1)}, u32[]{:S(2)}, u32[]{:S(2)}) collective-permute-start(bf16[1,128,256]{2,1,0:T(8,128)(2,1)S(1)} %get-tuple-element.62), channel_id=1, source_target_pairs={{0,24},{4,28},{8,16},{12,20},{16,8},{20,12},{24,0},{28,4},{1,25},{... | collective-permute-start | bytes 196616 | tf_op jit(solution)/shard_map/ppermute | solution.py:21
  18.0 7.7 %collective-permute-start.7 = (bf16[1,128,256]{2,1,0:T(8,128)(2,1)S(1)}, bf16[1,128,256]{2,1,0:T(8,128)(2,1)S(1)}, u32[]{:S(2)}, u32[]{:S(2)}) collective-permute-start(bf16[1,128,256]{2,1,0:T(8,128)(2,1)S(1)} %get-tuple-element.63), channel_id=1, source_target_pairs={{0,28},{4,24},{8,20},{12,16},{16,12},{20,8},{24,4},{28,0},{1,29},{... | collective-permute-start | bytes 196616 | tf_op jit(solution)/shard_map/ppermute | solution.py:21
  21.7 9.4 %collective-permute-start.2 = (bf16[2,128,256]{2,1,0:T(8,128)(2,1)S(1)}, bf16[2,128,256]{2,1,0:T(8,128)(2,1)S(1)}, u32[]{:S(2)}, u32[]{:S(2)}) collective-permute-start(bf16[2,128,256]{2,1,0:T(8,128)(2,1)S(1)} %get-tuple-element.58), channel_id=1, source_target_pairs={{0,8},{4,12},{8,0},{12,4},{16,24},{20,28},{24,16},{28,20},{1,9},{5... | collective-permute-start | bytes 393224 | tf_op jit(solution)/shard_map/ppermute | solution.py:21
  21.7 9.4 %collective-permute-start.3 = (bf16[2,128,256]{2,1,0:T(8,128)(2,1)S(1)}, bf16[2,128,256]{2,1,0:T(8,128)(2,1)S(1)}, u32[]{:S(2)}, u32[]{:S(2)}) collective-permute-start(bf16[2,128,256]{2,1,0:T(8,128)(2,1)S(1)} %get-tuple-element.59), channel_id=1, source_target_pairs={{0,12},{4,8},{8,4},{12,0},{16,28},{20,24},{24,20},{28,16},{1,13},{... | collective-permute-start | bytes 393224 | tf_op jit(solution)/shard_map/ppermute | solution.py:21
  23.7 7.4 %collective-permute-start.8 = (bf16[1,128,256]{2,1,0:T(8,128)(2,1)S(1)}, bf16[1,128,256]{2,1,0:T(8,128)(2,1)S(1)}, u32[]{:S(2)}, u32[]{:S(2)}) collective-permute-start(bf16[1,128,256]{2,1,0:T(8,128)(2,1)S(1)} %get-tuple-element.65), channel_id=1, source_target_pairs={{0,4},{4,0},{8,12},{12,8},{16,20},{20,16},{24,28},{28,24},{1,5},{5... | collective-permute-start | bytes 196616 | tf_op jit(solution)/shard_map/ppermute | solution.py:21
  25.7 6.7 %collective-permute-start.9 = (bf16[1,128,256]{2,1,0:T(8,128)(2,1)S(1)}, bf16[1,128,256]{2,1,0:T(8,128)(2,1)S(1)}, u32[]{:S(2)}, u32[]{:S(2)}) collective-permute-start(bf16[1,128,256]{2,1,0:T(8,128)(2,1)S(1)} %get-tuple-element.66), channel_id=1, source_target_pairs={{0,8},{4,12},{8,0},{12,4},{16,24},{20,28},{24,16},{28,20},{1,9},{5... | collective-permute-start | bytes 196616 | tf_op jit(solution)/shard_map/ppermute | solution.py:21
  25.7 7.4 %collective-permute-start.10 = (bf16[1,128,256]{2,1,0:T(8,128)(2,1)S(1)}, bf16[1,128,256]{2,1,0:T(8,128)(2,1)S(1)}, u32[]{:S(2)}, u32[]{:S(2)}) collective-permute-start(bf16[1,128,256]{2,1,0:T(8,128)(2,1)S(1)} %get-tuple-element.67), channel_id=1, source_target_pairs={{0,12},{4,8},{8,4},{12,0},{16,28},{20,24},{24,20},{28,16},{1,13},{... | collective-permute-start | bytes 196616 | tf_op jit(solution)/shard_map/ppermute | solution.py:21
  34.5 10.1 %copy-start = (bf16[1024,1024]{1,0:T(8,128)(2,1)S(1)}, bf16[1024,1024]{1,0:T(8,128)(2,1)}, u32[]{:S(2)}) copy-start(bf16[1024,1024]{1,0:T(8,128)(2,1)} %weight_one_ref.3) | copy-start | bytes 6291460
  34.5 10.1 %copy-start.1 = (bf16[1024,1024]{1,0:T(8,128)(2,1)S(1)}, bf16[1024,1024]{1,0:T(8,128)(2,1)}, u32[]{:S(2)}) copy-start(bf16[1024,1024]{1,0:T(8,128)(2,1)} %weight_two_ref.3) | copy-start | bytes 6291460
  35.8 2.2 %collective-permute-start.11 = (bf16[2,128,256]{2,1,0:T(8,128)(2,1)S(1)}, bf16[2,128,256]{2,1,0:T(8,128)(2,1)S(1)}, u32[]{:S(2)}, u32[]{:S(2)}) collective-permute-start(bf16[2,128,256]{2,1,0:T(8,128)(2,1)S(1)} %get-tuple-element.70), channel_id=1, source_target_pairs={{0,1},{1,0},{2,3},{3,2},{4,5},{5,4},{6,7},{7,6},{8,9},{9,8},{10,11... | collective-permute-start | bytes 393224 | tf_op jit(solution)/shard_map/ppermute | solution.py:21
  35.9 5.5 %collective-permute-start.13 = (bf16[2,128,256]{2,1,0:T(8,128)(2,1)S(1)}, bf16[2,128,256]{2,1,0:T(8,128)(2,1)S(1)}, u32[]{:S(2)}, u32[]{:S(2)}) collective-permute-start(bf16[2,128,256]{2,1,0:T(8,128)(2,1)S(1)} %shard_map.70), channel_id=1, source_target_pairs={{0,3},{1,2},{2,1},{3,0},{4,7},{5,6},{6,5},{7,4},{8,11},{9,10},{10,... | collective-permute-start | bytes 393224 | tf_op jit(solution)/shard_map/ppermute | solution.py:21
  37.5 7.1 %collective-permute-start.12 = (bf16[2,128,256]{2,1,0:T(8,128)(2,1)S(1)}, bf16[2,128,256]{2,1,0:T(8,128)(2,1)S(1)}, u32[]{:S(2)}, u32[]{:S(2)}) collective-permute-start(bf16[2,128,256]{2,1,0:T(8,128)(2,1)S(1)} %get-tuple-element.71), channel_id=1, source_target_pairs={{0,2},{1,3},{2,0},{3,1},{4,6},{5,7},{6,4},{7,5},{8,10},{9,11},{10,... | collective-permute-start | bytes 393224 | tf_op jit(solution)/shard_map/ppermute | solution.py:21
  45.3 4.6 %collective-permute-start.14 = (bf16[1,128,256]{2,1,0:T(8,128)(2,1)S(1)}, bf16[1,128,256]{2,1,0:T(8,128)(2,1)S(1)}, u32[]{:S(2)}, u32[]{:S(2)}) collective-permute-start(bf16[1,128,256]{2,1,0:T(8,128)(2,1)S(1)} %get-tuple-element.73), channel_id=1, source_target_pairs={{0,1},{1,0},{2,3},{3,2},{4,5},{5,4},{6,7},{7,6},{8,9},{9,8},{10,11... | collective-permute-start | bytes 196616 | tf_op jit(solution)/shard_map/ppermute | solution.py:21
  45.4 4.6 %collective-permute-start.15 = (bf16[1,128,256]{2,1,0:T(8,128)(2,1)S(1)}, bf16[1,128,256]{2,1,0:T(8,128)(2,1)S(1)}, u32[]{:S(2)}, u32[]{:S(2)}) collective-permute-start(bf16[1,128,256]{2,1,0:T(8,128)(2,1)S(1)} %get-tuple-element.74), channel_id=1, source_target_pairs={{0,2},{1,3},{2,0},{3,1},{4,6},{5,7},{6,4},{7,5},{8,10},{9,11},{10,... | collective-permute-start | bytes 196616 | tf_op jit(solution)/shard_map/ppermute | solution.py:21
  47.0 4.1 %collective-permute-start.16 = (bf16[1,128,256]{2,1,0:T(8,128)(2,1)S(1)}, bf16[1,128,256]{2,1,0:T(8,128)(2,1)S(1)}, u32[]{:S(2)}, u32[]{:S(2)}) collective-permute-start(bf16[1,128,256]{2,1,0:T(8,128)(2,1)S(1)} %get-tuple-element.75), channel_id=1, source_target_pairs={{0,3},{1,2},{2,1},{3,0},{4,7},{5,6},{6,5},{7,4},{8,11},{9,10},{10,... | collective-permute-start | bytes 196616 | tf_op jit(solution)/shard_map/ppermute | solution.py:21
  48.1 4.2 %collective-permute-start.17 = (bf16[1,128,256]{2,1,0:T(8,128)(2,1)S(1)}, bf16[1,128,256]{2,1,0:T(8,128)(2,1)S(1)}, u32[]{:S(2)}, u32[]{:S(2)}) collective-permute-start(bf16[1,128,256]{2,1,0:T(8,128)(2,1)S(1)} %get-tuple-element.77), channel_id=1, source_target_pairs={{0,1},{1,0},{2,3},{3,2},{4,5},{5,4},{6,7},{7,6},{8,9},{9,8},{10,11... | collective-permute-start | bytes 196616 | tf_op jit(solution)/shard_map/ppermute | solution.py:21
  48.5 4.3 %collective-permute-start.18 = (bf16[1,128,256]{2,1,0:T(8,128)(2,1)S(1)}, bf16[1,128,256]{2,1,0:T(8,128)(2,1)S(1)}, u32[]{:S(2)}, u32[]{:S(2)}) collective-permute-start(bf16[1,128,256]{2,1,0:T(8,128)(2,1)S(1)} %get-tuple-element.78), channel_id=1, source_target_pairs={{0,2},{1,3},{2,0},{3,1},{4,6},{5,7},{6,4},{7,5},{8,10},{9,11},{10,... | collective-permute-start | bytes 196616 | tf_op jit(solution)/shard_map/ppermute | solution.py:21
  49.9 4.3 %collective-permute-start.19 = (bf16[1,128,256]{2,1,0:T(8,128)(2,1)S(1)}, bf16[1,128,256]{2,1,0:T(8,128)(2,1)S(1)}, u32[]{:S(2)}, u32[]{:S(2)}) collective-permute-start(bf16[1,128,256]{2,1,0:T(8,128)(2,1)S(1)} %get-tuple-element.79), channel_id=1, source_target_pairs={{0,3},{1,2},{2,1},{3,0},{4,7},{5,6},{6,5},{7,4},{8,11},{9,10},{10,... | collective-permute-start | bytes 196616 | tf_op jit(solution)/shard_map/ppermute | solution.py:21
  51.0 18.2 %collective-permute-start.20 = (bf16[2,128,256]{2,1,0:T(8,128)(2,1)S(1)}, bf16[2,128,256]{2,1,0:T(8,128)(2,1)S(1)}, u32[]{:S(2)}, u32[]{:S(2)}) collective-permute-start(bf16[2,128,256]{2,1,0:T(8,128)(2,1)S(1)} %shard_map.74), channel_id=1, source_target_pairs={{0,16},{4,20},{8,24},{12,28},{16,0},{20,4},{24,8},{28,12},{1,17},{... | collective-permute-start | bytes 393224 | tf_op jit(solution)/shard_map/ppermute | solution.py:21
  54.4 12.3 %collective-permute-start.24 = (bf16[1,128,256]{2,1,0:T(8,128)(2,1)S(1)}, bf16[1,128,256]{2,1,0:T(8,128)(2,1)S(1)}, u32[]{:S(2)}, u32[]{:S(2)}) collective-permute-start(bf16[1,128,256]{2,1,0:T(8,128)(2,1)S(1)} %get-tuple-element.84), channel_id=1, source_target_pairs={{0,16},{4,20},{8,24},{12,28},{16,0},{20,4},{24,8},{28,12},{1,17},{... | collective-permute-start | bytes 196616 | tf_op jit(solution)/shard_map/ppermute | solution.py:21
  55.6 13.6 %collective-permute-start.25 = (bf16[1,128,256]{2,1,0:T(8,128)(2,1)S(1)}, bf16[1,128,256]{2,1,0:T(8,128)(2,1)S(1)}, u32[]{:S(2)}, u32[]{:S(2)}) collective-permute-start(bf16[1,128,256]{2,1,0:T(8,128)(2,1)S(1)} %get-tuple-element.85), channel_id=1, source_target_pairs={{0,20},{4,16},{8,28},{12,24},{16,4},{20,0},{24,12},{28,8},{1,21},{... | collective-permute-start | bytes 196616 | tf_op jit(solution)/shard_map/ppermute | solution.py:21
  58.3 15.6 %collective-permute-start.21 = (bf16[2,128,256]{2,1,0:T(8,128)(2,1)S(1)}, bf16[2,128,256]{2,1,0:T(8,128)(2,1)S(1)}, u32[]{:S(2)}, u32[]{:S(2)}) collective-permute-start(bf16[2,128,256]{2,1,0:T(8,128)(2,1)S(1)} %get-tuple-element.81), channel_id=1, source_target_pairs={{0,4},{4,0},{8,12},{12,8},{16,20},{20,16},{24,28},{28,24},{1,5},{5... | collective-permute-start | bytes 393224 | tf_op jit(solution)/shard_map/ppermute | solution.py:21
  58.8 12.4 %collective-permute-start.26 = (bf16[1,128,256]{2,1,0:T(8,128)(2,1)S(1)}, bf16[1,128,256]{2,1,0:T(8,128)(2,1)S(1)}, u32[]{:S(2)}, u32[]{:S(2)}) collective-permute-start(bf16[1,128,256]{2,1,0:T(8,128)(2,1)S(1)} %get-tuple-element.86), channel_id=1, source_target_pairs={{0,24},{4,28},{8,16},{12,20},{16,8},{20,12},{24,0},{28,4},{1,25},{... | collective-permute-start | bytes 196616 | tf_op jit(solution)/shard_map/ppermute | solution.py:21
  66.7 7.2 %collective-permute-start.27 = (bf16[1,128,256]{2,1,0:T(8,128)(2,1)S(1)}, bf16[1,128,256]{2,1,0:T(8,128)(2,1)S(1)}, u32[]{:S(2)}, u32[]{:S(2)}) collective-permute-start(bf16[1,128,256]{2,1,0:T(8,128)(2,1)S(1)} %get-tuple-element.87), channel_id=1, source_target_pairs={{0,28},{4,24},{8,20},{12,16},{16,12},{20,8},{24,4},{28,0},{1,29},{... | collective-permute-start | bytes 196616 | tf_op jit(solution)/shard_map/ppermute | solution.py:21
  69.2 8.2 %collective-permute-start.22 = (bf16[2,128,256]{2,1,0:T(8,128)(2,1)S(1)}, bf16[2,128,256]{2,1,0:T(8,128)(2,1)S(1)}, u32[]{:S(2)}, u32[]{:S(2)}) collective-permute-start(bf16[2,128,256]{2,1,0:T(8,128)(2,1)S(1)} %get-tuple-element.82), channel_id=1, source_target_pairs={{0,8},{4,12},{8,0},{12,4},{16,24},{20,28},{24,16},{28,20},{1,9},{5... | collective-permute-start | bytes 393224 | tf_op jit(solution)/shard_map/ppermute | solution.py:21
  69.2 9.8 %collective-permute-start.23 = (bf16[2,128,256]{2,1,0:T(8,128)(2,1)S(1)}, bf16[2,128,256]{2,1,0:T(8,128)(2,1)S(1)}, u32[]{:S(2)}, u32[]{:S(2)}) collective-permute-start(bf16[2,128,256]{2,1,0:T(8,128)(2,1)S(1)} %get-tuple-element.83), channel_id=1, source_target_pairs={{0,12},{4,8},{8,4},{12,0},{16,28},{20,24},{24,20},{28,16},{1,13},{... | collective-permute-start | bytes 393224 | tf_op jit(solution)/shard_map/ppermute | solution.py:21
  71.2 7.8 %collective-permute-start.28 = (bf16[1,128,256]{2,1,0:T(8,128)(2,1)S(1)}, bf16[1,128,256]{2,1,0:T(8,128)(2,1)S(1)}, u32[]{:S(2)}, u32[]{:S(2)}) collective-permute-start(bf16[1,128,256]{2,1,0:T(8,128)(2,1)S(1)} %get-tuple-element.88), channel_id=1, source_target_pairs={{0,4},{4,0},{8,12},{12,8},{16,20},{20,16},{24,28},{28,24},{1,5},{5... | collective-permute-start | bytes 196616 | tf_op jit(solution)/shard_map/ppermute | solution.py:21
  73.9 6.3 %collective-permute-start.29 = (bf16[1,128,256]{2,1,0:T(8,128)(2,1)S(1)}, bf16[1,128,256]{2,1,0:T(8,128)(2,1)S(1)}, u32[]{:S(2)}, u32[]{:S(2)}) collective-permute-start(bf16[1,128,256]{2,1,0:T(8,128)(2,1)S(1)} %get-tuple-element.89), channel_id=1, source_target_pairs={{0,8},{4,12},{8,0},{12,4},{16,24},{20,28},{24,16},{28,20},{1,9},{5... | collective-permute-start | bytes 196616 | tf_op jit(solution)/shard_map/ppermute | solution.py:21
  73.9 7.0 %collective-permute-start.30 = (bf16[1,128,256]{2,1,0:T(8,128)(2,1)S(1)}, bf16[1,128,256]{2,1,0:T(8,128)(2,1)S(1)}, u32[]{:S(2)}, u32[]{:S(2)}) collective-permute-start(bf16[1,128,256]{2,1,0:T(8,128)(2,1)S(1)} %get-tuple-element.90), channel_id=1, source_target_pairs={{0,12},{4,8},{8,4},{12,0},{16,28},{20,24},{24,20},{28,16},{1,13},{... | collective-permute-start | bytes 196616 | tf_op jit(solution)/shard_map/ppermute | solution.py:21
  81.7 7.7 %collective-permute-start.31 = (bf16[2,128,256]{2,1,0:T(8,128)(2,1)S(1)}, bf16[2,128,256]{2,1,0:T(8,128)(2,1)S(1)}, u32[]{:S(2)}, u32[]{:S(2)}) collective-permute-start(bf16[2,128,256]{2,1,0:T(8,128)(2,1)S(1)} %get-tuple-element.91), channel_id=1, source_target_pairs={{0,4},{4,8},{8,12},{12,16},{16,20},{20,24},{24,28},{28,0},{1,5},{5... | collective-permute-start | bytes 393224 | tf_op jit(solution)/shard_map/ppermute | solution.py:399

commit v3 on v2

--- a/solution.py
+++ b/solution.py
@@ -128,23 +128,24 @@
         outs[k - 1][0] = pair_ref[which_ref[k]]
 
 
-def fill_pool(domains, own_ref, arrived, pool_ref):
+def fill_early_kernel(domains, own_ref, *refs):
+    *arrived, pool_ref = refs
     half = domains // 2
     rows = own_ref.shape[0]
     pool_ref[0:rows] = own_ref[...]
-    pair, near, far, relay = split_arrived(half, arrived)
-    pool_ref[rows : rows + 2] = pair[...]
+    pool_ref[rows : rows + 2] = arrived[0][...]
     for k in range(1, half):
-        pool_ref[rows + 2 * k : rows + 2 * k + 2] = near[k - 1][...]
-        pool_ref[rows + 2 * (half + k)] = relay[k - 1][0]
-    for k in range(half, domains):
-        pool_ref[rows + 2 * k + 1] = far[k - half][0]
-
-
-def split_arrived(half, arrived):
-    cuts = (1, half, 2 * half)
-    pair, near, far, relay = (arrived[i:j] for i, j in zip((0,) + cuts, cuts + (None,)))
-    return pair[0], near, far, relay
+        pool_ref[rows + 2 * k : rows + 2 * k + 2] = arrived[k][...]
+    pool_ref[rows + 2 * half + 1] = arrived[half][0]
+    for k in range(half + 2, domains):
+        pool_ref[rows + 2 * k + 1] = arrived[k - 1][0]
+
+
+def fill_late(domains, rows, late, pool_ref):
+    half = domains // 2
+    pool_ref[rows + 2 * (half + 1) + 1] = late[0][0]
+    for k in range(1, half):
+        pool_ref[rows + 2 * (half + k)] = late[k][0]
 
 
 def sum_row(r, table_ref, adjacency_ref, pool_ref):
@@ -161,9 +162,9 @@
     return total.astype(BF16)
 
 
-def first_sum_kernel(domains, feats, j, table_ref, deal_ref, adjacency_ref, own_ref, *refs):
-    *arrived, pool_ref, out_ref = refs
-    fill_pool(domains, own_ref, arrived, pool_ref)
+def first_sum_kernel(domains, feats, j, table_ref, deal_ref, adjacency_ref, *refs):
+    _, *late, pool_ref, out_ref = refs
+    fill_late(domains, adjacency_ref.shape[0], late, pool_ref)
     part_sum_kernel(feats, [j], table_ref, deal_ref, adjacency_ref, pool_ref, out_ref)
 
 
@@ -176,9 +177,9 @@
             out_ref[i] = sum_row(deal_ref[i * feats + rank], table_ref, adjacency_ref, pool_ref)
 
 
-def leaving_sum_kernel(domains, table_ref, slots_ref, adjacency_ref, own_ref, *refs):
-    *arrived, pool_ref, out_ref = refs
-    fill_pool(domains, own_ref, arrived, pool_ref)
+def leaving_sum_kernel(domains, table_ref, slots_ref, adjacency_ref, *refs):
+    _, *late, pool_ref, out_ref = refs
+    fill_late(domains, adjacency_ref.shape[0], late, pool_ref)
 
     @pl.loop(0, out_ref.shape[0])
     def _(i):
@@ -193,22 +194,36 @@
             out_ref[r] = sum_row(r, table_ref, adjacency_ref, pool_ref)
 
 
-def dense_kernel(feats, chunk, weight_one_ref, weight_two_ref, *refs):
-    parts, outs, hidden_ref = refs[:feats], refs[feats : 2 * feats], refs[2 * feats]
+def first_products(js, parts, chunk, weight_ref, c):
     feat = lax.axis_index("feat")
     width = parts[0].shape[2]
-    columns = weight_one_ref.shape[1]
-    rows = [part[chunk] for part in parts]
-    for c in range(0, columns, width):
-        total = None
-        for j in range(feats):
-            start = pl.multiple_of((feat ^ j) * width, width)
-            part = jnp.dot(
-                rows[j],
-                weight_one_ref[pl.ds(start, width), c : c + width],
-                preferred_element_type=F32,
+    total = None
+    for j, part in zip(js, parts, strict=True):
+        start = pl.multiple_of((feat ^ j) * width, width)
+        weight = weight_ref[pl.ds(start, width), c : c + width]
+        product = jnp.dot(part[chunk], weight, preferred_element_type=F32)
+        total = product if total is None else total + product
+    return total
+
+
+def dense_early_kernel(weight_one_ref, *refs):
+    *parts, total_ref = refs
+    width = parts[0].shape[2]
+    for chunk in range(total_ref.shape[0]):
+        for c in range(0, weight_one_ref.shape[1], width):
+            total_ref[chunk, :, c : c + width] = first_products(
+                range(2), parts, chunk, weight_one_ref, c
             )
-            total = part if total is None else total + part
+
+
+def dense_kernel(feats, chunk, weight_one_ref, weight_two_ref, total_ref, *refs):
+    n_parts = feats - 2
+    parts, outs, hidden_ref = refs[:n_parts], refs[n_parts:-1], refs[-1]
+    feat = lax.axis_index("feat")
+    width = parts[0].shape[2]
+    for c in range(0, weight_one_ref.shape[1], width):
+        late = first_products(range(2, feats), parts, chunk, weight_one_ref, c)
+        total = total_ref[chunk, :, c : c + width] + late
         hidden_ref[:, c : c + width] = jnp.maximum(total, 0.0).astype(BF16)
     for j in range(feats):
         start = pl.multiple_of((feat ^ j) * width, width)
@@ -274,7 +289,7 @@
     return place_and_run
 
 
-def exchange(domains, pair, sends, which):
+def exchange(domains, own, pair, sends, which):
     half = domains // 2
     shape = pair.shape[1:]
     near, far = sends[: half - 1], sends[half - 1 :]
@@ -289,7 +304,15 @@
         moved=4 * pair.size * half,
     )(which, pair)
     relay = [swap(relay[k - 1], "dom", k) for k in range(1, half)]
-    return [pair, *near, *far, *relay]
+    early = [pair, *near, far[0], *far[2:]]
+    pool = call(
+        functools.partial(fill_early_kernel, domains),
+        [block((own.shape[0] + 2 * domains, *shape))],
+        [VMEM] * (1 + len(early)),
+        [VMEM],
+        moved=8 * own.size,
+    )(own, *early)[0]
+    return [pool, far[1], *relay]
 
 
 def on_device(features, adjacency, tile_src, mig_slot, weight_one, weight_two):
@@ -325,7 +348,7 @@
         [SMEM] * 3 + [VMEM] * len(near_far),
         moved=8 * size * width * domains,
     )(mig, named, own)
-    arrived = exchange(domains, pair, sends, which)
+    arrived = exchange(domains, own, pair, sends, which)
     table, adjacency = call(
         functools.partial(table_kernel, domains, rows),
         [scalars(named.shape), block(adjacency.shape)],
@@ -341,11 +364,12 @@
     pool_one, parts[2] = call(
         functools.partial(first_sum_kernel, domains, feats, 2),
         [pool, whole],
-        [SMEM, SMEM] + [VMEM] * (2 + len(arrived)),
+        [SMEM, SMEM] + [VMEM] * (1 + len(arrived)),
         [VMEM] * 2,
         flops=work * per,
         moved=read * per,
-    )(table, deal, adjacency, own, *arrived)
+        input_output_aliases={3: 0},
+    )(table, deal, adjacency, *arrived)
     for js in [[j] for j in range(3, feats)] + [[1, 0]]:
         outs = call(
             functools.partial(part_sum_kernel, feats, js),
@@ -359,17 +383,25 @@
             parts[j] = out
     parts = [p if j == 0 else swap(p, "feat", j) for j, p in enumerate(parts)]
 
+    total = call(
+        dense_early_kernel,
+        [pltpu.VMEM((per, size, weight_one.shape[1]), F32)],
+        [VMEM] * 3,
+        [VMEM],
+        flops=2 * per * size * weight_one.size * 2 // feats,
+        moved=weight_one.size * 2,
+    )(weight_one, *parts[:2])[0]
     columns = []
     for i in range(per):
         outs = call(
             functools.partial(dense_kernel, feats, i),
             [one] * feats,
-            [VMEM] * (2 + feats),
+            [VMEM] * (1 + feats),
             [VMEM] * feats,
             [pltpu.VMEM((size, weight_one.shape[1]), BF16)],
             flops=4 * size * weight_one.size,
             moved=weight_one.size * 4,
-        )(weight_one, weight_two, *parts)
+        )(weight_one, weight_two, total, *parts[2:])
         columns += [c if j == 0 else swap(c, "feat", j) for j, c in enumerate(outs)]
 
     pair = call(
@@ -386,16 +418,17 @@
         [VMEM] * (1 + len(near_far)),
         moved=8 * size * width * domains,
     )(slots, deal, *columns)
-    arrived = exchange(domains, pair, sends, which)
+    arrived = exchange(domains, own, pair, sends, which)
 
     pool_two, leaving = call(
         functools.partial(leaving_sum_kernel, domains),
         [pool, block((2, size, width))],
-        [SMEM, SMEM] + [VMEM] * (2 + len(arrived)),
+        [SMEM, SMEM] + [VMEM] * (1 + len(arrived)),
         [VMEM] * 2,
         flops=work * 2,
         moved=read * 2,
-    )(table, slots, adjacency, own, *arrived)
+        input_output_aliases={3: 0},
+    )(table, slots, adjacency, *arrived)
     moved = lax.ppermute(leaving, "dom", [(i, (i + 1) % domains) for i in range(domains)])
     out = call(
         staying_sum_kernel,

time: 90.2 us -> 86.8 us (0.962)
  waiting for transfers between devices: 32.1 us -> 29.4 us
    ppermute x31, waiting for transfers between devices: 28.7 us -> 25.3 us  [swap(): lax.ppermute(value, axis, [(i, i ^ flip) for i in range(lax.axis_size(axi...]
    pallas_call x15 -> x18, Pallas kernels: 12.1 us -> 12.3 us  [place_and_run(): return run(*placed)]
  transfers between devices with their start and end apart: 32 -> 32, of which waited for: 15 -> 13; matrix products, arithmetic and copies ran while one was open for 0% -> 0% of each run, Pallas kernels for 7% -> 8%
where the time goes in v3:
time: 86.8 us; the launch traced here: 86.6 us
  starting transfers between devices  44.7 us (51%)
  waiting for transfers between devices  29.4 us (34%)
  Pallas kernels  12.3 us (14%)
    ppermute x31, starting transfers between devices, swap(): lax.ppermute(value, axis, [(i, i ^ flip) for i in range(lax.axis_size(axi...  43.8 us
    ppermute x31, waiting for transfers between devices, swap(): lax.ppermute(value, axis, [(i, i ^ flip) for i in range(lax.axis_size(axi...  25.3 us
    pallas_call x18, Pallas kernels, place_and_run(): return run(*placed)  12.3 us
    ppermute x1, waiting for transfers between devices, on_device(): lax.ppermute(leaving, 'dom', [(i, (i + 1) % domains) for i in range(domai...  4.03 us
  transfers between devices with their start and end apart: 32, of which 13 were waited for; matrix products, arithmetic and copies ran while one was open for 0% of the time, Pallas kernels for 8%

profile of v3, /device:TPU:0, one launch (start us, length us, event | category | flops | bytes accessed | tf_op | source)
XLA Modules:
  0.0 86.6 jit_solution(14925417330395556044)
XLA Ops:
  0.0 1.1 %shard_map.64 = (s32[16,64]{1,0:T(8,128)S(1)}, s32[2,8]{1,0:T(2,128)S(4)}, bf16[8,128,256]{2,1,0:T(8,128)(2,1)S(1)}, bf16[2,128,256]{2,1,0:T(8,128)(2,1)S(1)}) custom-call(s32[16,64]{1,0:T(8,128)} %bitcast.5, s32[2,8]{1,0:T(2,128)} %bitcast.6, bf16[8,128,256]{2,1,0:T(8,128)(2,1)} %bitcast.4), custom_call_target="tpu_custom_call" | custom-call | bytes 524288 | tf_op jit(solution)/shard_map/pallas_call | solution.py:287
  1.1 4.1 %collective-permute-start = (bf16[2,128,256]{2,1,0:T(8,128)(2,1)S(1)}, bf16[2,128,256]{2,1,0:T(8,128)(2,1)S(1)}, u32[]{:S(2)}, u32[]{:S(2)}) collective-permute-start(bf16[2,128,256]{2,1,0:T(8,128)(2,1)S(1)} %get-tuple-element.56), channel_id=1, source_target_pairs={{0,16},{4,20},{8,24},{12,28},{16,0},{20,4},{24,8},{28,12},{1,17},{... | collective-permute-start | bytes 393224 | tf_op jit(solution)/shard_map/ppermute | solution.py:21
  5.2 0.3 shard_map.65
  5.6 1.8 %collective-permute-start.1 = (bf16[2,128,256]{2,1,0:T(8,128)(2,1)S(1)}, bf16[2,128,256]{2,1,0:T(8,128)(2,1)S(1)}, u32[]{:S(2)}, u32[]{:S(2)}) collective-permute-start(bf16[2,128,256]{2,1,0:T(8,128)(2,1)S(1)} %get-tuple-element.57), channel_id=1, source_target_pairs={{0,4},{4,0},{8,12},{12,8},{16,20},{20,16},{24,28},{28,24},{1,5},{5... | collective-permute-start | bytes 393224 | tf_op jit(solution)/shard_map/ppermute | solution.py:21
  7.4 1.6 %collective-permute-start.2 = (bf16[2,128,256]{2,1,0:T(8,128)(2,1)S(1)}, bf16[2,128,256]{2,1,0:T(8,128)(2,1)S(1)}, u32[]{:S(2)}, u32[]{:S(2)}) collective-permute-start(bf16[2,128,256]{2,1,0:T(8,128)(2,1)S(1)} %get-tuple-element.58), channel_id=1, source_target_pairs={{0,8},{4,12},{8,0},{12,4},{16,24},{20,28},{24,16},{28,20},{1,9},{5... | collective-permute-start | bytes 393224 | tf_op jit(solution)/shard_map/ppermute | solution.py:21
  9.0 2.5 %collective-permute-start.5 = (bf16[1,128,256]{2,1,0:T(8,128)(2,1)S(1)}, bf16[1,128,256]{2,1,0:T(8,128)(2,1)S(1)}, u32[]{:S(2)}, u32[]{:S(2)}) collective-permute-start(bf16[1,128,256]{2,1,0:T(8,128)(2,1)S(1)} %get-tuple-element.61), channel_id=1, source_target_pairs={{0,24},{4,28},{8,16},{12,20},{16,8},{20,12},{24,0},{28,4},{1,25},{... | collective-permute-start | bytes 196616 | tf_op jit(solution)/shard_map/ppermute | solution.py:21
  11.5 5.0 %collective-permute-done.4.refs_4_ = bf16[1,128,256]{2,1,0:T(8,128)(2,1)S(1)} collective-permute-done((bf16[1,128,256]{2,1,0:T(8,128)(2,1)S(1)}, bf16[1,128,256]{2,1,0:T(8,128)(2,1)S(1)}, u32[]{:S(2)}, u32[]{:S(2)}) %collective-permute-start.4) | collective-permute-done | bytes 65568 | tf_op jit(solution)/shard_map/ppermute | solution.py:21
  16.5 3.9 %collective-permute-start.6 = (bf16[1,128,256]{2,1,0:T(8,128)(2,1)S(1)}, bf16[1,128,256]{2,1,0:T(8,128)(2,1)S(1)}, u32[]{:S(2)}, u32[]{:S(2)}) collective-permute-start(bf16[1,128,256]{2,1,0:T(8,128)(2,1)S(1)} %get-tuple-element.62), channel_id=1, source_target_pairs={{0,28},{4,24},{8,20},{12,16},{16,12},{20,8},{24,4},{28,0},{1,29},{... | collective-permute-start | bytes 196616 | tf_op jit(solution)/shard_map/ppermute | solution.py:21
  20.4 2.4 %collective-permute-start.7 = (bf16[1,128,256]{2,1,0:T(8,128)(2,1)S(1)}, bf16[1,128,256]{2,1,0:T(8,128)(2,1)S(1)}, u32[]{:S(2)}, u32[]{:S(2)}) collective-permute-start(bf16[1,128,256]{2,1,0:T(8,128)(2,1)S(1)} %get-tuple-element.63), channel_id=1, source_target_pairs={{0,20},{4,16},{8,28},{12,24},{16,4},{20,0},{24,12},{28,8},{1,21},{... | collective-permute-start | bytes 196616 | tf_op jit(solution)/shard_map/ppermute | solution.py:21
  22.8 1.2 %collective-permute-done.6.refs_6_ = bf16[1,128,256]{2,1,0:T(8,128)(2,1)S(1)} collective-permute-done((bf16[1,128,256]{2,1,0:T(8,128)(2,1)S(1)}, bf16[1,128,256]{2,1,0:T(8,128)(2,1)S(1)}, u32[]{:S(2)}, u32[]{:S(2)}) %collective-permute-start.6) | collective-permute-done | bytes 65568 | tf_op jit(solution)/shard_map/ppermute | solution.py:21
  24.0 1.0 %collective-permute-start.8 = (bf16[1,128,256]{2,1,0:T(8,128)(2,1)S(1)}, bf16[1,128,256]{2,1,0:T(8,128)(2,1)S(1)}, u32[]{:S(2)}, u32[]{:S(2)}) collective-permute-start(bf16[1,128,256]{2,1,0:T(8,128)(2,1)S(1)} %get-tuple-element.65), channel_id=1, source_target_pairs={{0,4},{4,0},{8,12},{12,8},{16,20},{20,16},{24,28},{28,24},{1,5},{5... | collective-permute-start | bytes 196616 | tf_op jit(solution)/shard_map/ppermute | solution.py:21
  25.1 2.4 %collective-permute-start.10 = (bf16[1,128,256]{2,1,0:T(8,128)(2,1)S(1)}, bf16[1,128,256]{2,1,0:T(8,128)(2,1)S(1)}, u32[]{:S(2)}, u32[]{:S(2)}) collective-permute-start(bf16[1,128,256]{2,1,0:T(8,128)(2,1)S(1)} %get-tuple-element.67), channel_id=1, source_target_pairs={{0,12},{4,8},{8,4},{12,0},{16,28},{20,24},{24,20},{28,16},{1,13},{... | collective-permute-start | bytes 196616 | tf_op jit(solution)/shard_map/ppermute | solution.py:21
  27.5 2.2 %shard_map.66 = (s32[16,64]{1,0:T(8,128)S(4)}, bf16[8,16,128,128]{3,2,1,0:T(8,128)(2,1)S(1)}) custom-call(s32[2,8]{1,0:T(2,128)S(4)} %get-tuple-element.49.mig, s32[16,64]{1,0:T(8,128)S(1)} %get-tuple-element.50.tiles_ref, bf16[8,16,128,128]{3,2,1,0:T(8,128)(2,1)} %adjacency_ref.1), custom_call_target="tpu_custom_call" | custom-call | bytes 4194304 | tf_op jit(solution)/shard_map/pallas_call | solution.py:287
  29.9 0.3 collective-permute-done.8.refs_2_
  30.1 0.7 collective-permute-done.10.refs_4_
  30.9 0.7 shard_map.69
  31.5 1.3 %shard_map.70 = (bf16[2,128,256]{2,1,0:T(8,128)(2,1)S(1)}, bf16[2,128,256]{2,1,0:T(8,128)(2,1)S(1)}) custom-call(s32[16,64]{1,0:T(8,128)S(4)} %get-tuple-element.53.table_ref, s32[9]{0:T(128)S(4)} %get-tuple-element.55.deal_ref, bf16[8,16,128,128]{3,2,1,0:T(8,128)(2,1)S(1)} %get-tuple-element.54.adjacency_ref, ...), custom_call_target="tpu_custom_call" | custom-call | flops 536870912 | bytes 2097152 | tf_op jit(solution)/shard_map/pallas_call | solution.py:287
  32.9 0.6 shard_map.72
  33.6 1.7 %collective-permute-start.13 = (bf16[2,128,256]{2,1,0:T(8,128)(2,1)S(1)}, bf16[2,128,256]{2,1,0:T(8,128)(2,1)S(1)}, u32[]{:S(2)}, u32[]{:S(2)}) collective-permute-start(bf16[2,128,256]{2,1,0:T(8,128)(2,1)S(1)} %shard_map.72), channel_id=1, source_target_pairs={{0,3},{1,2},{2,1},{3,0},{4,7},{5,6},{6,5},{7,4},{8,11},{9,10},{10,... | collective-permute-start | bytes 393224 | tf_op jit(solution)/shard_map/ppermute | solution.py:21
  35.3 0.5 collective-permute-start.12
  35.8 0.4 shard_map.71.total_ref
  36.2 2.9 %collective-permute-done.13.refs_1_ = bf16[2,128,256]{2,1,0:T(8,128)(2,1)S(1)} collective-permute-done((bf16[2,128,256]{2,1,0:T(8,128)(2,1)S(1)}, bf16[2,128,256]{2,1,0:T(8,128)(2,1)S(1)}, u32[]{:S(2)}, u32[]{:S(2)}) %collective-permute-start.13) | collective-permute-done | bytes 131104 | tf_op jit(solution)/shard_map/ppermute | solution.py:21
  39.2 3.1 %collective-permute-done.12.refs_0_ = bf16[2,128,256]{2,1,0:T(8,128)(2,1)S(1)} collective-permute-done((bf16[2,128,256]{2,1,0:T(8,128)(2,1)S(1)}, bf16[2,128,256]{2,1,0:T(8,128)(2,1)S(1)}, u32[]{:S(2)}, u32[]{:S(2)}) %collective-permute-start.12) | collective-permute-done | bytes 131104 | tf_op jit(solution)/shard_map/ppermute | solution.py:21
  42.3 0.6 shard_map.73
  43.0 1.6 %collective-permute-start.15 = (bf16[1,128,256]{2,1,0:T(8,128)(2,1)S(1)}, bf16[1,128,256]{2,1,0:T(8,128)(2,1)S(1)}, u32[]{:S(2)}, u32[]{:S(2)}) collective-permute-start(bf16[1,128,256]{2,1,0:T(8,128)(2,1)S(1)} %get-tuple-element.74), channel_id=1, source_target_pairs={{0,2},{1,3},{2,0},{3,1},{4,6},{5,7},{6,4},{7,5},{8,10},{9,11},{10,... | collective-permute-start | bytes 196616 | tf_op jit(solution)/shard_map/ppermute | solution.py:21
  44.6 0.2 collective-permute-start.16
  44.8 0.6 shard_map.74
  45.5 0.4 collective-permute-start.17
  45.9 1.6 %collective-permute-start.18 = (bf16[1,128,256]{2,1,0:T(8,128)(2,1)S(1)}, bf16[1,128,256]{2,1,0:T(8,128)(2,1)S(1)}, u32[]{:S(2)}, u32[]{:S(2)}) collective-permute-start(bf16[1,128,256]{2,1,0:T(8,128)(2,1)S(1)} %get-tuple-element.78), channel_id=1, source_target_pairs={{0,2},{1,3},{2,0},{3,1},{4,6},{5,7},{6,4},{7,5},{8,10},{9,11},{10,... | collective-permute-start | bytes 196616 | tf_op jit(solution)/shard_map/ppermute | solution.py:21
  47.5 1.2 %collective-permute-done.16.refs_3_ = bf16[1,128,256]{2,1,0:T(8,128)(2,1)S(1)} collective-permute-done((bf16[1,128,256]{2,1,0:T(8,128)(2,1)S(1)}, bf16[1,128,256]{2,1,0:T(8,128)(2,1)S(1)}, u32[]{:S(2)}, u32[]{:S(2)}) %collective-permute-start.16) | collective-permute-done | bytes 65568 | tf_op jit(solution)/shard_map/ppermute | solution.py:21
  48.7 3.5 %collective-permute-start.20 = (bf16[2,128,256]{2,1,0:T(8,128)(2,1)S(1)}, bf16[2,128,256]{2,1,0:T(8,128)(2,1)S(1)}, u32[]{:S(2)}, u32[]{:S(2)}) collective-permute-start(bf16[2,128,256]{2,1,0:T(8,128)(2,1)S(1)} %shard_map.76), channel_id=1, source_target_pairs={{0,16},{4,20},{8,24},{12,28},{16,0},{20,4},{24,8},{28,12},{1,17},{... | collective-permute-start | bytes 393224 | tf_op jit(solution)/shard_map/ppermute | solution.py:21
  52.3 3.1 %collective-permute-start.24 = (bf16[1,128,256]{2,1,0:T(8,128)(2,1)S(1)}, bf16[1,128,256]{2,1,0:T(8,128)(2,1)S(1)}, u32[]{:S(2)}, u32[]{:S(2)}) collective-permute-start(bf16[1,128,256]{2,1,0:T(8,128)(2,1)S(1)} %get-tuple-element.84), channel_id=1, source_target_pairs={{0,16},{4,20},{8,24},{12,28},{16,0},{20,4},{24,8},{28,12},{1,17},{... | collective-permute-start | bytes 196616 | tf_op jit(solution)/shard_map/ppermute | solution.py:21
  55.4 0.6 collective-permute-start.21
  56.0 0.7 collective-permute-start.22
  56.7 0.9 %collective-permute-start.25 = (bf16[1,128,256]{2,1,0:T(8,128)(2,1)S(1)}, bf16[1,128,256]{2,1,0:T(8,128)(2,1)S(1)}, u32[]{:S(2)}, u32[]{:S(2)}) collective-permute-start(bf16[1,128,256]{2,1,0:T(8,128)(2,1)S(1)} %get-tuple-element.85), channel_id=1, source_target_pairs={{0,24},{4,28},{8,16},{12,20},{16,8},{20,12},{24,0},{28,4},{1,25},{... | collective-permute-start | bytes 196616 | tf_op jit(solution)/shard_map/ppermute | solution.py:21
  57.5 5.9 %collective-permute-done.24.refs_4_ = bf16[1,128,256]{2,1,0:T(8,128)(2,1)S(1)} collective-permute-done((bf16[1,128,256]{2,1,0:T(8,128)(2,1)S(1)}, bf16[1,128,256]{2,1,0:T(8,128)(2,1)S(1)}, u32[]{:S(2)}, u32[]{:S(2)}) %collective-permute-start.24) | collective-permute-done | bytes 65568 | tf_op jit(solution)/shard_map/ppermute | solution.py:21
  63.5 3.2 %collective-permute-start.26 = (bf16[1,128,256]{2,1,0:T(8,128)(2,1)S(1)}, bf16[1,128,256]{2,1,0:T(8,128)(2,1)S(1)}, u32[]{:S(2)}, u32[]{:S(2)}) collective-permute-start(bf16[1,128,256]{2,1,0:T(8,128)(2,1)S(1)} %get-tuple-element.86), channel_id=1, source_target_pairs={{0,28},{4,24},{8,20},{12,16},{16,12},{20,8},{24,4},{28,0},{1,29},{... | collective-permute-start | bytes 196616 | tf_op jit(solution)/shard_map/ppermute | solution.py:21
  66.7 2.4 %collective-permute-start.27 = (bf16[1,128,256]{2,1,0:T(8,128)(2,1)S(1)}, bf16[1,128,256]{2,1,0:T(8,128)(2,1)S(1)}, u32[]{:S(2)}, u32[]{:S(2)}) collective-permute-start(bf16[1,128,256]{2,1,0:T(8,128)(2,1)S(1)} %get-tuple-element.87), channel_id=1, source_target_pairs={{0,20},{4,16},{8,28},{12,24},{16,4},{20,0},{24,12},{28,8},{1,21},{... | collective-permute-start | bytes 196616 | tf_op jit(solution)/shard_map/ppermute | solution.py:21
  69.1 2.1 %collective-permute-done.26.refs_6_ = bf16[1,128,256]{2,1,0:T(8,128)(2,1)S(1)} collective-permute-done((bf16[1,128,256]{2,1,0:T(8,128)(2,1)S(1)}, bf16[1,128,256]{2,1,0:T(8,128)(2,1)S(1)}, u32[]{:S(2)}, u32[]{:S(2)}) %collective-permute-start.26) | collective-permute-done | bytes 65568 | tf_op jit(solution)/shard_map/ppermute | solution.py:21
  71.1 0.8 collective-permute-start.28
  72.0 2.7 %collective-permute-start.30 = (bf16[1,128,256]{2,1,0:T(8,128)(2,1)S(1)}, bf16[1,128,256]{2,1,0:T(8,128)(2,1)S(1)}, u32[]{:S(2)}, u32[]{:S(2)}) collective-permute-start(bf16[1,128,256]{2,1,0:T(8,128)(2,1)S(1)} %get-tuple-element.90), channel_id=1, source_target_pairs={{0,12},{4,8},{8,4},{12,0},{16,28},{20,24},{24,20},{28,16},{1,13},{... | collective-permute-start | bytes 196616 | tf_op jit(solution)/shard_map/ppermute | solution.py:21
  74.7 1.3 %collective-permute-done.28.refs_2_ = bf16[1,128,256]{2,1,0:T(8,128)(2,1)S(1)} collective-permute-done((bf16[1,128,256]{2,1,0:T(8,128)(2,1)S(1)}, bf16[1,128,256]{2,1,0:T(8,128)(2,1)S(1)}, u32[]{:S(2)}, u32[]{:S(2)}) %collective-permute-start.28) | collective-permute-done | bytes 65568 | tf_op jit(solution)/shard_map/ppermute | solution.py:21
  76.2 1.3 %collective-permute-done.30.refs_4_ = bf16[1,128,256]{2,1,0:T(8,128)(2,1)S(1)} collective-permute-done((bf16[1,128,256]{2,1,0:T(8,128)(2,1)S(1)}, bf16[1,128,256]{2,1,0:T(8,128)(2,1)S(1)}, u32[]{:S(2)}, u32[]{:S(2)}) %collective-permute-start.30) | collective-permute-done | bytes 65568 | tf_op jit(solution)/shard_map/ppermute | solution.py:21
  77.6 0.7 shard_map.79
  78.2 0.9 %collective-permute-start.31 = (bf16[2,128,256]{2,1,0:T(8,128)(2,1)S(1)}, bf16[2,128,256]{2,1,0:T(8,128)(2,1)S(1)}, u32[]{:S(2)}, u32[]{:S(2)}) collective-permute-start(bf16[2,128,256]{2,1,0:T(8,128)(2,1)S(1)} %get-tuple-element.91), channel_id=1, source_target_pairs={{0,4},{4,8},{8,12},{12,16},{16,20},{20,24},{24,28},{28,0},{1,5},{5... | collective-permute-start | bytes 393224 | tf_op jit(solution)/shard_map/ppermute | solution.py:432
  79.1 2.8 %shard_map.80.out_in_ref = bf16[8,128,256]{2,1,0:T(8,128)(2,1)} custom-call(s32[16,64]{1,0:T(8,128)S(4)} %get-tuple-element.53.table_ref, s32[16]{0:T(128)S(4)} %get-tuple-element.52.slots_ref, bf16[8,16,128,128]{3,2,1,0:T(8,128)(2,1)S(1)} %get-tuple-element.54.adjacency_ref, bf16[24,128,256]{2,1,0:T(8,128)(2,1)S(1)} %get-tuple-element.92.pool_ref), custom_call_target="tpu_custom_call" | custom-call | flops 805306368 | bytes 3145728 | tf_op jit(solution)/shard_map/pallas_call | solution.py:287
  81.9 4.0 %collective-permute-done.31.moved_ref = bf16[2,128,256]{2,1,0:T(8,128)(2,1)S(1)} collective-permute-done((bf16[2,128,256]{2,1,0:T(8,128)(2,1)S(1)}, bf16[2,128,256]{2,1,0:T(8,128)(2,1)S(1)}, u32[]{:S(2)}, u32[]{:S(2)}) %collective-permute-start.31) | collective-permute-done | bytes 131104 | tf_op jit(solution)/shard_map/ppermute | solution.py:432
  86.0 0.7 shard_map.81
  (38 shorter events, 0.8 us)
Async XLA Ops:
  1.1 19.3 %collective-permute-start = (bf16[2,128,256]{2,1,0:T(8,128)(2,1)S(1)}, bf16[2,128,256]{2,1,0:T(8,128)(2,1)S(1)}, u32[]{:S(2)}, u32[]{:S(2)}) collective-permute-start(bf16[2,128,256]{2,1,0:T(8,128)(2,1)S(1)} %get-tuple-element.56), channel_id=1, source_target_pairs={{0,16},{4,20},{8,24},{12,28},{16,0},{20,4},{24,8},{28,12},{1,17},{... | collective-permute-start | bytes 393224 | tf_op jit(solution)/shard_map/ppermute | solution.py:21
  5.5 10.9 %collective-permute-start.4 = (bf16[1,128,256]{2,1,0:T(8,128)(2,1)S(1)}, bf16[1,128,256]{2,1,0:T(8,128)(2,1)S(1)}, u32[]{:S(2)}, u32[]{:S(2)}) collective-permute-start(bf16[1,128,256]{2,1,0:T(8,128)(2,1)S(1)} %get-tuple-element.60), channel_id=1, source_target_pairs={{0,16},{4,20},{8,24},{12,28},{16,0},{20,4},{24,8},{28,12},{1,17},{... | collective-permute-start | bytes 196616 | tf_op jit(solution)/shard_map/ppermute | solution.py:21
  5.6 19.5 %collective-permute-start.1 = (bf16[2,128,256]{2,1,0:T(8,128)(2,1)S(1)}, bf16[2,128,256]{2,1,0:T(8,128)(2,1)S(1)}, u32[]{:S(2)}, u32[]{:S(2)}) collective-permute-start(bf16[2,128,256]{2,1,0:T(8,128)(2,1)S(1)} %get-tuple-element.57), channel_id=1, source_target_pairs={{0,4},{4,0},{8,12},{12,8},{16,20},{20,16},{24,28},{28,24},{1,5},{5... | collective-permute-start | bytes 393224 | tf_op jit(solution)/shard_map/ppermute | solution.py:21
  7.4 17.7 %collective-permute-start.2 = (bf16[2,128,256]{2,1,0:T(8,128)(2,1)S(1)}, bf16[2,128,256]{2,1,0:T(8,128)(2,1)S(1)}, u32[]{:S(2)}, u32[]{:S(2)}) collective-permute-start(bf16[2,128,256]{2,1,0:T(8,128)(2,1)S(1)} %get-tuple-element.58), channel_id=1, source_target_pairs={{0,8},{4,12},{8,0},{12,4},{16,24},{20,28},{24,16},{28,20},{1,9},{5... | collective-permute-start | bytes 393224 | tf_op jit(solution)/shard_map/ppermute | solution.py:21
  9.0 11.4 %collective-permute-start.5 = (bf16[1,128,256]{2,1,0:T(8,128)(2,1)S(1)}, bf16[1,128,256]{2,1,0:T(8,128)(2,1)S(1)}, u32[]{:S(2)}, u32[]{:S(2)}) collective-permute-start(bf16[1,128,256]{2,1,0:T(8,128)(2,1)S(1)} %get-tuple-element.61), channel_id=1, source_target_pairs={{0,24},{4,28},{8,16},{12,20},{16,8},{20,12},{24,0},{28,4},{1,25},{... | collective-permute-start | bytes 196616 | tf_op jit(solution)/shard_map/ppermute | solution.py:21
  16.5 7.6 %collective-permute-start.6 = (bf16[1,128,256]{2,1,0:T(8,128)(2,1)S(1)}, bf16[1,128,256]{2,1,0:T(8,128)(2,1)S(1)}, u32[]{:S(2)}, u32[]{:S(2)}) collective-permute-start(bf16[1,128,256]{2,1,0:T(8,128)(2,1)S(1)} %get-tuple-element.62), channel_id=1, source_target_pairs={{0,28},{4,24},{8,20},{12,16},{16,12},{20,8},{24,4},{28,0},{1,29},{... | collective-permute-start | bytes 196616 | tf_op jit(solution)/shard_map/ppermute | solution.py:21
  20.4 9.4 %collective-permute-start.3 = (bf16[2,128,256]{2,1,0:T(8,128)(2,1)S(1)}, bf16[2,128,256]{2,1,0:T(8,128)(2,1)S(1)}, u32[]{:S(2)}, u32[]{:S(2)}) collective-permute-start(bf16[2,128,256]{2,1,0:T(8,128)(2,1)S(1)} %get-tuple-element.59), channel_id=1, source_target_pairs={{0,12},{4,8},{8,4},{12,0},{16,28},{20,24},{24,20},{28,16},{1,13},{... | collective-permute-start | bytes 393224 | tf_op jit(solution)/shard_map/ppermute | solution.py:21
  20.4 9.5 %collective-permute-start.7 = (bf16[1,128,256]{2,1,0:T(8,128)(2,1)S(1)}, bf16[1,128,256]{2,1,0:T(8,128)(2,1)S(1)}, u32[]{:S(2)}, u32[]{:S(2)}) collective-permute-start(bf16[1,128,256]{2,1,0:T(8,128)(2,1)S(1)} %get-tuple-element.63), channel_id=1, source_target_pairs={{0,20},{4,16},{8,28},{12,24},{16,4},{20,0},{24,12},{28,8},{1,21},{... | collective-permute-start | bytes 196616 | tf_op jit(solution)/shard_map/ppermute | solution.py:21
  24.0 6.1 %collective-permute-start.8 = (bf16[1,128,256]{2,1,0:T(8,128)(2,1)S(1)}, bf16[1,128,256]{2,1,0:T(8,128)(2,1)S(1)}, u32[]{:S(2)}, u32[]{:S(2)}) collective-permute-start(bf16[1,128,256]{2,1,0:T(8,128)(2,1)S(1)} %get-tuple-element.65), channel_id=1, source_target_pairs={{0,4},{4,0},{8,12},{12,8},{16,20},{20,16},{24,28},{28,24},{1,5},{5... | collective-permute-start | bytes 196616 | tf_op jit(solution)/shard_map/ppermute | solution.py:21
  25.1 5.0 %collective-permute-start.9 = (bf16[1,128,256]{2,1,0:T(8,128)(2,1)S(1)}, bf16[1,128,256]{2,1,0:T(8,128)(2,1)S(1)}, u32[]{:S(2)}, u32[]{:S(2)}) collective-permute-start(bf16[1,128,256]{2,1,0:T(8,128)(2,1)S(1)} %get-tuple-element.66), channel_id=1, source_target_pairs={{0,8},{4,12},{8,0},{12,4},{16,24},{20,28},{24,16},{28,20},{1,9},{5... | collective-permute-start | bytes 196616 | tf_op jit(solution)/shard_map/ppermute | solution.py:21
  25.1 5.8 %collective-permute-start.10 = (bf16[1,128,256]{2,1,0:T(8,128)(2,1)S(1)}, bf16[1,128,256]{2,1,0:T(8,128)(2,1)S(1)}, u32[]{:S(2)}, u32[]{:S(2)}) collective-permute-start(bf16[1,128,256]{2,1,0:T(8,128)(2,1)S(1)} %get-tuple-element.67), channel_id=1, source_target_pairs={{0,12},{4,8},{8,4},{12,0},{16,28},{20,24},{24,20},{28,16},{1,13},{... | collective-permute-start | bytes 196616 | tf_op jit(solution)/shard_map/ppermute | solution.py:21
  32.8 2.9 %copy-start = (bf16[1024,1024]{1,0:T(8,128)(2,1)S(1)}, bf16[1024,1024]{1,0:T(8,128)(2,1)}, u32[]{:S(2)}) copy-start(bf16[1024,1024]{1,0:T(8,128)(2,1)} %weight_one_ref.5) | copy-start | bytes 6291460
  32.8 2.9 %collective-permute-start.11 = (bf16[2,128,256]{2,1,0:T(8,128)(2,1)S(1)}, bf16[2,128,256]{2,1,0:T(8,128)(2,1)S(1)}, u32[]{:S(2)}, u32[]{:S(2)}) collective-permute-start(bf16[2,128,256]{2,1,0:T(8,128)(2,1)S(1)} %get-tuple-element.70), channel_id=1, source_target_pairs={{0,1},{1,0},{2,3},{3,2},{4,5},{5,4},{6,7},{7,6},{8,9},{9,8},{10,11... | collective-permute-start | bytes 393224 | tf_op jit(solution)/shard_map/ppermute | solution.py:21
  33.6 8.7 %copy-start.1 = (bf16[1024,1024]{1,0:T(8,128)(2,1)S(1)}, bf16[1024,1024]{1,0:T(8,128)(2,1)}, u32[]{:S(2)}) copy-start(bf16[1024,1024]{1,0:T(8,128)(2,1)} %weight_two_ref.3) | copy-start | bytes 6291460
  33.6 5.6 %collective-permute-start.13 = (bf16[2,128,256]{2,1,0:T(8,128)(2,1)S(1)}, bf16[2,128,256]{2,1,0:T(8,128)(2,1)S(1)}, u32[]{:S(2)}, u32[]{:S(2)}) collective-permute-start(bf16[2,128,256]{2,1,0:T(8,128)(2,1)S(1)} %shard_map.72), channel_id=1, source_target_pairs={{0,3},{1,2},{2,1},{3,0},{4,7},{5,6},{6,5},{7,4},{8,11},{9,10},{10,... | collective-permute-start | bytes 393224 | tf_op jit(solution)/shard_map/ppermute | solution.py:21
  35.3 7.0 %collective-permute-start.12 = (bf16[2,128,256]{2,1,0:T(8,128)(2,1)S(1)}, bf16[2,128,256]{2,1,0:T(8,128)(2,1)S(1)}, u32[]{:S(2)}, u32[]{:S(2)}) collective-permute-start(bf16[2,128,256]{2,1,0:T(8,128)(2,1)S(1)} %get-tuple-element.71), channel_id=1, source_target_pairs={{0,2},{1,3},{2,0},{3,1},{4,6},{5,7},{6,4},{7,5},{8,10},{9,11},{10,... | collective-permute-start | bytes 393224 | tf_op jit(solution)/shard_map/ppermute | solution.py:21
  42.9 4.6 %collective-permute-start.14 = (bf16[1,128,256]{2,1,0:T(8,128)(2,1)S(1)}, bf16[1,128,256]{2,1,0:T(8,128)(2,1)S(1)}, u32[]{:S(2)}, u32[]{:S(2)}) collective-permute-start(bf16[1,128,256]{2,1,0:T(8,128)(2,1)S(1)} %get-tuple-element.73), channel_id=1, source_target_pairs={{0,1},{1,0},{2,3},{3,2},{4,5},{5,4},{6,7},{7,6},{8,9},{9,8},{10,11... | collective-permute-start | bytes 196616 | tf_op jit(solution)/shard_map/ppermute | solution.py:21
  43.0 4.5 %collective-permute-start.15 = (bf16[1,128,256]{2,1,0:T(8,128)(2,1)S(1)}, bf16[1,128,256]{2,1,0:T(8,128)(2,1)S(1)}, u32[]{:S(2)}, u32[]{:S(2)}) collective-permute-start(bf16[1,128,256]{2,1,0:T(8,128)(2,1)S(1)} %get-tuple-element.74), channel_id=1, source_target_pairs={{0,2},{1,3},{2,0},{3,1},{4,6},{5,7},{6,4},{7,5},{8,10},{9,11},{10,... | collective-permute-start | bytes 196616 | tf_op jit(solution)/shard_map/ppermute | solution.py:21
  44.6 4.1 %collective-permute-start.16 = (bf16[1,128,256]{2,1,0:T(8,128)(2,1)S(1)}, bf16[1,128,256]{2,1,0:T(8,128)(2,1)S(1)}, u32[]{:S(2)}, u32[]{:S(2)}) collective-permute-start(bf16[1,128,256]{2,1,0:T(8,128)(2,1)S(1)} %get-tuple-element.75), channel_id=1, source_target_pairs={{0,3},{1,2},{2,1},{3,0},{4,7},{5,6},{6,5},{7,4},{8,11},{9,10},{10,... | collective-permute-start | bytes 196616 | tf_op jit(solution)/shard_map/ppermute | solution.py:21
  45.5 6.8 %collective-permute-start.17 = (bf16[1,128,256]{2,1,0:T(8,128)(2,1)S(1)}, bf16[1,128,256]{2,1,0:T(8,128)(2,1)S(1)}, u32[]{:S(2)}, u32[]{:S(2)}) collective-permute-start(bf16[1,128,256]{2,1,0:T(8,128)(2,1)S(1)} %get-tuple-element.77), channel_id=1, source_target_pairs={{0,1},{1,0},{2,3},{3,2},{4,5},{5,4},{6,7},{7,6},{8,9},{9,8},{10,11... | collective-permute-start | bytes 196616 | tf_op jit(solution)/shard_map/ppermute | solution.py:21
  45.9 6.3 %collective-permute-start.18 = (bf16[1,128,256]{2,1,0:T(8,128)(2,1)S(1)}, bf16[1,128,256]{2,1,0:T(8,128)(2,1)S(1)}, u32[]{:S(2)}, u32[]{:S(2)}) collective-permute-start(bf16[1,128,256]{2,1,0:T(8,128)(2,1)S(1)} %get-tuple-element.78), channel_id=1, source_target_pairs={{0,2},{1,3},{2,0},{3,1},{4,6},{5,7},{6,4},{7,5},{8,10},{9,11},{10,... | collective-permute-start | bytes 196616 | tf_op jit(solution)/shard_map/ppermute | solution.py:21
  47.4 4.8 %collective-permute-start.19 = (bf16[1,128,256]{2,1,0:T(8,128)(2,1)S(1)}, bf16[1,128,256]{2,1,0:T(8,128)(2,1)S(1)}, u32[]{:S(2)}, u32[]{:S(2)}) collective-permute-start(bf16[1,128,256]{2,1,0:T(8,128)(2,1)S(1)} %get-tuple-element.79), channel_id=1, source_target_pairs={{0,3},{1,2},{2,1},{3,0},{4,7},{5,6},{6,5},{7,4},{8,11},{9,10},{10,... | collective-permute-start | bytes 196616 | tf_op jit(solution)/shard_map/ppermute | solution.py:21
  48.7 18.0 %collective-permute-start.20 = (bf16[2,128,256]{2,1,0:T(8,128)(2,1)S(1)}, bf16[2,128,256]{2,1,0:T(8,128)(2,1)S(1)}, u32[]{:S(2)}, u32[]{:S(2)}) collective-permute-start(bf16[2,128,256]{2,1,0:T(8,128)(2,1)S(1)} %shard_map.76), channel_id=1, source_target_pairs={{0,16},{4,20},{8,24},{12,28},{16,0},{20,4},{24,8},{28,12},{1,17},{... | collective-permute-start | bytes 393224 | tf_op jit(solution)/shard_map/ppermute | solution.py:21
  52.3 11.1 %collective-permute-start.24 = (bf16[1,128,256]{2,1,0:T(8,128)(2,1)S(1)}, bf16[1,128,256]{2,1,0:T(8,128)(2,1)S(1)}, u32[]{:S(2)}, u32[]{:S(2)}) collective-permute-start(bf16[1,128,256]{2,1,0:T(8,128)(2,1)S(1)} %get-tuple-element.84), channel_id=1, source_target_pairs={{0,16},{4,20},{8,24},{12,28},{16,0},{20,4},{24,8},{28,12},{1,17},{... | collective-permute-start | bytes 196616 | tf_op jit(solution)/shard_map/ppermute | solution.py:21
  55.4 16.6 %collective-permute-start.21 = (bf16[2,128,256]{2,1,0:T(8,128)(2,1)S(1)}, bf16[2,128,256]{2,1,0:T(8,128)(2,1)S(1)}, u32[]{:S(2)}, u32[]{:S(2)}) collective-permute-start(bf16[2,128,256]{2,1,0:T(8,128)(2,1)S(1)} %get-tuple-element.81), channel_id=1, source_target_pairs={{0,4},{4,0},{8,12},{12,8},{16,20},{20,16},{24,28},{28,24},{1,5},{5... | collective-permute-start | bytes 393224 | tf_op jit(solution)/shard_map/ppermute | solution.py:21
  56.0 16.0 %collective-permute-start.22 = (bf16[2,128,256]{2,1,0:T(8,128)(2,1)S(1)}, bf16[2,128,256]{2,1,0:T(8,128)(2,1)S(1)}, u32[]{:S(2)}, u32[]{:S(2)}) collective-permute-start(bf16[2,128,256]{2,1,0:T(8,128)(2,1)S(1)} %get-tuple-element.82), channel_id=1, source_target_pairs={{0,8},{4,12},{8,0},{12,4},{16,24},{20,28},{24,16},{28,20},{1,9},{5... | collective-permute-start | bytes 393224 | tf_op jit(solution)/shard_map/ppermute | solution.py:21
  56.7 10.0 %collective-permute-start.25 = (bf16[1,128,256]{2,1,0:T(8,128)(2,1)S(1)}, bf16[1,128,256]{2,1,0:T(8,128)(2,1)S(1)}, u32[]{:S(2)}, u32[]{:S(2)}) collective-permute-start(bf16[1,128,256]{2,1,0:T(8,128)(2,1)S(1)} %get-tuple-element.85), channel_id=1, source_target_pairs={{0,24},{4,28},{8,16},{12,20},{16,8},{20,12},{24,0},{28,4},{1,25},{... | collective-permute-start | bytes 196616 | tf_op jit(solution)/shard_map/ppermute | solution.py:21
  63.5 7.7 %collective-permute-start.26 = (bf16[1,128,256]{2,1,0:T(8,128)(2,1)S(1)}, bf16[1,128,256]{2,1,0:T(8,128)(2,1)S(1)}, u32[]{:S(2)}, u32[]{:S(2)}) collective-permute-start(bf16[1,128,256]{2,1,0:T(8,128)(2,1)S(1)} %get-tuple-element.86), channel_id=1, source_target_pairs={{0,28},{4,24},{8,20},{12,16},{16,12},{20,8},{24,4},{28,0},{1,29},{... | collective-permute-start | bytes 196616 | tf_op jit(solution)/shard_map/ppermute | solution.py:21
  66.7 8.0 %collective-permute-start.23 = (bf16[2,128,256]{2,1,0:T(8,128)(2,1)S(1)}, bf16[2,128,256]{2,1,0:T(8,128)(2,1)S(1)}, u32[]{:S(2)}, u32[]{:S(2)}) collective-permute-start(bf16[2,128,256]{2,1,0:T(8,128)(2,1)S(1)} %get-tuple-element.83), channel_id=1, source_target_pairs={{0,12},{4,8},{8,4},{12,0},{16,28},{20,24},{24,20},{28,16},{1,13},{... | collective-permute-start | bytes 393224 | tf_op jit(solution)/shard_map/ppermute | solution.py:21
  66.7 8.0 %collective-permute-start.27 = (bf16[1,128,256]{2,1,0:T(8,128)(2,1)S(1)}, bf16[1,128,256]{2,1,0:T(8,128)(2,1)S(1)}, u32[]{:S(2)}, u32[]{:S(2)}) collective-permute-start(bf16[1,128,256]{2,1,0:T(8,128)(2,1)S(1)} %get-tuple-element.87), channel_id=1, source_target_pairs={{0,20},{4,16},{8,28},{12,24},{16,4},{20,0},{24,12},{28,8},{1,21},{... | collective-permute-start | bytes 196616 | tf_op jit(solution)/shard_map/ppermute | solution.py:21
  71.1 4.9 %collective-permute-start.28 = (bf16[1,128,256]{2,1,0:T(8,128)(2,1)S(1)}, bf16[1,128,256]{2,1,0:T(8,128)(2,1)S(1)}, u32[]{:S(2)}, u32[]{:S(2)}) collective-permute-start(bf16[1,128,256]{2,1,0:T(8,128)(2,1)S(1)} %get-tuple-element.88), channel_id=1, source_target_pairs={{0,4},{4,0},{8,12},{12,8},{16,20},{20,16},{24,28},{28,24},{1,5},{5... | collective-permute-start | bytes 196616 | tf_op jit(solution)/shard_map/ppermute | solution.py:21
  72.0 4.3 %collective-permute-start.29 = (bf16[1,128,256]{2,1,0:T(8,128)(2,1)S(1)}, bf16[1,128,256]{2,1,0:T(8,128)(2,1)S(1)}, u32[]{:S(2)}, u32[]{:S(2)}) collective-permute-start(bf16[1,128,256]{2,1,0:T(8,128)(2,1)S(1)} %get-tuple-element.89), channel_id=1, source_target_pairs={{0,8},{4,12},{8,0},{12,4},{16,24},{20,28},{24,16},{28,20},{1,9},{5... | collective-permute-start | bytes 196616 | tf_op jit(solution)/shard_map/ppermute | solution.py:21
  72.0 5.6 %collective-permute-start.30 = (bf16[1,128,256]{2,1,0:T(8,128)(2,1)S(1)}, bf16[1,128,256]{2,1,0:T(8,128)(2,1)S(1)}, u32[]{:S(2)}, u32[]{:S(2)}) collective-permute-start(bf16[1,128,256]{2,1,0:T(8,128)(2,1)S(1)} %get-tuple-element.90), channel_id=1, source_target_pairs={{0,12},{4,8},{8,4},{12,0},{16,28},{20,24},{24,20},{28,16},{1,13},{... | collective-permute-start | bytes 196616 | tf_op jit(solution)/shard_map/ppermute | solution.py:21
  78.2 7.7 %collective-permute-start.31 = (bf16[2,128,256]{2,1,0:T(8,128)(2,1)S(1)}, bf16[2,128,256]{2,1,0:T(8,128)(2,1)S(1)}, u32[]{:S(2)}, u32[]{:S(2)}) collective-permute-start(bf16[2,128,256]{2,1,0:T(8,128)(2,1)S(1)} %get-tuple-element.91), channel_id=1, source_target_pairs={{0,4},{4,8},{8,12},{12,16},{16,20},{20,24},{24,28},{28,0},{1,5},{5... | collective-permute-start | bytes 393224 | tf_op jit(solution)/shard_map/ppermute | solution.py:432
